TPU v7x, 32 devices: a whole 2x2x4 slice. The times are simulated.
32 devices in a mesh: dp: 2 (over core), ctx: 4 (over z), fsdp: 4 (over y, x).
Axes of the slice: x: 2, y: 2, z: 4, core: 2. Of those that a mesh axis runs over, the one named last changes fastest.
Arguments:
- tokens: bfloat16 [8, 2, 1024, 2048], P(('dp', 'fsdp'), None, 'ctx'), may hold values from -6 to 6
- cotangent: bfloat16 [8, 2, 1024, 2048], P(('dp', 'fsdp'), None, 'ctx'), may hold values from -6 to 6
- lengths: int32 [8, 2], P(('dp', 'fsdp')), may hold values from 513 to 1024, as said below
- deal: int32 [8, 2, 8], P(('dp', 'fsdp')), may hold values from 0 to 7, each once within a row
- ln_gain: bfloat16 [2048], P('fsdp'), may hold values from 0.5 to 1.5
- ln_bias: bfloat16 [2048], P('fsdp'), may hold values from -1 to 1
- w_qkv: bfloat16 [2048, 6144], P('fsdp'), may hold values from -0.125 to 0.125
- b_qkv: bfloat16 [6144], P('fsdp'), may hold values from -1 to 1
- w_out: bfloat16 [2048, 2048], P('fsdp'), may hold values from -3 to 3
- b_out: bfloat16 [2048], P('fsdp'), may hold values from -2.5 to 2.5
- w_up: bfloat16 [2048, 8192], P('fsdp'), may hold values from -0.125 to 0.125
- b_up: bfloat16 [8192], P('fsdp'), may hold values from -1 to 1
- w_down: bfloat16 [8192, 2048], P('fsdp'), may hold values from -0.0625 to 0.0625
- b_down: bfloat16 [2048], P('fsdp'), may hold values from -2.5 to 2.5
Outputs:
- outputs: bfloat16 [8, 2, 1024, 2048], P(('dp', 'fsdp'), None, 'ctx')
- input_grad: bfloat16 [8, 2, 1024, 2048], P(('dp', 'fsdp'), None, 'ctx')
- grad_ln_gain: float32 [2048], P('fsdp')
- grad_ln_bias: float32 [2048], P('fsdp')
- grad_w_qkv: float32 [2048, 6144], P('fsdp')
- grad_b_qkv: float32 [6144], P('fsdp')
- grad_w_out: float32 [2048, 2048], P('fsdp')
- grad_b_out: float32 [2048], P('fsdp')
- grad_w_up: float32 [2048, 8192], P('fsdp')
- grad_b_up: float32 [8192], P('fsdp')
- grad_w_down: float32 [8192, 2048], P('fsdp')
- grad_b_down: float32 [2048], P('fsdp')
Inputs may be any that keep to these rules, and one draw needn't show every extreme that they name: lengths[g, m] tokens fill the first positions of a sequence, the rest is padding; in every draw one sequence is exactly 1024 long and one exactly 513. Each row of deal is a permutation of the 8 blocks of a sequence.
All inputs are finite; a program needn't handle non-finite values.
Results may differ from a plain program's by a relative error of at most 0.02.
Values may be sent and summed in bfloat16 or wider, within the bound.
No kernel may reach another device: no remote copies, remote signals or barrier semaphores. Data moves between devices by JAX's collectives and lax.ppermute only.
A program may use at most 832 MiB of HBM per device.

v0:
```python
import jax
import jax.numpy as jnp
from jax import lax
from jax.sharding import PartitionSpec as P

HEAD_DIM = 64
ROT = 32


EPS = 1e-05
BASE = 10000.0


def contract_rows(left, right):
    return lax.dot_general(
        left, right, (((0,), (0,)), ((), ())), preferred_element_type=jnp.float32
    )


def contract_cols(left, right):
    return lax.dot_general(
        left, right, (((1,), (1,)), ((), ())), preferred_element_type=jnp.float32
    )


def angles_of(positions):
    half = ROT // 2
    freqs = BASE ** (-(jnp.arange(half, dtype=jnp.float32) * 2.0) / ROT)
    angles = positions.astype(jnp.float32)[:, None] * freqs[None, :]
    return (jnp.cos(angles)[:, None, :], jnp.sin(angles)[:, None, :])


def rotate(values, cosine, sine):
    half = ROT // 2
    first = values[..., :half]
    second = values[..., half:ROT]
    return jnp.concatenate(
        [first * cosine - second * sine, second * cosine + first * sine, values[..., ROT:]], axis=-1
    )


def rotate_back(values, cosine, sine):
    half = ROT // 2
    first = values[..., :half]
    second = values[..., half:ROT]
    return jnp.concatenate(
        [first * cosine + second * sine, second * cosine - first * sine, values[..., ROT:]], axis=-1
    )


def layer_step(weights, inputs, upstream, length, deal_row):
    gain, shift, w_qkv, b_qkv, w_out, b_out, w_up, b_up, w_down, b_down = weights
    row_count, width = inputs.shape
    block_rows = row_count // 2
    head_count = width // HEAD_DIM
    scale = HEAD_DIM ** (-0.5)
    place = lax.axis_index("ctx")
    offsets = jnp.arange(block_rows, dtype=jnp.int32)
    own_blocks = lax.dynamic_slice_in_dim(deal_row, 2 * place, 2)
    local_pos = (own_blocks[:, None] * block_rows + offsets[None, :]).reshape(row_count)
    every_pos = (deal_row[:, None] * block_rows + offsets[None, :]).reshape(-1)
    valid = (local_pos < length).astype(jnp.float32)[:, None]
    allowed = (every_pos[None, :] <= local_pos[:, None]) & (every_pos[None, :] < length)
    cosine, sine = angles_of(local_pos)
    inputs_f = inputs.astype(jnp.float32)
    gain_f = gain.astype(jnp.float32)
    centered = inputs_f - jnp.mean(inputs_f, axis=-1, keepdims=True)
    variance = jnp.mean(centered * centered, axis=-1, keepdims=True)
    inv_std = lax.rsqrt(variance + EPS)
    normed = centered * inv_std
    hidden = (normed * gain_f + shift.astype(jnp.float32)).astype(jnp.bfloat16)
    joined = jnp.dot(hidden, w_qkv, preferred_element_type=jnp.float32) + b_qkv.astype(jnp.float32)
    query = (
        rotate(joined[:, :width].reshape(row_count, head_count, HEAD_DIM), cosine, sine)
        .reshape(row_count, width)
        .astype(jnp.bfloat16)
    )
    keyed = (
        rotate(joined[:, width : 2 * width].reshape(row_count, head_count, HEAD_DIM), cosine, sine)
        .reshape(row_count, width)
        .astype(jnp.bfloat16)
    )
    valued = joined[:, 2 * width :].astype(jnp.bfloat16)
    keys_all, values_all = (
        lax.all_gather(keyed, "ctx", axis=0, tiled=True),
        lax.all_gather(valued, "ctx", axis=0, tiled=True),
    )
    total_keys = keys_all.shape[0]
    group = min(8, head_count)
    span = group * HEAD_DIM

    def heads_of(array, start, count):
        return array[:, start : start + span].reshape(count, group, HEAD_DIM)

    def block_scores(start):
        raw = (
            jnp.einsum(
                "qhd,khd->hqk",
                heads_of(query, start, row_count),
                heads_of(keys_all, start, total_keys),
                preferred_element_type=jnp.float32,
            )
            * scale
        )
        return jnp.where(allowed[None], raw, -1e30)

    attended_parts = []
    lse_parts = []
    for start in range(0, width, span):
        masked = block_scores(start)
        highest = jnp.max(masked, axis=-1, keepdims=True)
        expo = jnp.exp(masked - highest)
        total = jnp.sum(expo, axis=-1, keepdims=True)
        weights_low = (expo / total).astype(jnp.bfloat16)
        mixed = jnp.einsum(
            "hqk,khd->qhd",
            weights_low,
            heads_of(values_all, start, total_keys),
            preferred_element_type=jnp.float32,
        )
        attended_parts.append(mixed.reshape(row_count, span))
        lse_parts.append(highest + jnp.log(total))
    attended = jnp.concatenate(attended_parts, axis=1).astype(jnp.bfloat16)
    branch = jnp.dot(attended, w_out, preferred_element_type=jnp.float32) + b_out.astype(
        jnp.float32
    )
    upward = jnp.dot(hidden, w_up, preferred_element_type=jnp.float32) + b_up.astype(jnp.float32)
    activated = jax.nn.gelu(upward, approximate=True).astype(jnp.bfloat16)
    feed = jnp.dot(activated, w_down, preferred_element_type=jnp.float32) + b_down.astype(
        jnp.float32
    )
    result = (valid * (inputs_f + branch + feed)).astype(jnp.bfloat16)
    grad_out = upstream.astype(jnp.float32) * valid
    grad_low = grad_out.astype(jnp.bfloat16)
    row_total = jnp.sum(grad_out, axis=0)
    d_down = contract_rows(activated, grad_low)
    d_wout = contract_rows(attended, grad_low)
    d_act = contract_cols(grad_low, w_down)
    _, gelu_pull = jax.vjp(lambda value: jax.nn.gelu(value, approximate=True), upward)
    d_upward = gelu_pull(d_act)[0].astype(jnp.bfloat16)
    d_wup = contract_rows(hidden, d_upward)
    d_bup = jnp.sum(d_upward.astype(jnp.float32), axis=0)
    d_attended = contract_cols(grad_low, w_out).astype(jnp.bfloat16)
    dq_parts = []
    dk_parts = []
    dv_parts = []
    delta_parts = []
    for index, start in enumerate(range(0, width, span)):
        masked = block_scores(start)
        probs = jnp.where(allowed[None], jnp.exp(masked - lse_parts[index]), 0.0)
        d_heads = heads_of(d_attended, start, row_count)
        d_probs = jnp.einsum(
            "qhd,khd->hqk",
            d_heads,
            heads_of(values_all, start, total_keys),
            preferred_element_type=jnp.float32,
        )
        delta = jnp.sum(probs * d_probs, axis=-1, keepdims=True)
        d_scores = (probs * (d_probs - delta)).astype(jnp.bfloat16)
        d_query = (
            jnp.einsum(
                "hqk,khd->qhd",
                d_scores,
                heads_of(keys_all, start, total_keys),
                preferred_element_type=jnp.float32,
            )
            * scale
        )
        dq_parts.append(d_query.reshape(row_count, span))
        delta_parts.append(delta[:, :, 0].T)
        d_keyed = (
            jnp.einsum(
                "hqk,qhd->khd",
                d_scores,
                heads_of(query, start, row_count),
                preferred_element_type=jnp.float32,
            )
            * scale
        )
        d_valued = jnp.einsum(
            "hqk,qhd->khd", probs.astype(jnp.bfloat16), d_heads, preferred_element_type=jnp.float32
        )
        dk_parts.append(d_keyed.reshape(total_keys, span))
        dv_parts.append(d_valued.reshape(total_keys, span))
    keys_grad_all = jnp.concatenate(dk_parts, axis=1)
    values_grad_all = jnp.concatenate(dv_parts, axis=1)
    keys_grad, values_grad = (
        lax.psum_scatter(
            keys_grad_all.astype(jnp.bfloat16), "ctx", scatter_dimension=0, tiled=True
        ).astype(jnp.float32),
        lax.psum_scatter(
            values_grad_all.astype(jnp.bfloat16), "ctx", scatter_dimension=0, tiled=True
        ).astype(jnp.float32),
    )
    query_grad = rotate_back(
        jnp.concatenate(dq_parts, axis=1).reshape(row_count, head_count, HEAD_DIM), cosine, sine
    ).reshape(row_count, width)
    keyed_grad = rotate_back(
        keys_grad.reshape(row_count, head_count, HEAD_DIM), cosine, sine
    ).reshape(row_count, width)
    d_joined = jnp.concatenate([query_grad, keyed_grad, values_grad], axis=1).astype(jnp.bfloat16)
    d_wqkv = contract_rows(hidden, d_joined)
    d_bqkv = jnp.sum(d_joined.astype(jnp.float32), axis=0)
    d_hidden = contract_cols(d_joined, w_qkv) + contract_cols(d_upward, w_up)
    d_gain = jnp.sum(d_hidden * normed, axis=0)
    d_shift = jnp.sum(d_hidden, axis=0)
    d_norm = d_hidden * gain_f
    d_inputs = inv_std * (
        d_norm
        - jnp.mean(d_norm, axis=-1, keepdims=True)
        - normed * jnp.mean(d_norm * normed, axis=-1, keepdims=True)
    )
    back = (grad_out + d_inputs).astype(jnp.bfloat16)
    return (
        result,
        back,
        (d_gain, d_shift, d_wqkv, d_bqkv, d_wout, row_total, d_wup, d_bup, d_down, row_total),
    )


def body(
    tokens,
    cotangent,
    lengths,
    deal,
    ln_gain,
    ln_bias,
    w_qkv,
    b_qkv,
    w_out,
    b_out,
    w_up,
    b_up,
    w_down,
    b_down,
):
    shards = (ln_gain, ln_bias, w_qkv, b_qkv, w_out, b_out, w_up, b_up, w_down, b_down)
    shard_count = lax.axis_size("fsdp")
    summed = tuple(
        (
            jnp.zeros((piece.shape[0] * shard_count,) + piece.shape[1:], jnp.float32)
            for piece in shards
        )
    )
    results = []
    backs = []
    for micro_index in range(tokens.shape[1]):
        gathered = (
            lax.all_gather(ln_gain, "fsdp", axis=0, tiled=True),
            lax.all_gather(ln_bias, "fsdp", axis=0, tiled=True),
            lax.all_gather(w_qkv, "fsdp", axis=0, tiled=True),
            lax.all_gather(b_qkv, "fsdp", axis=0, tiled=True),
            lax.all_gather(w_out, "fsdp", axis=0, tiled=True),
            lax.all_gather(b_out, "fsdp", axis=0, tiled=True),
            lax.all_gather(w_up, "fsdp", axis=0, tiled=True),
            lax.all_gather(b_up, "fsdp", axis=0, tiled=True),
            lax.all_gather(w_down, "fsdp", axis=0, tiled=True),
            lax.all_gather(b_down, "fsdp", axis=0, tiled=True),
        )
        result, back, local = layer_step(
            gathered,
            tokens[0, micro_index],
            cotangent[0, micro_index],
            lengths[0, micro_index],
            deal[0, micro_index],
        )
        results.append(result)
        backs.append(back)
        summed = tuple((older + newer for older, newer in zip(summed, local)))
    summed = (
        lax.psum_scatter(
            summed[0].astype(jnp.bfloat16), "fsdp", scatter_dimension=0, tiled=True
        ).astype(jnp.float32),
        lax.psum_scatter(
            summed[1].astype(jnp.bfloat16), "fsdp", scatter_dimension=0, tiled=True
        ).astype(jnp.float32),
        lax.psum_scatter(
            summed[2].astype(jnp.bfloat16), "fsdp", scatter_dimension=0, tiled=True
        ).astype(jnp.float32),
        lax.psum_scatter(
            summed[3].astype(jnp.bfloat16), "fsdp", scatter_dimension=0, tiled=True
        ).astype(jnp.float32),
        lax.psum_scatter(
            summed[4].astype(jnp.bfloat16), "fsdp", scatter_dimension=0, tiled=True
        ).astype(jnp.float32),
        lax.psum_scatter(
            summed[5].astype(jnp.bfloat16), "fsdp", scatter_dimension=0, tiled=True
        ).astype(jnp.float32),
        lax.psum_scatter(
            summed[6].astype(jnp.bfloat16), "fsdp", scatter_dimension=0, tiled=True
        ).astype(jnp.float32),
        lax.psum_scatter(
            summed[7].astype(jnp.bfloat16), "fsdp", scatter_dimension=0, tiled=True
        ).astype(jnp.float32),
        lax.psum_scatter(
            summed[8].astype(jnp.bfloat16), "fsdp", scatter_dimension=0, tiled=True
        ).astype(jnp.float32),
        lax.psum_scatter(
            summed[9].astype(jnp.bfloat16), "fsdp", scatter_dimension=0, tiled=True
        ).astype(jnp.float32),
    )
    totals = (
        lax.psum(summed[0].astype(jnp.bfloat16), ("dp", "ctx")).astype(jnp.float32),
        lax.psum(summed[1].astype(jnp.bfloat16), ("dp", "ctx")).astype(jnp.float32),
        lax.psum(summed[2].astype(jnp.bfloat16), ("dp", "ctx")).astype(jnp.float32),
        lax.psum(summed[3].astype(jnp.bfloat16), ("dp", "ctx")).astype(jnp.float32),
        lax.psum(summed[4].astype(jnp.bfloat16), ("dp", "ctx")).astype(jnp.float32),
        lax.psum(summed[5].astype(jnp.bfloat16), ("dp", "ctx")).astype(jnp.float32),
        lax.psum(summed[6].astype(jnp.bfloat16), ("dp", "ctx")).astype(jnp.float32),
        lax.psum(summed[7].astype(jnp.bfloat16), ("dp", "ctx")).astype(jnp.float32),
        lax.psum(summed[8].astype(jnp.bfloat16), ("dp", "ctx")).astype(jnp.float32),
        lax.psum(summed[9].astype(jnp.bfloat16), ("dp", "ctx")).astype(jnp.float32),
    )
    stacked_out = jnp.stack(results)[None]
    stacked_back = jnp.stack(backs)[None]
    return (
        stacked_out,
        stacked_back,
        totals[0],
        totals[1],
        totals[2],
        totals[3],
        totals[4],
        totals[5],
        totals[6],
        totals[7],
        totals[8],
        totals[9],
    )


def solution(mesh):
    in_specs = (
        P(("dp", "fsdp"), None, "ctx", None),
        P(("dp", "fsdp"), None, "ctx", None),
        P(("dp", "fsdp"), None),
        P(("dp", "fsdp"), None, None),
        P("fsdp"),
        P("fsdp"),
        P("fsdp", None),
        P("fsdp"),
        P("fsdp", None),
        P("fsdp"),
        P("fsdp", None),
        P("fsdp"),
        P("fsdp", None),
        P("fsdp"),
    )
    out_specs = (
        P(("dp", "fsdp"), None, "ctx", None),
        P(("dp", "fsdp"), None, "ctx", None),
        P("fsdp"),
        P("fsdp"),
        P("fsdp", None),
        P("fsdp"),
        P("fsdp", None),
        P("fsdp"),
        P("fsdp", None),
        P("fsdp"),
        P("fsdp", None),
        P("fsdp"),
    )
    return jax.shard_map(body, mesh=mesh, in_specs=in_specs, out_specs=out_specs, check_vma=False)
```

profile of v0, /device:TPU:0, one launch (start us, length us, event | category | flops | bytes accessed | tf_op | source)
XLA Modules:
  0.0 3160.1 jit_solution(15819114740749781028)
XLA Ops:
  34.9 205.6 %all-gather.14.cloned.1.call-done = bf16[2048,6144]{1,0:T(8,128)(2,1)} async-done(((bf16[512,6144]{1,0:T(8,128)(2,1)}), bf16[2048,6144]{1,0:T(8,128)(2,1)}) %all-gather.14.cloned.1.call-update) | async-done | bytes 25165840 | tf_op jit(solution)/shard_map/all_gather | solution.py:251
  306.2 23.7 all-gather.20.cloned.1.call-done
  358.4 53.9 %all-gather.16.cloned.1.call-done = bf16[1024,2048]{1,0:T(8,128)(2,1)} async-done(((bf16[256,2048]{1,0:T(8,128)(2,1)}), bf16[1024,2048]{1,0:T(8,128)(2,1)}) %all-gather.16.cloned.1.call-update) | async-done | bytes 4194320 | tf_op jit(solution)/shard_map/all_gather | solution.py:86
  423.9 69.8 %all-gather.26.cloned.1.call-done = bf16[1024,2048]{1,0:T(8,128)(2,1)} async-done(((bf16[256,2048]{1,0:T(8,128)(2,1)}), bf16[1024,2048]{1,0:T(8,128)(2,1)}) %all-gather.26.cloned.1.call-update) | async-done | bytes 4194320 | tf_op jit(solution)/shard_map/all_gather | solution.py:86
  498.9 75.3 %all-gather.18.cloned.1.call-done = bf16[1024,2048]{0,1:T(8,128)(2,1)} async-done(((bf16[256,2048]{0,1:T(8,128)(2,1)}), bf16[1024,2048]{0,1:T(8,128)(2,1)}) %all-gather.18.cloned.1.call-update) | async-done | bytes 4194320 | tf_op jit(solution)/shard_map/all_gather | solution.py:85
  586.8 68.1 %all-gather.28.cloned.1.call-done = bf16[1024,2048]{0,1:T(8,128)(2,1)} async-done(((bf16[256,2048]{0,1:T(8,128)(2,1)}), bf16[1024,2048]{0,1:T(8,128)(2,1)}) %all-gather.28.cloned.1.call-update) | async-done | bytes 4194320 | tf_op jit(solution)/shard_map/all_gather | solution.py:85
  742.1 27.0 multiply_convert_fusion.7
  851.0 26.9 multiply_convert_fusion.3
  1014.4 31.4 reduce-scatter.15.cloned.1.call-done
  1066.5 59.4 %reduce-scatter.19.cloned.1.call-done = bf16[256,2048]{0,1:T(8,128)(2,1)} async-done(((bf16[1024,2048]{0,1:T(8,128)(2,1)}), bf16[256,2048]{0,1:T(8,128)(2,1)}) %reduce-scatter.19.cloned.1.call-update) | async-done | bytes 1048592 | tf_op jit(solution)/shard_map/reduce_scatter | solution.py:191
  1125.9 32.0 %add_convert_fusion.2 = bf16[2048,6144]{1,0:T(8,128)(2,1)} fusion(f32[2048,6144]{1,0:T(8,128)} %fusion.190, bf16[256,2048]{0,1:T(8,128)(2,1)} %reduce-scatter.19.cloned.1.call-done, bf16[256,2048]{0,1:T(8,128)(2,1)} %bitcast.429, bf16[256,2048]{0,1:T(8,128)(2,1)S(1)} %bitcast.426, f32[256]{0:T(256)S(1)} %copy-done.110, f32[256]{0:T(256)S(1)} %copy-done.107, ...), kind=kOutput, calls=%fused_computation.2 | convolution fusion | flops 6480199680 | bytes 79710208 | tf_op jit(solution)/shard_map/dot_general | solution.py:15
  1167.0 258.5 %all-gather.22.cloned.1.call-done = bf16[2048,8192]{1,0:T(8,128)(2,1)} async-done(((bf16[512,8192]{1,0:T(8,128)(2,1)}), bf16[2048,8192]{1,0:T(8,128)(2,1)}) %all-gather.22.cloned.1.call-update) | async-done | bytes 33554448 | tf_op jit(solution)/shard_map/all_gather | solution.py:255
  1466.2 258.3 %all-gather.24.cloned.1.call-done = bf16[8192,2048]{1,0:T(8,128)(2,1)} async-done(((bf16[2048,2048]{1,0:T(8,128)(2,1)}), bf16[8192,2048]{1,0:T(8,128)(2,1)}) %all-gather.24.cloned.1.call-update) | async-done | bytes 33554448 | tf_op jit(solution)/shard_map/all_gather | solution.py:257
  1724.5 21.7 convert_reduce_fusion.1
  1746.3 22.1 convert_reduce_fusion
  1768.4 27.0 fusion.207
  1795.4 37.4 %add_convert_fusion.1 = bf16[2048,8192]{1,0:T(8,128)(2,1)} fusion(f32[2048,8192]{1,0:T(8,128)} %fusion.207, bf16[256,8192]{1,0:T(8,128)(2,1)} %get-tuple-element.162, f32[256]{0:T(256)S(1)} %copy-done.110, f32[256]{0:T(256)S(1)} %copy-done.107, f32[2048]{0:T(1024)S(1)} %bitcast.481, f32[2048]{0:T(1024)S(1)} %bitcast.469, ...), kind=kOutput, calls=%fused_computation.1 | convolution fusion | flops 8626634752 | bytes 105924608 | tf_op jit(solution)/shard_map/dot_general | solution.py:15
  1832.8 29.9 fusion.192
  1862.7 39.7 %add_convert_fusion = bf16[8192,2048]{1,0:T(8,128)(2,1)} fusion(f32[8192,2048]{1,0:T(8,128)} %fusion.192, f32[256]{0:T(256)S(1)} %copy-done.154, bf16[1,2,256,2048]{3,2,1,0:T(8,128)(2,1)} %param.15, f32[256,8192]{1,0:T(8,128)} %convolution_add_fusion), kind=kOutput, calls=%fused_computation | convolution fusion | flops 8643936256 | bytes 110101504 | tf_op jit(solution)/shard_map/dot_general | solution.py:15
  1980.1 59.7 %reduce-scatter.21.cloned.1.call-done = bf16[512,6144]{1,0:T(8,128)(2,1)} async-done(((bf16[2048,6144]{1,0:T(8,128)(2,1)}), bf16[512,6144]{1,0:T(8,128)(2,1)}) %reduce-scatter.21.cloned.1.call-update) | async-done | bytes 6291472 | tf_op jit(solution)/shard_map/reduce_scatter | solution.py:277
  2039.9 291.6 %reduce-scatter.25.cloned.1.call-done = bf16[512,8192]{1,0:T(8,128)(2,1)} async-done(((bf16[2048,8192]{1,0:T(8,128)(2,1)}), bf16[512,8192]{1,0:T(8,128)(2,1)}) %reduce-scatter.25.cloned.1.call-update) | async-done | bytes 8388624
  2331.5 291.9 %reduce-scatter.27.cloned.1.call-done = bf16[2048,2048]{1,0:T(8,128)(2,1)} async-done(((bf16[8192,2048]{1,0:T(8,128)(2,1)}), bf16[2048,2048]{1,0:T(8,128)(2,1)}) %reduce-scatter.27.cloned.1.call-update) | async-done | bytes 8388624
  2711.2 29.8 all-reduce.7
  2746.4 373.6 %all-reduce.12.cloned.1.call-done = (bf16[512,6144]{1,0:T(8,128)(2,1)}, bf16[512,2048]{1,0:T(8,128)(2,1)}, bf16[512,8192]{1,0:T(8,128)(2,1)}, bf16[2048,2048]{1,0:T(8,128)(2,1)}) async-done(((bf16[512,6144]{1,0:T(8,128)(2,1)}, bf16[512,2048]{1,0:T(8,128)(2,1)}, bf16[512,8192]{1,0:T(8,128)(2,1)}, bf16[2048,2048]{1,0:T(8,128)(2,1)}), (bf16[512,6144]{1,0:T(8,128)(2,1)}, bf16[512,2048]{1,0:T(8,128)(2,1)}, ...) | async-done | bytes 25165840 | tf_op jit(solution)/shard_map/psum | solution.py:305
  (643 shorter events, 726.4 us)
Async XLA Ops:
  7.2 233.2 %all-gather.14.cloned.1.call-start = ((), (), s32[]{:S(2)}) async-start(), calls=%async_computation.8 | async-start | bytes 31457280 | tf_op jit(solution)/shard_map/all_gather | solution.py:251
  8.0 322.0 %all-gather.20.cloned.1.call-start = ((), (), s32[]{:S(2)}) async-start(), calls=%async_computation.11 | async-start | bytes 10485760 | tf_op jit(solution)/shard_map/all_gather | solution.py:253
  8.7 403.6 %all-gather.16.cloned.1.call-start = ((), (), s32[]{:S(2)}) async-start(), calls=%async_computation.9 | async-start | bytes 5242880 | tf_op jit(solution)/shard_map/all_gather | solution.py:86
  18.3 237.9 %copy-start.39 = (f32[4,1,512]{2,1,0:T(1,128)}, f32[4,1,512]{2,1,0:T(1,128)S(1)}, u32[]{:S(2)}) copy-start(f32[4,1,512]{2,1,0:T(1,128)S(1)} %convert_element_type.392) | copy-start | bytes 24580
  26.4 229.8 %copy-start.42 = (f32[4,1,512]{2,1,0:T(1,128)}, f32[4,1,512]{2,1,0:T(1,128)S(1)}, u32[]{:S(2)}) copy-start(f32[4,1,512]{2,1,0:T(1,128)S(1)} %convert_element_type.393) | copy-start | bytes 24580
  34.2 218.1 %copy-start.80 = (f32[256]{0:T(256)}, f32[256]{0:T(256)S(1)}, u32[]{:S(2)}) copy-start(f32[256]{0:T(256)S(1)} %get-tuple-element.164) | copy-start | bytes 3076
  34.2 222.0 %copy-start.106 = (f32[256]{0:T(256)}, f32[256]{0:T(256)S(1)}, u32[]{:S(2)}) copy-start(f32[256]{0:T(256)S(1)} %get-tuple-element.163) | copy-start | bytes 3076
  34.9 217.4 %copy-start.99 = (f32[256]{0:T(256)}, f32[256]{0:T(256)S(1)}, u32[]{:S(2)}) copy-start(f32[256]{0:T(256)S(1)} %add_rsqrt_fusion.1) | copy-start | bytes 3076
  256.1 237.5 %all-gather.26.cloned.1.call-start = ((), (), s32[]{:S(2)}) async-start(), calls=%async_computation.14 | async-start | bytes 5242880 | tf_op jit(solution)/shard_map/all_gather | solution.py:86
  271.9 302.2 %all-gather.18.cloned.1.call-start = ((), (), s32[]{:S(2)}) async-start(), calls=%async_computation.10 | async-start | bytes 5242880 | tf_op jit(solution)/shard_map/all_gather | solution.py:85
  286.2 368.8 %all-gather.28.cloned.1.call-start = ((), (), s32[]{:S(2)}) async-start(), calls=%async_computation.15 | async-start | bytes 5242880 | tf_op jit(solution)/shard_map/all_gather | solution.py:85
  304.6 696.2 %reduce-scatter.13.cloned.1.call-start = ((), (), s32[]{:S(2)}) async-start(), calls=%async_computation.16 | async-start | bytes 5242880 | tf_op jit(solution)/shard_map/reduce_scatter | solution.py:188
  782.4 222.3 %reduce-scatter.17.cloned.1.call-start = ((), (), s32[]{:S(2)}) async-start(), calls=%async_computation.18 | async-start | bytes 5242880 | tf_op jit(solution)/shard_map/reduce_scatter | solution.py:188
  891.1 154.7 %reduce-scatter.15.cloned.1.call-start = ((), (), s32[]{:S(2)}) async-start(), calls=%async_computation.17 | async-start | bytes 5242880 | tf_op jit(solution)/shard_map/reduce_scatter | solution.py:191
  910.6 215.3 %reduce-scatter.19.cloned.1.call-start = ((), (), s32[]{:S(2)}) async-start(), calls=%async_computation.19 | async-start | bytes 5242880 | tf_op jit(solution)/shard_map/reduce_scatter | solution.py:191
  930.2 495.3 %all-gather.22.cloned.1.call-start = ((), (), s32[]{:S(2)}) async-start(), calls=%async_computation.12 | async-start | bytes 41943040 | tf_op jit(solution)/shard_map/all_gather | solution.py:255
  931.0 793.5 %all-gather.24.cloned.1.call-start = ((), (), s32[]{:S(2)}) async-start(), calls=%async_computation.13 | async-start | bytes 41943040 | tf_op jit(solution)/shard_map/all_gather | solution.py:257
  931.6 1048.6 %reduce-scatter.23.cloned.1.call-start = ((), (), s32[]{:S(2)}) async-start(), calls=%async_computation.21 | async-start | bytes 10485760 | tf_op jit(solution)/shard_map/reduce_scatter | solution.py:283
  979.6 1060.3 %reduce-scatter.21.cloned.1.call-start = ((), (), s32[]{:S(2)}) async-start(), calls=%async_computation.20 | async-start | bytes 31457280 | tf_op jit(solution)/shard_map/reduce_scatter | solution.py:277
  1157.9 1173.6 %reduce-scatter.25.cloned.1.call-start = ((), (), s32[]{:S(2)}) async-start(), calls=%async_computation.22 | async-start | bytes 41943040
  1447.2 277.3 %copy-start.157 = (f32[256]{0:T(256)S(1)}, f32[256]{0:T(256)}, u32[]{:S(2)}) copy-start(f32[256]{0:T(256)} %copy-done.155) | copy-start | bytes 3076
  1832.8 790.6 %reduce-scatter.27.cloned.1.call-start = ((), (), s32[]{:S(2)}) async-start(), calls=%async_computation.23 | async-start | bytes 41943040
  1902.5 1217.5 %all-reduce.12.cloned.1.call-start = ((), (), s32[]{:S(2)}) async-start(), calls=%async_computation.24 | async-start | bytes 50331648 | tf_op jit(solution)/shard_map/psum | solution.py:305
  2742.2 410.5 %copy-start.158 = (f32[512]{0:T(512)}, f32[512]{0:T(512)S(1)}, u32[]{:S(2)}) copy-start(f32[512]{0:T(512)S(1)} %convert_element_type.381) | copy-start | bytes 6148
  (187 other events, 2265.0 us)
Sparse Core Ops, SparseCore 0:
  9.9 230.4 all-gather.13
  242.3 87.6 all-gather.19
  331.5 80.7 all-gather.15
  414.3 79.2 all-gather.25
  495.0 79.0 all-gather.17
  576.2 78.7 all-gather.27
  782.5 74.9 reduce-scatter.12
  891.2 74.8 reduce-scatter.16
  968.4 77.2 reduce-scatter.14
  1048.6 77.2 reduce-scatter.18
  1127.7 297.7 all-gather.21
  1427.3 297.2 all-gather.23
  1728.1 86.4 reduce-scatter.22
  1817.9 221.9 reduce-scatter.20
  2042.8 288.6 reduce-scatter.24
  2334.7 288.6 reduce-scatter.26
  2626.1 493.8 all-reduce.11
where the time goes:
time: 3170 us; the launch traced here: 3160 us
  waiting for transfers between devices  2120 us (67%)
  matrix products  665 us (21%)
  other arithmetic  161 us (5%)
  local copies, waits for them, and re-layouts  95.5 us (3%)
  blocking collectives  93.8 us (3%)
    unnamed x19, waiting for transfers between devices  586 us
    psum x1, waiting for transfers between devices, body(): lax.psum(summed[2].astype(jnp.bfloat16), ('dp', 'ctx')).astype(jnp.float32)  374 us
    all_gather x1, waiting for transfers between devices, body(): lax.all_gather(w_up, 'fsdp', axis=0, tiled=True)  259 us
    all_gather x1, waiting for transfers between devices, body(): lax.all_gather(w_down, 'fsdp', axis=0, tiled=True)  258 us
    dot_general x8, matrix products, contract_rows(): lax.dot_general(left, right, (((0,), (0,)), ((), ())), preferred_element_...  206 us
    all_gather x1, waiting for transfers between devices, body(): lax.all_gather(w_qkv, 'fsdp', axis=0, tiled=True)  206 us
    all_gather x2, waiting for transfers between devices, layer_step(): lax.all_gather(keyed, 'ctx', axis=0, tiled=True)  143 us
    all_gather x2, waiting for transfers between devices, layer_step(): lax.all_gather(valued, 'ctx', axis=0, tiled=True)  124 us
  transfers between devices with their start and end apart: 17, of which 14 were waited for; matrix products, arithmetic and copies ran while one was open for 24% of the time, Pallas kernels for 0%

commit v1 on v0

--- a/solution.py
+++ b/solution.py
@@ -1,6 +1,8 @@
 import jax
 import jax.numpy as jnp
 from jax import lax
+from jax.experimental import pallas as pl
+from jax.experimental.pallas import tpu as pltpu
 from jax.sharding import PartitionSpec as P
 
 HEAD_DIM = 64
@@ -218,7 +220,7 @@
     )
 
 
-def body(
+def gathered_body(
     tokens,
     cotangent,
     lengths,
@@ -329,6 +331,367 @@
     )
 
 
+SWAP = [(0, 1), (1, 0)]
+
+
+def swap_dp(value):
+    return lax.ppermute(value, "dp", SWAP)
+
+
+def by_core(core, mine, other, axis):
+    first = jnp.where(core == 0, mine, other)
+    second = jnp.where(core == 0, other, mine)
+    return jnp.stack([first, second], axis=axis)
+
+
+def pick(array, index, axis):
+    return lax.dynamic_index_in_dim(array, index, axis, keepdims=False)
+
+
+def to_plane(rows, core, blk):
+    micro, count, width = rows.shape
+    split = rows.reshape(micro, 2, blk, width)
+    received = swap_dp(pick(split, 1 - core, 1))
+    lined = by_core(core, pick(split, core, 1), received, 0).reshape(2 * micro, blk, width)
+    dealt = lax.all_to_all(lined, "ctx", 0, 0, tiled=True)
+    own = lax.all_gather(dealt.reshape(-1, width), "fsdp", axis=0, tiled=True)
+    return own, swap_dp(own)
+
+
+def to_home(part_own, part_oth, core, micro, blk):
+    width = part_own.shape[1]
+    total = (part_own + swap_dp(part_oth).astype(jnp.float32)).astype(jnp.bfloat16)
+    mine = lax.psum_scatter(total, "fsdp", scatter_dimension=0, tiled=True)
+    lined = lax.all_to_all(mine.reshape(-1, blk, width), "ctx", 0, 0, tiled=True)
+    lined = lined.reshape(2, micro, blk, width)
+    kept = pick(lined, core, 0)
+    received = swap_dp(pick(lined, 1 - core, 0))
+    return by_core(core, kept, received, 1).reshape(micro, 2 * blk, width)
+
+
+def columns_of(weight, parts, core, shards):
+    rows, total = weight.shape
+    width = total // (parts * shards * 2)
+    mine = pick(weight.reshape(rows, parts, shards, 2, width), core, 3)
+    sent = mine.transpose(2, 0, 1, 3).reshape(shards * rows, parts * width)
+    return lax.all_to_all(sent, "fsdp", 0, 0, tiled=True)
+
+
+def line_sum(value, place):
+    inward = lax.ppermute(value, "ctx", [(0, 1), (3, 2)])
+    half = value + inward
+    across = lax.ppermute(half, "ctx", [(1, 2), (2, 1)])
+    whole = half + across
+    outward = lax.ppermute(whole, "ctx", [(1, 0), (2, 3)])
+    inner = (place == 1) | (place == 2)
+    return jnp.where(inner, whole, outward)
+
+
+def sum_ctx(value, place):
+    if lax.axis_size("ctx") == 4:
+        return line_sum(value, place)
+    return lax.psum(value, "ctx")
+
+
+GELU_C = 0.7978845608028654
+GELU_A = 0.044715
+
+
+def gelu_pair(value):
+    square = value * value
+    tanh = jnp.tanh(GELU_C * value * (1.0 + GELU_A * square))
+    half = 0.5 * (1.0 + tanh)
+    slope = half + 0.5 * value * (1.0 - tanh * tanh) * (GELU_C * (1.0 + 3.0 * GELU_A * square))
+    return value * half, slope
+
+
+def rope_tables(seq_len):
+    lane = jnp.arange(2 * HEAD_DIM, dtype=jnp.int32) % HEAD_DIM
+    half = ROT // 2
+    turned = lane < ROT
+    index = jnp.where(turned, lane % half, 0).astype(jnp.float32)
+    freqs = BASE ** (-(index * 2.0) / ROT)
+    angles = jnp.arange(seq_len, dtype=jnp.float32)[:, None] * freqs[None, :]
+    sine = jnp.sin(angles)
+    cosine = jnp.where(turned[None], jnp.cos(angles), 1.0)
+    up = jnp.where((lane < half)[None], -sine, 0.0)
+    down = jnp.where(((lane >= half) & turned)[None], sine, 0.0)
+    return cosine, up, down
+
+
+def attention_call(deal_own, deal_oth, lengths, joined_own, joined_oth, datt_own, datt_oth, blk):
+    seqs, half_rows, wide = joined_own.shape
+    heads_wide = wide // 3
+    pairs = heads_wide // 128
+    seq_len = 2 * half_rows
+    per_side = half_rows // blk
+    step = 256
+    tables = rope_tables(seq_len)
+    scale = HEAD_DIM ** (-0.5)
+    half = ROT // 2
+    contract_last = (((1,), (1,)), ((), ()))
+    contract_first = (((0,), (0,)), ((), ()))
+
+    def kernel(own_at, oth_at, len_at, cos_ref, up_ref, down_ref, q0, k0, v0, d0, q1, k1, v1, d1,
+               att0, dq0, dk0, dv0, att1, dq1, dk1, dv1,
+               qs, ks, vs, ds, att_s, dq_s, dk_s, dv_s):
+        seq = pl.program_id(0)
+        length = len_at[seq]
+
+        def turn(x, at):
+            return (x * cos_ref[at, :] + pltpu.roll(x, 128 - half, 1) * up_ref[at, :]
+                    + pltpu.roll(x, half, 1) * down_ref[at, :])
+
+        def unturn(x, at):
+            return (x * cos_ref[at, :] - pltpu.roll(x, 128 - half, 1) * up_ref[at, :]
+                    - pltpu.roll(x, half, 1) * down_ref[at, :])
+
+        sides = ((own_at, q0, k0, v0, d0, att0, dq0, dk0, dv0), (oth_at, q1, k1, v1, d1, att1, dq1, dk1, dv1))
+        for where_at, q_ref, k_ref, v_ref, d_ref, *_ in sides:
+            for j in range(per_side):
+                at = pl.ds(pl.multiple_of(where_at[seq, j] * blk, blk), blk)
+                here = slice(j * blk, (j + 1) * blk)
+                qs[at, :] = (turn(q_ref[0, here, :].astype(jnp.float32), at)).astype(jnp.bfloat16) * jnp.bfloat16(scale)
+                ks[at, :] = turn(k_ref[0, here, :].astype(jnp.float32), at).astype(jnp.bfloat16)
+                vs[at, :] = v_ref[0, here, :]
+                ds[at, :] = d_ref[0, here, :]
+        att_s[...] = jnp.zeros_like(att_s)
+        dq_s[...] = jnp.zeros_like(dq_s)
+        dk_s[...] = jnp.zeros_like(dk_s)
+        dv_s[...] = jnp.zeros_like(dv_s)
+        lane = lax.broadcasted_iota(jnp.int32, (1, 128), 1)
+
+        def one_head(h, carry):
+            chosen = (lane // HEAD_DIM) == h
+            keep_f = jnp.where(chosen, 1.0, 0.0)
+            keep = keep_f.astype(jnp.bfloat16)
+            for i in range(seq_len // step):
+                rows = slice(i * step, (i + 1) * step)
+                n = (i + 1) * step
+                q = qs[rows, :] * keep
+                d = ds[rows, :] * keep
+                k = ks[:n, :]
+                v = vs[:n, :]
+                s = lax.dot_general(q, k, contract_last, preferred_element_type=jnp.float32)
+                q_pos = i * step + lax.broadcasted_iota(jnp.int32, (step, 1), 0)
+                limit = jnp.minimum(q_pos, length - 1)
+                k_pos = lax.broadcasted_iota(jnp.int32, (step, n), 1)
+                s = jnp.where(k_pos <= limit, s, -1e30)
+                e = jnp.exp(s - jnp.max(s, axis=-1, keepdims=True))
+                p = e * (1.0 / jnp.sum(e, axis=-1, keepdims=True))
+                p_low = p.astype(jnp.bfloat16)
+                dp = lax.dot_general(d, v, contract_last, preferred_element_type=jnp.float32)
+                delta = jnp.sum(p * dp, axis=-1, keepdims=True)
+                dsc = (p * (dp - delta)).astype(jnp.bfloat16)
+                att_s[rows, :] += keep_f * jnp.dot(p_low, v, preferred_element_type=jnp.float32)
+                dq_s[rows, :] += keep_f * jnp.dot(dsc, k, preferred_element_type=jnp.float32)
+                dk_s[:n, :] += lax.dot_general(dsc, q, contract_first, preferred_element_type=jnp.float32)
+                dv_s[:n, :] += lax.dot_general(p_low, d, contract_first, preferred_element_type=jnp.float32)
+            return carry
+
+        lax.fori_loop(0, 128 // HEAD_DIM, one_head, 0)
+        for where_at, _, _, _, _, att_ref, dq_ref, dk_ref, dv_ref in sides:
+            for j in range(per_side):
+                at = pl.ds(pl.multiple_of(where_at[seq, j] * blk, blk), blk)
+                here = slice(j * blk, (j + 1) * blk)
+                att_ref[0, here, :] = att_s[at, :].astype(jnp.bfloat16)
+                dq_ref[0, here, :] = unturn(dq_s[at, :] * scale, at).astype(jnp.bfloat16)
+                dk_ref[0, here, :] = unturn(dk_s[at, :], at).astype(jnp.bfloat16)
+                dv_ref[0, here, :] = dv_s[at, :].astype(jnp.bfloat16)
+
+    def lanes(offset):
+        return pl.BlockSpec((1, half_rows, 128), lambda s, p, *_: (s, 0, offset + p))
+
+    table = pl.BlockSpec((seq_len, 128), lambda s, p, *_: (0, 0))
+    side_in = [lanes(0), lanes(pairs), lanes(2 * pairs), lanes(0)]
+    side_out = [lanes(0)] * 4
+    narrow = jax.ShapeDtypeStruct((seqs, half_rows, heads_wide), jnp.bfloat16)
+    work = seqs * pairs * 2 * seq_len * seq_len * 64
+    result = pl.pallas_call(
+        kernel,
+        grid_spec=pltpu.PrefetchScalarGridSpec(
+            num_scalar_prefetch=3,
+            grid=(seqs, pairs),
+            in_specs=[table] * 3 + side_in + side_in,
+            out_specs=side_out + side_out,
+            scratch_shapes=[pltpu.VMEM((seq_len, 128), jnp.bfloat16)] * 4
+            + [pltpu.VMEM((seq_len, 128), jnp.float32)] * 4,
+        ),
+        out_shape=[narrow] * 8,
+        compiler_params=pltpu.CompilerParams(
+            dimension_semantics=("arbitrary", "arbitrary"), vmem_limit_bytes=56 * 1024 * 1024
+        ),
+        cost_estimate=pl.CostEstimate(
+            flops=12 * work, transcendentals=work // 64, bytes_accessed=2 * 8 * seqs * seq_len * heads_wide
+        ),
+    )(deal_own, deal_oth, lengths, *tables, joined_own, joined_own, joined_own, datt_own,
+      joined_oth, joined_oth, joined_oth, datt_oth)
+    return result[:4], result[4:]
+
+
+def plane_body(
+    tokens, cotangent, lengths, deal, ln_gain, ln_bias, w_qkv, b_qkv, w_out, b_out, w_up, b_up, w_down, b_down
+):
+    shards = lax.axis_size("fsdp")
+    core = lax.axis_index("dp")
+    place = lax.axis_index("ctx")
+    shard = lax.axis_index("fsdp")
+    _, micro, rows, width = tokens.shape
+    blocks = deal.shape[2]
+    lined = lax.axis_size("ctx")
+    blk = rows * lined // blocks
+    hidden_units = w_down.shape[0] // 2
+    head_cols = w_out.shape[0] // 2
+    low = jnp.bfloat16
+    wide = jnp.float32
+
+    small = jnp.concatenate([ln_gain, ln_bias, b_qkv, b_out, b_up, b_down])
+    small = lax.all_gather(small, "fsdp", axis=0, tiled=False).astype(wide)
+    bounds = [0]
+    for piece in (ln_gain, ln_bias, b_qkv, b_out, b_up, b_down):
+        bounds.append(bounds[-1] + piece.shape[0])
+    gain, shift, bias_qkv, bias_out, bias_up, bias_down = (
+        small[:, a:b].reshape(-1) for a, b in zip(bounds[:-1], bounds[1:])
+    )
+    meta = jnp.concatenate([deal[0].reshape(-1), lengths[0]])
+    meta = lax.all_gather(meta, ("dp", "fsdp"), axis=0, tiled=False).reshape(2, shards, -1)
+    meta = pick(meta, place // micro, 0)
+    plane_deal = pick(meta[:, : micro * blocks].reshape(shards, micro, blocks), place % micro, 1)
+    plane_len = pick(meta[:, micro * blocks :], place % micro, 1)
+    plane_deal = plane_deal.reshape(shards, lined, 2)
+    deal_own = pick(plane_deal, core, 2)
+    deal_oth = pick(plane_deal, 1 - core, 2)
+
+    own_blocks = lax.dynamic_slice_in_dim(deal[0], 2 * place, 2, axis=1)
+    local_pos = (own_blocks[:, :, None] * blk + jnp.arange(blk, dtype=jnp.int32)).reshape(micro, rows)
+    valid = (local_pos < lengths[0][:, None])[:, :, None]
+    inputs = tokens[0].astype(wide)
+    centered = inputs - jnp.mean(inputs, axis=-1, keepdims=True)
+    inv_std = lax.rsqrt(jnp.mean(centered * centered, axis=-1, keepdims=True) + EPS)
+    hidden_home = (centered * inv_std * gain + shift).astype(low)
+    gout_home = jnp.where(valid, cotangent[0], jnp.zeros((), low))
+
+    up_w = columns_of(w_up, 1, core, shards)
+    hidden = to_plane(hidden_home, core, blk)
+    qkv_w = columns_of(w_qkv, 3, core, shards)
+    gout = to_plane(gout_home, core, blk)
+    down_w = lax.dynamic_slice_in_dim(w_down, core * hidden_units, hidden_units, 0)
+    out_w = lax.dynamic_slice_in_dim(w_out, core * head_cols, head_cols, 0)
+    up_b = lax.dynamic_slice_in_dim(bias_up, (2 * shard + core) * hidden_units, hidden_units)
+    qkv_b = pick(bias_qkv.reshape(3, 2 * shards, head_cols), 2 * shard + core, 1).reshape(-1)
+
+    acts, dups, joins, datts = [], [], [], []
+    for h, g in zip(hidden, gout):
+        upward = jnp.dot(h, up_w, preferred_element_type=wide) + up_b
+        act, slope = gelu_pair(upward)
+        acts.append(act.astype(low))
+        joins.append((jnp.dot(h, qkv_w, preferred_element_type=wide) + qkv_b).astype(low))
+        dups.append((contract_cols(g, down_w) * slope.astype(low).astype(wide)).astype(low))
+        datts.append(contract_cols(g, out_w).astype(low))
+
+    def both(first, second):
+        return (contract_rows(first[0], second[0]) + contract_rows(first[1], second[1])).astype(low)
+
+    g_down = both(acts, gout)
+    g_up = both(hidden, dups)
+    g_up = lax.all_to_all(g_up, "fsdp", 0, 0, tiled=True)
+    t_down = sum_ctx(g_down, place)
+    t_up = sum_ctx(g_up, place)
+
+    per_seq = (shards, lined * blk, -1)
+    side_own, side_oth = attention_call(
+        deal_own, deal_oth, plane_len,
+        joins[0].reshape(per_seq), joins[1].reshape(per_seq),
+        datts[0].reshape(per_seq), datts[1].reshape(per_seq), blk,
+    )
+    flat = lambda piece: piece.reshape(shards * lined * blk, -1)
+    atts = [flat(side_own[0]), flat(side_oth[0])]
+    dfused = [jnp.concatenate([flat(piece) for piece in side[1:]], axis=1) for side in (side_own, side_oth)]
+
+    g_out = both(atts, gout)
+    g_qkv = both(hidden, dfused)
+    g_qkv = lax.all_to_all(g_qkv, "fsdp", 0, 0, tiled=True)
+    t_out = sum_ctx(g_out, place)
+    t_qkv = sum_ctx(g_qkv, place)
+
+    def forward_part(side):
+        return jnp.dot(acts[side], down_w, preferred_element_type=wide) + jnp.dot(
+            atts[side], out_w, preferred_element_type=wide
+        )
+
+    def backward_part(side):
+        return contract_cols(dups[side], up_w) + contract_cols(dfused[side], qkv_w)
+
+    mixed = to_home(forward_part(0), forward_part(1).astype(low), core, micro, blk)
+    d_hidden = to_home(backward_part(0), backward_part(1).astype(low), core, micro, blk).astype(wide)
+
+    result = jnp.where(valid, inputs + mixed.astype(wide) + bias_out + bias_down, 0.0).astype(low)
+    normed = centered * inv_std
+    d_norm = d_hidden * gain
+    d_inputs = inv_std * (
+        d_norm
+        - jnp.mean(d_norm, axis=-1, keepdims=True)
+        - normed * jnp.mean(d_norm * normed, axis=-1, keepdims=True)
+    )
+    back = (gout_home.astype(wide) + d_inputs).astype(low)
+
+    def column_sum(pair):
+        return sum(jnp.sum(piece.astype(wide), axis=0) for piece in pair)
+
+    spot = 2 * shard + core
+    s_up = lax.dynamic_update_slice_in_dim(
+        jnp.zeros((2 * shards * hidden_units,), wide), column_sum(dups), spot * hidden_units, 0
+    )
+    s_qkv = lax.dynamic_update_slice(
+        jnp.zeros((3, 2 * shards, head_cols), wide),
+        column_sum(dfused).reshape(3, 1, head_cols), (0, spot, 0),
+    ).reshape(-1)
+    s_gout = jnp.sum(gout_home.astype(wide), axis=(0, 1))
+    s_gain = jnp.sum(d_hidden * normed, axis=(0, 1))
+    s_shift = jnp.sum(d_hidden, axis=(0, 1))
+    sums = lax.psum(jnp.concatenate([s_gain, s_shift, s_gout, s_up, s_qkv]), ("dp", "ctx", "fsdp"))
+    at = 0
+    pieces = []
+    for size in (width, width, width, s_up.shape[0], s_qkv.shape[0]):
+        part = sums[at : at + size]
+        pieces.append(lax.dynamic_slice_in_dim(part, shard * (size // shards), size // shards))
+        at += size
+    d_gain, d_shift, d_row, d_bup, d_bqkv = pieces
+
+    def rows_out(mine):
+        pair = by_core(core, mine, swap_dp(mine), 0)
+        return pair.reshape(-1, mine.shape[1]).astype(wide)
+
+    def cols_out(mine, parts):
+        local = mine.shape[0] // shards
+        pair = by_core(core, mine, swap_dp(mine), 0)
+        pair = pair.reshape(2, shards, local, parts, -1).transpose(2, 3, 1, 0, 4)
+        return pair.reshape(local, -1).astype(wide)
+
+    return (
+        result[None], back[None], d_gain, d_shift, cols_out(t_qkv, 3), d_bqkv,
+        rows_out(t_out), d_row, cols_out(t_up, 1), d_bup, rows_out(t_down), d_row,
+    )
+
+
+def plane_fits(mesh, shapes):
+    tokens, _, _, deal = shapes[:4]
+    sizes = dict(mesh.shape)
+    dp, ctx, fsdp = sizes["dp"], sizes["ctx"], sizes["fsdp"]
+    micro, seq_len, width = tokens.shape[1:]
+    blocks = deal.shape[2]
+    heads = width // HEAD_DIM
+    return (
+        dp == 2
+        and dp * micro == ctx
+        and tokens.shape[0] == dp * fsdp
+        and blocks == dp * ctx
+        and heads % (2 * dp * fsdp) == 0
+        and seq_len % 256 == 0
+        and (seq_len // blocks) % 128 == 0
+    )
+
+
 def solution(mesh):
     in_specs = (
         P(("dp", "fsdp"), None, "ctx", None),
@@ -360,4 +723,9 @@
         P("fsdp", None),
         P("fsdp"),
     )
-    return jax.shard_map(body, mesh=mesh, in_specs=in_specs, out_specs=out_specs, check_vma=False)
+
+    def program(*arrays):
+        body = plane_body if plane_fits(mesh, arrays) else gathered_body
+        return jax.shard_map(body, mesh=mesh, in_specs=in_specs, out_specs=out_specs, check_vma=False)(*arrays)
+
+    return program

time: 3170 us -> 1570 us (0.50)
  waiting for transfers between devices: 2120 us -> 659 us
  matrix products: 665 us -> 312 us
  Pallas kernels: 0 us -> 70.9 us
  starting transfers between devices: 1.52 us -> 65 us
  blocking collectives: 93.8 us -> 155 us
  local copies, waits for them, and re-layouts: 95.5 us -> 144 us
    all_gather x8 -> x2, waiting for transfers between devices: 1010 us -> 118 us  [to_plane(): own = lax.all_gather(dealt.reshape(-1, width), 'fsdp', axis=0, tiled=True)]
    unnamed x19 -> x5, waiting for transfers between devices: 586 us -> 0.08 us
    ppermute x0 -> x24, waiting for transfers between devices: none -> 408 us  [the longest x4 248 us: line_sum(): outward = lax.ppermute(whole, 'ctx', [(1, 0), (2, 3)])]
    psum x1, waiting for transfers between devices: 374 us -> 113 us  [plane_body(): lax.psum(jnp.concatenate([s_gain, s_shift, s_gout, s_up, s_qkv]), ('dp',...]
    dot_general x56 -> x8, matrix products: 338 us -> 108 us  [the longest x2 37.9 us: forward_part(): jnp.dot(acts[side], down_w, preferred_element_type=wide)]
    reduce_scatter x6 -> x2, waiting for transfers between devices: 151 us -> 0.01 us  [to_home(): mine = lax.psum_scatter(total, 'fsdp', scatter_dimension=0, tiled=True)]
    dot_general x8, matrix products: 206 us -> 93 us  [contract_rows(): lax.dot_general(left, right, (((0,), (0,)), ((), ())), preferred_element_...]
    all_to_all x0 -> x2, blocking collectives: none -> 105 us  [to_plane(): dealt = lax.all_to_all(lined, 'ctx', 0, 0, tiled=True)]
  transfers between devices with their start and end apart: 17 -> 35, of which waited for: 14 -> 10; matrix products, arithmetic and copies ran while one was open for 24% -> 32% of each run, Pallas kernels for 0% -> 5%
where the time goes in v1:
time: 1570 us; the launch traced here: 1560 us
  waiting for transfers between devices  659 us (42%)
  matrix products  312 us (20%)
  blocking collectives  155 us (10%)
  local copies, waits for them, and re-layouts  144 us (9%)
  other arithmetic  135 us (9%)
  Pallas kernels  70.9 us (5%)
  starting transfers between devices  65 us (4%)
  between operations  15.9 us (1%)
    ppermute x4, waiting for transfers between devices, line_sum(): outward = lax.ppermute(whole, 'ctx', [(1, 0), (2, 3)])  248 us
    ppermute x4, waiting for transfers between devices, line_sum(): inward = lax.ppermute(value, 'ctx', [(0, 1), (3, 2)])  155 us
    all_gather x2, waiting for transfers between devices, to_plane(): own = lax.all_gather(dealt.reshape(-1, width), 'fsdp', axis=0, tiled=True)  118 us
    psum x1, waiting for transfers between devices, plane_body(): lax.psum(jnp.concatenate([s_gain, s_shift, s_gout, s_up, s_qkv]), ('dp',...  113 us
    dot_general x8, matrix products, contract_cols(): lax.dot_general(left, right, (((1,), (1,)), ((), ())), preferred_element_...  111 us
    all_to_all x2, blocking collectives, to_plane(): dealt = lax.all_to_all(lined, 'ctx', 0, 0, tiled=True)  105 us
    dot_general x8, matrix products, contract_rows(): lax.dot_general(left, right, (((0,), (0,)), ((), ())), preferred_element_...  93 us
    pallas_call x1, Pallas kernels, attention_call(): pl.pallas_call(kernel, grid_spec=pltpu.PrefetchScalarGridSpec(num_scalar_...  70.9 us
  transfers between devices with their start and end apart: 35, of which 10 were waited for; matrix products, arithmetic and copies ran while one was open for 32% of the time, Pallas kernels for 5%

profile of v1, /device:TPU:0, one launch (start us, length us, event | category | flops | bytes accessed | tf_op | source)
XLA Modules:
  0.0 1557.1 jit_solution(13846563735945005513)
XLA Ops:
  36.3 53.3 %all_to_all.68 = bf16[4,128,2048]{2,1,0:T(8,128)(2,1)} all-to-all(bf16[4,128,2048]{2,1,0:T(8,128)(2,1)S(1)} %bitcast.228), channel_id=1, replica_groups=mesh['dp'=2,'ctx'=4,'fsdp'=4] {'ctx'}, dimensions={0} | all-to-all | bytes 4194304 | tf_op jit(solution)/shard_map/all_to_all | solution.py:356
  95.3 52.0 %all_to_all.69 = bf16[4,128,2048]{2,1,0:T(8,128)(2,1)} all-to-all(bf16[4,128,2048]{2,1,0:T(8,128)(2,1)S(1)} %bitcast.229), channel_id=1, replica_groups=mesh['dp'=2,'ctx'=4,'fsdp'=4] {'ctx'}, dimensions={0} | all-to-all | bytes 4194304 | tf_op jit(solution)/shard_map/all_to_all | solution.py:356
  147.3 28.2 %all-gather.6.cloned.1.call-done = bf16[2048,2048]{1,0:T(8,128)(2,1)} async-done(((bf16[512,2048]{1,0:T(8,128)(2,1)}), bf16[2048,2048]{1,0:T(8,128)(2,1)}) %all-gather.6.cloned.1.call-update) | async-done | bytes 8388624 | tf_op jit(solution)/shard_map/all_gather | solution.py:357
  175.5 89.5 %all-gather.8.cloned.1.call-done = bf16[2048,2048]{1,0:T(8,128)(2,1)} async-done(((bf16[512,2048]{1,0:T(8,128)(2,1)}), bf16[2048,2048]{1,0:T(8,128)(2,1)}) %all-gather.8.cloned.1.call-update) | async-done | bytes 8388624 | tf_op jit(solution)/shard_map/all_gather | solution.py:357
  283.8 39.5 %all-reduce.1 = s32[2,4,18]{2,1,0:T(4,128)S(1)} all-reduce(s32[2,4,18]{2,1,0:T(4,128)S(1)} %reshape.372), channel_id=3, replica_groups=mesh['dp'=2,'ctx'=4,'fsdp'=4] {'dp','fsdp'}, use_global_device_ids=true, to_apply=%add | all-reduce | flops 144 | bytes 1152
  395.1 70.9 %shard_map.229 = (bf16[4,512,256]{2,1,0:T(8,128)(2,1)}, bf16[4,512,256]{2,1,0:T(8,128)(2,1)}, bf16[4,512,256]{2,1,0:T(8,128)(2,1)}, bf16[4,512,256]{2,1,0:T(8,12...) custom-call(s32[4,4]{1,0:T(4,128)} %bitcast.279, ...), custom_call_target="tpu_custom_call" | custom-call | flops 12884901888 | bytes 16777216 | tf_op jit(solution)/shard_map/pallas_call | solution.py:510
  490.7 20.3 %convert_reduce_fusion = (f32[1024]{0:T(1024)}, bf16[2048,1024]{1,0:T(8,128)(2,1)S(1)}) fusion(f32[2048,1024]{1,0:T(8,128)S(1)} %fusion.46, f32[1024]{0:T(1024)S(1)} %dynamic_slice.88, bf16[2048,2048]{1,0:T(8,128)(2,1)} %collective-permute-done.3, bf16[2048,2048]{1,0:T(8,128)(2,1)} %param.26, s32[]{:T(128)S(6)} %select_n.260), kind=kOutput, calls=%fused_computation.10 | convolution fusion | flops 8638168064 | bytes 25174020 | tf_op jit(solution)/shard_map/dot_general | solution.py:23
  511.0 16.7 %add_convert_fusion.1 = bf16[2048,2048]{1,0:T(8,128)(2,1)} fusion(f32[2048,2048]{1,0:T(8,128)} %fusion.40, bf16[2048,1024]{1,0:T(8,128)(2,1)S(1)} %get-tuple-element.89, bf16[2048,1024]{1,0:T(8,128)(2,1)} %bitcast.15), kind=kOutput, calls=%fused_computation.2 | convolution fusion | flops 8598323200 | bytes 33554432 | tf_op jit(solution)/shard_map/dot_general | solution.py:23
  544.0 18.9 %convert_reduce_fusion.1 = (f32[1024]{0:T(1024)}, bf16[2048,1024]{1,0:T(8,128)(2,1)}) fusion(f32[2048,1024]{1,0:T(8,128)S(1)} %fusion.45, f32[1024]{0:T(1024)S(1)} %dynamic_slice.88, bf16[2048,2048]{1,0:T(8,128)(2,1)} %all-gather.8.cloned.1.call-done, bf16[2048,2048]{1,0:T(8,128)(2,1)} %param.26, s32[]{:T(128)S(6)} %select_n.260), kind=kOutput, calls=%fused_computation.11 | convolution fusion | flops 8638168064 | bytes 25174020 | tf_op jit(solution)/shard_map/dot_general | solution.py:23
  562.9 14.8 fusion.43
  587.5 19.6 %add_convert_fusion = bf16[2048,2048]{1,0:T(8,128)(2,1)} fusion(bf16[2048,2048]{1,0:T(8,128)(2,1)} %collective-permute-done.6, f32[2048,2048]{1,0:T(8,128)} %fusion.42, bf16[2048,1024]{1,0:T(8,128)(2,1)} %get-tuple-element.87, bf16[2048,1024]{1,0:T(8,128)(2,1)} %bitcast.15), kind=kOutput, calls=%fused_computation.1 | convolution fusion | flops 8606711808 | bytes 41943040 | tf_op jit(solution)/shard_map/dot_general | solution.py:23
  607.1 14.6 fusion.48
  621.8 19.1 %fusion.4 = f32[2048,2048]{1,0:T(8,128)} fusion(bf16[2048,2048]{1,0:T(8,128)(2,1)} %param.26, s32[]{:T(128)S(6)} %select_n.260, f32[2048,1024]{1,0:T(8,128)} %copy-done.38, f32[1024]{0:T(1024)S(1)} %dynamic_slice.88), kind=kOutput, calls=%fused_computation.53 | convolution fusion | flops 8610906112 | bytes 29364228 | tf_op jit(solution)/shard_map/dot_general | solution.py:618
  653.2 15.5 add_convert_fusion.5
  673.9 18.5 %add_convert_fusion.4 = bf16[1024,2048]{1,0:T(8,128)(2,1)} fusion(f32[1024,2048]{1,0:T(8,128)} %fusion.43, bf16[2048,2048]{1,0:T(8,128)(2,1)} %collective-permute-done.3, f32[2048,1024]{1,0:T(8,128)} %copy-done.38, f32[1024]{0:T(1024)S(1)} %dynamic_slice.88), kind=kOutput, calls=%fused_computation.8 | convolution fusion | flops 8615100416 | bytes 29364224 | tf_op jit(solution)/shard_map/dot_general | solution.py:17
  718.3 20.0 %all-to-all-done.7 = bf16[4,512,1024]{2,1,0:T(8,128)(2,1)} async-done(((bf16[4,512,1024]{2,1,0:T(8,128)(2,1)}), bf16[4,512,1024]{2,1,0:T(8,128)(2,1)}, u32[]{:S(2)}, u32[]{:S(2)}) %all-to-all-start.7) | async-done | bytes 4194336 | tf_op jit(solution)/shard_map/all_to_all | solution.py:597
  743.5 18.7 %fusion.6 = f32[2048,2048]{1,0:T(8,128)} fusion(bf16[2048,2048]{1,0:T(8,128)(2,1)} %param.26, s32[]{:T(128)S(6)} %select_n.260, f32[2048,1024]{1,0:T(8,128)} %copy-done.39, f32[1024]{0:T(1024)S(1)} %dynamic_slice.88), kind=kOutput, calls=%fused_computation.55 | convolution fusion | flops 8610906112 | bytes 29364228 | tf_op jit(solution)/shard_map/dot_general | solution.py:618
  796.5 147.2 %collective-permute-done.8 = bf16[2048,768]{0,1:T(8,128)(2,1)S(1)} collective-permute-done((bf16[2048,768]{0,1:T(8,128)(2,1)}, bf16[2048,768]{0,1:T(8,128)(2,1)S(1)}, u32[]{:S(2)}, u32[]{:S(2)}) %collective-permute-start.8) | collective-permute-done | bytes 3145760 | tf_op jit(solution)/shard_map/ppermute | solution.py:381
  1002.0 159.3 %collective-permute-done.14 = bf16[256,2048]{1,0:T(8,128)(2,1)} collective-permute-done((bf16[256,2048]{1,0:T(8,128)(2,1)S(1)}, bf16[256,2048]{1,0:T(8,128)(2,1)}, u32[]{:S(2)}, u32[]{:S(2)}) %collective-permute-start.14) | collective-permute-done | bytes 1048608 | tf_op jit(solution)/shard_map/ppermute | solution.py:385
  1185.1 88.5 %collective-permute-done.18 = bf16[2048,1024]{1,0:T(8,128)(2,1)} collective-permute-done((bf16[2048,1024]{1,0:T(8,128)(2,1)}, bf16[2048,1024]{1,0:T(8,128)(2,1)}, u32[]{:S(2)}, u32[]{:S(2)}) %collective-permute-start.18) | collective-permute-done | bytes 4194336 | tf_op jit(solution)/shard_map/ppermute | solution.py:385
  1308.1 13.1 copy.66
  1378.9 16.6 %copy.67 = f32[512,1,4,2,1024]{0,4,3,2,1:T(8,128)} copy(f32[512,1,4,2,1024]{4,0,2,1,3:T(8,128)} %convert_bitcast_fusion) | data formatting | bytes 33554432 | tf_op jit(solution)/shard_map/convert_element_type | solution.py:669
  1395.5 17.4 %copy.69 = f32[512,8192]{1,0:T(8,128)} copy(f32[512,8192]{0,1:T(8,128)} %bitcast.209) | data formatting | bytes 33554432
  1431.2 113.5 %all-reduce.4.cloned.1.call-done = f32[20480]{0:T(1024)} async-done(((f32[20480]{0:T(1024)}), f32[20480]{0:T(1024)}) %all-reduce.4.cloned.1.call-update) | async-done | bytes 81936 | tf_op jit(solution)/shard_map/psum | solution.py:652
  (305 shorter events, 455.5 us)
Async XLA Ops:
  7.2 168.3 %all-gather.6.cloned.1.call-start = ((), (), s32[]{:S(2)}) async-start(), calls=%async_computation.10 | async-start | bytes 10485760 | tf_op jit(solution)/shard_map/all_gather | solution.py:357
  89.6 175.4 %all-gather.8.cloned.1.call-start = ((), (), s32[]{:S(2)}) async-start(), calls=%async_computation.11 | async-start | bytes 10485760 | tf_op jit(solution)/shard_map/all_gather | solution.py:357
  175.5 202.7 %collective-permute-start.2 = (bf16[2048,2048]{1,0:T(8,128)(2,1)}, bf16[2048,2048]{1,0:T(8,128)(2,1)}, u32[]{:S(2)}, u32[]{:S(2)}) collective-permute-start(bf16[2048,2048]{1,0:T(8,128)(2,1)} %all-gather.6.cloned.1.call-done), channel_id=1, source_target_pairs={{0,16},{16,0},{1,17},{17,1},{2,18},{18,2},{3,19},{19,3},{4,20},{20... | collective-permute-start | bytes 25165832 | tf_op jit(solution)/shard_map/ppermute | solution.py:338
  265.0 123.4 %collective-permute-start.3 = (bf16[2048,2048]{1,0:T(8,128)(2,1)}, bf16[2048,2048]{1,0:T(8,128)(2,1)}, u32[]{:S(2)}, u32[]{:S(2)}) collective-permute-start(bf16[2048,2048]{1,0:T(8,128)(2,1)} %all-gather.8.cloned.1.call-done), channel_id=1, source_target_pairs={{0,16},{16,0},{1,17},{17,1},{2,18},{18,2},{3,19},{19,3},{4,20},{20... | collective-permute-start | bytes 25165832 | tf_op jit(solution)/shard_map/ppermute | solution.py:338
  277.6 73.7 %all-to-all-start.2 = ((bf16[4,512,768]{1,2,0:T(8,128)(2,1)}), bf16[4,512,768]{1,2,0:T(8,128)(2,1)}, u32[]{:S(2)}, u32[]{:S(2)}) async-start(bf16[4,512,768]{1,2,0:T(8,128)(2,1)} %bitcast.225), calls=%async_computation.2 | async-start | bytes 6291456 | tf_op jit(solution)/shard_map/all_to_all | solution.py:377
  351.3 127.0 %all-to-all-start.1 = ((bf16[4,512,1024]{2,1,0:T(8,128)(2,1)}), bf16[4,512,1024]{2,1,0:T(8,128)(2,1)}, u32[]{:S(2)}, u32[]{:S(2)}) async-start(bf16[4,512,1024]{2,1,0:T(8,128)(2,1)} %bitcast.220), calls=%async_computation.1 | async-start | bytes 8388608 | tf_op jit(solution)/shard_map/all_to_all | solution.py:377
  356.2 824.2 %reduce-scatter.5.cloned.1.call-start = ((), (), s32[]{:S(2)}) async-start(), calls=%async_computation.13 | async-start | bytes 10485760 | tf_op jit(solution)/shard_map/reduce_scatter | solution.py:364
  652.9 114.7 %collective-permute-start.4 = (bf16[2048,2048]{1,0:T(8,128)(2,1)}, bf16[2048,2048]{1,0:T(8,128)(2,1)}, u32[]{:S(2)}, u32[]{:S(2)}) collective-permute-start(bf16[2048,2048]{1,0:T(8,128)(2,1)} %add_convert_fusion.3), channel_id=1, source_target_pairs={{0,16},{16,0},{1,17},{17,1},{2,18},{18,2},{3,19},{19,3},{4,20},{20... | collective-permute-start | bytes 25165832 | tf_op jit(solution)/shard_map/ppermute | solution.py:338
  668.7 69.6 %all-to-all-start.7 = ((bf16[4,512,1024]{2,1,0:T(8,128)(2,1)}), bf16[4,512,1024]{2,1,0:T(8,128)(2,1)}, u32[]{:S(2)}, u32[]{:S(2)}) async-start(bf16[4,512,1024]{2,1,0:T(8,128)(2,1)} %bitcast.234), calls=%async_computation.9 | async-start | bytes 8388608 | tf_op jit(solution)/shard_map/all_to_all | solution.py:597
  692.4 96.1 %collective-permute-start.20 = (bf16[1024,2048]{1,0:T(8,128)(2,1)}, bf16[1024,2048]{1,0:T(8,128)(2,1)}, u32[]{:S(2)}, u32[]{:S(2)}) collective-permute-start(bf16[1024,2048]{1,0:T(8,128)(2,1)} %add_convert_fusion.4), channel_id=1, source_target_pairs={{0,4},{12,8},{1,5},{13,9},{2,6},{14,10},{3,7},{15,11},{16,20},{28,... | collective-permute-start | bytes 12582920 | tf_op jit(solution)/shard_map/ppermute | solution.py:381
  743.5 601.7 %reduce-scatter.3.cloned.1.call-start = ((), (), s32[]{:S(2)}) async-start(), calls=%async_computation.12 | async-start | bytes 10485760 | tf_op jit(solution)/shard_map/reduce_scatter | solution.py:364
  762.3 185.5 %collective-permute-start.16 = (bf16[2048,1024]{1,0:T(8,128)(2,1)}, bf16[2048,1024]{1,0:T(8,128)(2,1)}, u32[]{:S(2)}, u32[]{:S(2)}) collective-permute-start(bf16[2048,1024]{1,0:T(8,128)(2,1)} %bitcast.70), channel_id=1, source_target_pairs={{0,4},{12,8},{1,5},{13,9},{2,6},{14,10},{3,7},{15,11},{16,20},{28,... | collective-permute-start | bytes 12582920 | tf_op jit(solution)/shard_map/ppermute | solution.py:381
  785.3 158.4 %collective-permute-start.8 = (bf16[2048,768]{0,1:T(8,128)(2,1)}, bf16[2048,768]{0,1:T(8,128)(2,1)S(1)}, u32[]{:S(2)}, u32[]{:S(2)}) collective-permute-start(bf16[2048,768]{0,1:T(8,128)(2,1)} %copy.71), channel_id=1, source_target_pairs={{0,4},{12,8},{1,5},{13,9},{2,6},{14,10},{3,7},{15,11},{16,20},{28,... | collective-permute-start | bytes 9437192 | tf_op jit(solution)/shard_map/ppermute | solution.py:381
  793.9 175.5 %collective-permute-start.21 = (bf16[1024,2048]{1,0:T(8,128)(2,1)S(1)}, bf16[1024,2048]{1,0:T(8,128)(2,1)}, u32[]{:S(2)}, u32[]{:S(2)}) collective-permute-start(bf16[1024,2048]{1,0:T(8,128)(2,1)S(1)} %add.392), channel_id=1, source_target_pairs={{4,8},{8,4},{5,9},{9,5},{6,10},{10,6},{7,11},{11,7},{20,24},{24,20... | collective-permute-start | bytes 12582920 | tf_op jit(solution)/shard_map/ppermute | solution.py:383
  975.5 191.5 %collective-permute-start.22 = (bf16[1024,2048]{1,0:T(8,128)(2,1)}, bf16[1024,2048]{1,0:T(8,128)(2,1)}, u32[]{:S(2)}, u32[]{:S(2)}) collective-permute-start(bf16[1024,2048]{1,0:T(8,128)(2,1)} %add.393), channel_id=1, source_target_pairs={{4,0},{8,12},{5,1},{9,13},{6,2},{10,14},{7,3},{11,15},{20,16},{24,... | collective-permute-start | bytes 12582920 | tf_op jit(solution)/shard_map/ppermute | solution.py:385
  981.8 180.9 %collective-permute-start.10 = (bf16[2048,768]{0,1:T(8,128)(2,1)}, bf16[2048,768]{0,1:T(8,128)(2,1)}, u32[]{:S(2)}, u32[]{:S(2)}) collective-permute-start(bf16[2048,768]{0,1:T(8,128)(2,1)} %add.382), channel_id=1, source_target_pairs={{4,0},{8,12},{5,1},{9,13},{6,2},{10,14},{7,3},{11,15},{20,16},{24,... | collective-permute-start | bytes 9437192 | tf_op jit(solution)/shard_map/ppermute | solution.py:385
  992.3 169.0 %collective-permute-start.14 = (bf16[256,2048]{1,0:T(8,128)(2,1)S(1)}, bf16[256,2048]{1,0:T(8,128)(2,1)}, u32[]{:S(2)}, u32[]{:S(2)}) collective-permute-start(bf16[256,2048]{1,0:T(8,128)(2,1)S(1)} %add.386), channel_id=1, source_target_pairs={{4,0},{8,12},{5,1},{9,13},{6,2},{10,14},{7,3},{11,15},{20,16},{24,... | collective-permute-start | bytes 3145736 | tf_op jit(solution)/shard_map/ppermute | solution.py:385
  1000.2 273.4 %collective-permute-start.18 = (bf16[2048,1024]{1,0:T(8,128)(2,1)}, bf16[2048,1024]{1,0:T(8,128)(2,1)}, u32[]{:S(2)}, u32[]{:S(2)}) collective-permute-start(bf16[2048,1024]{1,0:T(8,128)(2,1)} %add.389), channel_id=1, source_target_pairs={{4,0},{8,12},{5,1},{9,13},{6,2},{10,14},{7,3},{11,15},{20,16},{24,... | collective-permute-start | bytes 12582920 | tf_op jit(solution)/shard_map/ppermute | solution.py:385
  1166.6 111.6 %collective-permute-start.11 = (bf16[2048,768]{0,1:T(8,128)(2,1)}, bf16[2048,768]{0,1:T(8,128)(2,1)}, u32[]{:S(2)}, u32[]{:S(2)}) collective-permute-start(bf16[2048,768]{0,1:T(8,128)(2,1)} %broadcast_select_fusion.4), channel_id=1, source_target_pairs={{0,16},{16,0},{1,17},{17,1},{2,18},{18,2},{3,19},{19,3},{4,20},{20... | collective-permute-start | bytes 9437192 | tf_op jit(solution)/shard_map/ppermute | solution.py:338
  1171.7 162.2 %collective-permute-start.23 = (bf16[1024,2048]{1,0:T(8,128)(2,1)}, bf16[1024,2048]{1,0:T(8,128)(2,1)}, u32[]{:S(2)}, u32[]{:S(2)}) collective-permute-start(bf16[1024,2048]{1,0:T(8,128)(2,1)} %broadcast_select_fusion), channel_id=1, source_target_pairs={{0,16},{16,0},{1,17},{17,1},{2,18},{18,2},{3,19},{19,3},{4,20},{20... | collective-permute-start | bytes 12582920 | tf_op jit(solution)/shard_map/ppermute | solution.py:338
  1180.4 164.8 %all-to-all-start.5 = ((bf16[4,128,2048]{2,1,0:T(8,128)(2,1)}), bf16[4,128,2048]{2,1,0:T(8,128)(2,1)}, u32[]{:S(2)}, u32[]{:S(2)}) async-start(bf16[4,128,2048]{2,1,0:T(8,128)(2,1)} %bitcast.240), calls=%async_computation.7 | async-start | bytes 4194304 | tf_op jit(solution)/shard_map/all_to_all | solution.py:365
  1278.2 86.2 %collective-permute-start.19 = (bf16[2048,1024]{1,0:T(8,128)(2,1)}, bf16[2048,1024]{1,0:T(8,128)(2,1)}, u32[]{:S(2)}, u32[]{:S(2)}) collective-permute-start(bf16[2048,1024]{1,0:T(8,128)(2,1)} %broadcast_select_fusion.1), channel_id=1, source_target_pairs={{0,16},{16,0},{1,17},{17,1},{2,18},{18,2},{3,19},{19,3},{4,20},{20... | collective-permute-start | bytes 12582920 | tf_op jit(solution)/shard_map/ppermute | solution.py:338
  1345.2 67.7 %all-to-all-start.4 = ((bf16[4,128,2048]{2,1,0:T(8,128)(2,1)}), bf16[4,128,2048]{2,1,0:T(8,128)(2,1)}, u32[]{:S(2)}, u32[]{:S(2)}) async-start(bf16[4,128,2048]{2,1,0:T(8,128)(2,1)} %bitcast.241), calls=%async_computation.5 | async-start | bytes 4194304 | tf_op jit(solution)/shard_map/all_to_all | solution.py:365
  1349.7 195.0 %all-reduce.4.cloned.1.call-start = ((), (), s32[]{:S(2)}) async-start(), calls=%async_computation.14 | async-start | bytes 163840 | tf_op jit(solution)/shard_map/psum | solution.py:652
  (57 other events, 1355.4 us)
Sparse Core Ops, SparseCore 0:
  89.7 85.7 all-gather.5
  177.3 87.5 all-gather.7
  607.3 126.3 reduce-scatter.4
  780.8 86.8 reduce-scatter.2
  1423.7 120.9 all-reduce.3

commit v2 on v1

--- a/solution.py
+++ b/solution.py
@@ -332,10 +332,35 @@
 
 
 SWAP = [(0, 1), (1, 0)]
+LOW = jnp.bfloat16
+SLOW = 1.8
+WIDE = jnp.float32
+
+
+def hint(flops, transcendentals, bytes_accessed):
+    return pl.CostEstimate(
+        flops=int(flops * SLOW), transcendentals=transcendentals, bytes_accessed=bytes_accessed
+    )
+
+
+def after(value, *others):
+    return lax.optimization_barrier((value,) + others)[0]
 
 
 def swap_dp(value):
     return lax.ppermute(value, "dp", SWAP)
+
+
+def swap_shard(value, bits):
+    return lax.ppermute(value, "fsdp", [(i, i ^ bits) for i in range(4)])
+
+
+def shift_ctx(value, steps):
+    return lax.ppermute(value, "ctx", [(i, (i + steps) % 4) for i in range(4)])
+
+
+def pick(array, index, axis):
+    return lax.dynamic_index_in_dim(array, index, axis, keepdims=False)
 
 
 def by_core(core, mine, other, axis):
@@ -344,53 +369,177 @@
     return jnp.stack([first, second], axis=axis)
 
 
-def pick(array, index, axis):
-    return lax.dynamic_index_in_dim(array, index, axis, keepdims=False)
-
-
-def to_plane(rows, core, blk):
-    micro, count, width = rows.shape
+def for_other(rows, core, blk):
+    micro, _, width = rows.shape
+    return swap_dp(pick(rows.reshape(micro, 2, blk, width), 1 - core, 1))
+
+
+def slots_of(rows, received, core, place, blk):
+    micro, _, width = rows.shape
     split = rows.reshape(micro, 2, blk, width)
-    received = swap_dp(pick(split, 1 - core, 1))
-    lined = by_core(core, pick(split, core, 1), received, 0).reshape(2 * micro, blk, width)
-    dealt = lax.all_to_all(lined, "ctx", 0, 0, tiled=True)
-    own = lax.all_gather(dealt.reshape(-1, width), "fsdp", axis=0, tiled=True)
-    return own, swap_dp(own)
-
-
-def to_home(part_own, part_oth, core, micro, blk):
-    width = part_own.shape[1]
-    total = (part_own + swap_dp(part_oth).astype(jnp.float32)).astype(jnp.bfloat16)
-    mine = lax.psum_scatter(total, "fsdp", scatter_dimension=0, tiled=True)
-    lined = lax.all_to_all(mine.reshape(-1, blk, width), "ctx", 0, 0, tiled=True)
-    lined = lined.reshape(2, micro, blk, width)
+    lined = by_core(core, pick(split, core, 1), received, 0).reshape(4, blk, width)
+    first = pick(lined, place, 0)
+    rest = [shift_ctx(pick(lined, (place + steps) % 4, 0), steps) for steps in (1, 2, 3)]
+    return first, rest
+
+
+def spread_first(rows):
+    return [(bits, 0, swap_shard(rows, bits)) for bits in (1, 2, 3)] + [(0, 0, rows)]
+
+
+def spread_rest(rows, start):
+    half = rows.shape[0] // 2
+    top, end = rows[:half], rows[half:]
+    x_top, y_end = swap_shard(top, 1), swap_shard(end, 2)
+    x_end, y_top = swap_shard(end, 1), swap_shard(top, 2)
+    d_top, d_end = swap_shard(x_top, 2), swap_shard(y_end, 1)
+    pairs = ((0, top, end), (1, x_top, x_end), (2, y_top, y_end), (3, d_top, d_end))
+    return [(bits, start, one) for bits, one, _ in pairs] + [(bits, start + half, two) for bits, _, two in pairs]
+
+
+def placed(pieces, shard, size, *gates):
+    whole = after(jnp.zeros((4 * size, pieces[0][2].shape[1]), LOW), *gates)
+    for bits, start, piece in pieces:
+        whole = lax.dynamic_update_slice(whole, piece, ((shard ^ bits) * size + start, 0))
+    return whole
+
+
+def plus(first, *others):
+    total = first.astype(WIDE)
+    for other in others:
+        total = total + other.astype(WIDE)
+    return total.astype(LOW)
+
+
+def collect(total, shard):
+    size = total.shape[0] // 4
+    half = size // 2
+
+    def part(bits, which):
+        return lax.dynamic_slice_in_dim(total, (shard ^ bits) * size + which * half, half, 0)
+
+    via_x, via_y = swap_shard(part(3, 0), 1), swap_shard(part(3, 1), 2)
+    x_top, y_end = swap_shard(part(1, 0), 1), swap_shard(part(2, 1), 2)
+    y_top = swap_shard(plus(part(2, 0), via_x), 2)
+    x_end = swap_shard(plus(part(1, 1), via_y), 1)
+    return jnp.concatenate([plus(part(0, 0), x_top, y_top), plus(part(0, 1), x_end, y_end)]), (via_x, via_y)
+
+
+def to_home(mine, core, place, blk):
+    width = mine.shape[1]
+    lined = jnp.concatenate([lax.dynamic_slice_in_dim(mine, (place - j) % 4 * blk, blk, 0) for j in range(4)])
+    lined = lax.all_to_all(lined.reshape(4, blk, width), "ctx", 0, 0, tiled=True).reshape(2, 2, blk, width)
     kept = pick(lined, core, 0)
     received = swap_dp(pick(lined, 1 - core, 0))
-    return by_core(core, kept, received, 1).reshape(micro, 2 * blk, width)
-
-
-def columns_of(weight, parts, core, shards):
-    rows, total = weight.shape
-    width = total // (parts * shards * 2)
-    mine = pick(weight.reshape(rows, parts, shards, 2, width), core, 3)
-    sent = mine.transpose(2, 0, 1, 3).reshape(shards * rows, parts * width)
-    return lax.all_to_all(sent, "fsdp", 0, 0, tiled=True)
+    return by_core(core, kept, received, 1).reshape(2, 2 * blk, width)
+
+
+def columns_cut(weight, parts, core, shard):
+    width = weight.shape[1] // (parts * 8)
+    pieces = []
+    for bits in range(4):
+        spot = 2 * (shard ^ bits) + core
+        pieces.append(jnp.concatenate(
+            [lax.dynamic_slice_in_dim(weight, (t * 8 + spot) * width, width, 1) for t in range(parts)], axis=1
+        ))
+    return pieces
+
+
+def columns_sent(pieces):
+    return [(bits, 0, piece if bits == 0 else swap_shard(piece, bits)) for bits, piece in enumerate(pieces)]
+
+
+def inward(value):
+    return lax.ppermute(value, "ctx", [(0, 1), (3, 2)])
+
+
+def across(value):
+    return lax.ppermute(value, "ctx", [(1, 2), (2, 1)])
+
+
+def outward(value):
+    return lax.ppermute(value, "ctx", [(1, 0), (2, 3)])
 
 
 def line_sum(value, place):
-    inward = lax.ppermute(value, "ctx", [(0, 1), (3, 2)])
-    half = value + inward
-    across = lax.ppermute(half, "ctx", [(1, 2), (2, 1)])
-    whole = half + across
-    outward = lax.ppermute(whole, "ctx", [(1, 0), (2, 3)])
-    inner = (place == 1) | (place == 2)
-    return jnp.where(inner, whole, outward)
-
-
-def sum_ctx(value, place):
-    if lax.axis_size("ctx") == 4:
-        return line_sum(value, place)
-    return lax.psum(value, "ctx")
+    half = value + inward(value)
+    whole = half + across(half)
+    return line_end(whole, outward(whole), place)
+
+
+def line_end(whole, received, place):
+    return jnp.where((place == 1) | (place == 2), whole, received)
+
+
+def every_sum(value, place):
+    value = value + swap_dp(value)
+    value = value + swap_shard(value, 1)
+    value = value + swap_shard(value, 2)
+    return line_sum(value, place)
+
+
+def lay_out(core, shard, own, oth, out_shape, grid, block, in_at, out_at):
+    def kernel(where, own_ref, oth_ref, out_ref):
+        side = pl.program_id(len(grid))
+
+        @pl.when(side == 0)
+        def _():
+            out_ref[...] = own_ref[...].astype(WIDE)
+
+        @pl.when(side == 1)
+        def _():
+            out_ref[...] = oth_ref[...].astype(WIDE)
+
+    source = pl.BlockSpec(block, lambda *args: in_at(*args[: len(grid)]))
+    target = pl.BlockSpec(block, lambda *args: out_at(*args[:-1], args[-1][0], args[-1][1]))
+    count = out_shape[0] * out_shape[1]
+    return pl.pallas_call(
+        kernel,
+        grid_spec=pltpu.PrefetchScalarGridSpec(
+            num_scalar_prefetch=1, grid=grid + (2,), in_specs=[source, source], out_specs=target
+        ),
+        out_shape=jax.ShapeDtypeStruct(out_shape, WIDE),
+        compiler_params=pltpu.CompilerParams(dimension_semantics=("arbitrary",) * (len(grid) + 1)),
+        cost_estimate=hint(flops=0, transcendentals=0, bytes_accessed=6 * count),
+    )(jnp.stack([core, shard]).astype(jnp.int32), own, oth)
+
+
+def rows_out(core, shard, own, oth):
+    rows, width = own.shape
+    tile = min(256, rows)
+    steps = rows // tile
+    return lay_out(
+        core, shard, own, oth, (2 * rows, width), (steps,), (tile, width),
+        lambda i: (i, 0), lambda i, s, c, f: ((c ^ s) * steps + i, 0),
+    )
+
+
+def cols_out(core, shard, own, oth, parts):
+    lines, columns, rows, width = own.shape
+    width = width // parts
+
+    def kernel(where, own_ref, oth_ref, out_ref):
+        side = pl.program_id(2)
+
+        @pl.when(side == 0)
+        def _():
+            out_ref[...] = own_ref[...].reshape(lines * rows, width).astype(WIDE)
+
+        @pl.when(side == 1)
+        def _():
+            out_ref[...] = oth_ref[...].reshape(lines * rows, width).astype(WIDE)
+
+    source = pl.BlockSpec((lines, 1, rows, width), lambda b, t, s, where: (0, b, 0, t))
+    target = pl.BlockSpec((lines * rows, width), lambda b, t, s, where: (0, t * 8 + 2 * b + (where[0] ^ s)))
+    return pl.pallas_call(
+        kernel,
+        grid_spec=pltpu.PrefetchScalarGridSpec(
+            num_scalar_prefetch=1, grid=(columns, parts, 2), in_specs=[source, source], out_specs=target
+        ),
+        out_shape=jax.ShapeDtypeStruct((lines * rows, 2 * columns * parts * width), WIDE),
+        compiler_params=pltpu.CompilerParams(dimension_semantics=("arbitrary",) * 3),
+        cost_estimate=pl.CostEstimate(flops=0, transcendentals=0, bytes_accessed=12 * own.size),
+    )(jnp.stack([core, shard]).astype(jnp.int32), own, oth)
 
 
 GELU_C = 0.7978845608028654
@@ -403,6 +552,186 @@
     half = 0.5 * (1.0 + tanh)
     slope = half + 0.5 * value * (1.0 - tanh * tanh) * (GELU_C * (1.0 + 3.0 * GELU_A * square))
     return value * half, slope
+
+
+ROWS_OF = (((0,), (0,)), ((), ()))
+COLS_OF = (((1,), (1,)), ((), ()))
+ROOM = 56 * 1024 * 1024
+
+
+def row_call(body, tiled, whole, widths, flops, tile=512):
+    count = tiled[0].shape[0]
+
+    def rows_spec(width):
+        return pl.BlockSpec((tile, width), lambda i: (i, 0))
+
+    moved = sum(a.size * a.dtype.itemsize for a in (*tiled, *whole)) + 2 * count * sum(widths)
+    return pl.pallas_call(
+        body,
+        grid=(count // tile,),
+        in_specs=[rows_spec(a.shape[1]) for a in tiled]
+        + [pl.BlockSpec(a.shape, lambda i: (0, 0), pipeline_mode=pl.Buffered(1)) for a in whole],
+        out_specs=[rows_spec(width) for width in widths],
+        out_shape=[jax.ShapeDtypeStruct((count, width), LOW) for width in widths],
+        compiler_params=pltpu.CompilerParams(dimension_semantics=("arbitrary",), vmem_limit_bytes=ROOM),
+        cost_estimate=hint(flops=flops, transcendentals=0, bytes_accessed=moved),
+    )(*tiled, *whole)
+
+
+def strips(width):
+    step = min(256, width)
+    return [slice(at, at + step) for at in range(0, width, step)]
+
+
+def up_call(rows, weight, bias):
+    def body(rows_ref, weight_ref, bias_ref, act_ref, slope_ref):
+        for at in strips(weight.shape[1]):
+            total = jnp.dot(rows_ref[...], weight_ref[:, at], preferred_element_type=WIDE) + bias_ref[:, at]
+            act, slope = gelu_pair(total)
+            act_ref[:, at] = act.astype(LOW)
+            slope_ref[:, at] = slope.astype(LOW)
+
+    width = weight.shape[1]
+    return row_call(body, [rows], [weight, bias[None]], [width, width], 2 * rows.shape[0] * weight.size)
+
+
+def join_call(rows, weight, bias):
+    def body(rows_ref, weight_ref, bias_ref, out_ref):
+        for at in strips(weight.shape[1]):
+            total = jnp.dot(rows_ref[...], weight_ref[:, at], preferred_element_type=WIDE)
+            out_ref[:, at] = (total + bias_ref[:, at]).astype(LOW)
+
+    return row_call(body, [rows], [weight, bias[None]], [weight.shape[1]], 2 * rows.shape[0] * weight.size)[0]
+
+
+def down_back_call(rows, slopes, down_w, out_w):
+    def body(rows_ref, slope_ref, down_ref, out_w_ref, dup_ref, datt_ref):
+        for at in strips(down_w.shape[0]):
+            total = lax.dot_general(rows_ref[...], down_ref[at, :], COLS_OF, preferred_element_type=WIDE)
+            dup_ref[:, at] = (total * slope_ref[:, at].astype(WIDE)).astype(LOW)
+        total = lax.dot_general(rows_ref[...], out_w_ref[...], COLS_OF, preferred_element_type=WIDE)
+        datt_ref[...] = total.astype(LOW)
+
+    flops = 2 * rows.shape[0] * (down_w.size + out_w.size)
+    return row_call(body, [rows, slopes], [down_w, out_w], [down_w.shape[0], out_w.shape[0]], flops)
+
+
+def forward_call(act, att, down_w, out_w, added=None):
+    def body(*refs):
+        act_ref, att_ref = refs[:2]
+        down_ref, out_w_ref, out_ref = refs[-3:]
+        for at in strips(down_w.shape[1]):
+            total = jnp.dot(act_ref[...], down_ref[:, at], preferred_element_type=WIDE)
+            total = total + jnp.dot(att_ref[...], out_w_ref[:, at], preferred_element_type=WIDE)
+            if added is not None:
+                total = total + refs[2][:, at].astype(WIDE)
+            out_ref[:, at] = total.astype(LOW)
+
+    tiled = [act, att] + ([] if added is None else [added])
+    flops = 2 * act.shape[0] * (down_w.size + out_w.size)
+    return row_call(body, tiled, [down_w, out_w], [down_w.shape[1]], flops)[0]
+
+
+def backward_call(dup, turned, up_w, qkv_w, added=None):
+    wide = turned[0].shape[1]
+
+    def body(*refs):
+        dup_ref, turned_refs = refs[0], refs[1:4]
+        up_ref, qkv_ref, out_ref = refs[-3:]
+        for at in strips(up_w.shape[0]):
+            total = lax.dot_general(dup_ref[...], up_ref[at, :], COLS_OF, preferred_element_type=WIDE)
+            for i, ref in enumerate(turned_refs):
+                part = qkv_ref[at, i * wide : (i + 1) * wide]
+                total = total + lax.dot_general(ref[...], part, COLS_OF, preferred_element_type=WIDE)
+            if added is not None:
+                total = total + refs[4][:, at].astype(WIDE)
+            out_ref[:, at] = total.astype(LOW)
+
+    tiled = [dup, *turned] + ([] if added is None else [added])
+    flops = 2 * dup.shape[0] * (up_w.size + qkv_w.size)
+    return row_call(body, tiled, [up_w, qkv_w], [up_w.shape[0]], flops)[0]
+
+
+def grad_call(left, rights, left_part=(0, 1), right_part=(0, 1), sums=False, dealt=False, tile=512):
+    steps = left[0].shape[0] // tile
+    left_cols = left[0].shape[1] // left_part[1]
+    right_cols = [pair[0].shape[1] // right_part[1] for pair in rights]
+    count = len(rights)
+    piece = left_cols // 16
+    made = 1 if dealt else count
+
+    def body(*refs):
+        ins, outs = refs[: 2 + 2 * count], refs[2 + 2 * count :]
+        grads, totals, accs = outs[:made], outs[made : len(outs) - count], outs[len(outs) - count :]
+        step = pl.program_id(0)
+
+        @pl.when(step == 0)
+        def _():
+            for ref in (*accs, *totals):
+                ref[...] = jnp.zeros_like(ref)
+
+        def add(left_ref, right_refs):
+            for i, ref in enumerate(right_refs):
+                for at in strips(right_cols[i]):
+                    accs[i][:, at] += lax.dot_general(
+                        left_ref[...], ref[:, at], ROWS_OF, preferred_element_type=WIDE
+                    )
+                if sums:
+                    totals[i][...] += jnp.sum(ref[...].astype(WIDE), axis=0, keepdims=True)
+
+        @pl.when(step < steps)
+        def _():
+            add(ins[0], ins[2 : 2 + count])
+
+        @pl.when(step >= steps)
+        def _():
+            add(ins[1], ins[2 + count :])
+
+        @pl.when(step == 2 * steps - 1)
+        def _():
+            if not dealt:
+                for grad, acc in zip(grads, accs):
+                    grad[...] = acc[...].astype(LOW)
+                return
+            start = 0
+            for acc, cols in zip(accs, right_cols):
+                for column in range(4):
+                    for line in range(4):
+                        at = (4 * column + line) * piece
+                        grads[0][line, column, :, start : start + cols] = acc[at : at + piece, :].astype(LOW)
+                start += cols
+
+    def side_spec(cols, part, side):
+        def at(step):
+            row = jnp.minimum(step, steps - 1) if side == 0 else jnp.maximum(step - steps, 0)
+            return (row, part)
+
+        return pl.BlockSpec((tile, cols), at)
+
+    def fixed(shape):
+        return pl.BlockSpec(shape, lambda step: (0,) * len(shape))
+
+    specs = [side_spec(left_cols, left_part[0], side) for side in (0, 1)]
+    specs += [side_spec(cols, right_part[0], side) for side in (0, 1) for cols in right_cols]
+    shapes = [jax.ShapeDtypeStruct((left_cols, cols), LOW) for cols in right_cols]
+    if dealt:
+        shapes = [jax.ShapeDtypeStruct((4, 4, piece, sum(right_cols)), LOW)]
+    if sums:
+        shapes += [jax.ShapeDtypeStruct((1, cols), WIDE) for cols in right_cols]
+    rows = 2 * left[0].shape[0]
+    return pl.pallas_call(
+        body,
+        grid=(2 * steps,),
+        in_specs=specs,
+        out_specs=[fixed(shape.shape) for shape in shapes],
+        out_shape=shapes,
+        scratch_shapes=[pltpu.VMEM((left_cols, cols), WIDE) for cols in right_cols],
+        compiler_params=pltpu.CompilerParams(dimension_semantics=("arbitrary",), vmem_limit_bytes=ROOM),
+        cost_estimate=hint(
+            flops=2 * rows * left_cols * sum(right_cols), transcendentals=0,
+            bytes_accessed=2 * rows * (left_cols + sum(right_cols)),
+        ),
+    )(*left, *[pair[0] for pair in rights], *[pair[1] for pair in rights])
 
 
 def rope_tables(seq_len):
@@ -419,23 +748,21 @@
     return cosine, up, down
 
 
-def attention_call(deal_own, deal_oth, lengths, joined_own, joined_oth, datt_own, datt_oth, blk):
-    seqs, half_rows, wide = joined_own.shape
+def attention_call(deal_own, deal_oth, lengths, joined_own, joined_oth, datt_own, datt_oth, tables, blk, base, seqs, earlier=()):
+    _, half_rows, wide = joined_own.shape
     heads_wide = wide // 3
     pairs = heads_wide // 128
     seq_len = 2 * half_rows
     per_side = half_rows // blk
     step = 256
-    tables = rope_tables(seq_len)
     scale = HEAD_DIM ** (-0.5)
     half = ROT // 2
     contract_last = (((1,), (1,)), ((), ()))
     contract_first = (((0,), (0,)), ((), ()))
 
-    def kernel(own_at, oth_at, len_at, cos_ref, up_ref, down_ref, q0, k0, v0, d0, q1, k1, v1, d1,
-               att0, dq0, dk0, dv0, att1, dq1, dk1, dv1,
-               qs, ks, vs, ds, att_s, dq_s, dk_s, dv_s):
-        seq = pl.program_id(0)
+    def kernel(own_at, oth_at, len_at, cos_ref, up_ref, down_ref, q0, k0, v0, d0, q1, k1, v1, d1, *rest):
+        att0, dq0, dk0, dv0, att1, dq1, dk1, dv1, qs, ks, vs, ds, att_s, dq_s, dk_s, dv_s = rest[len(earlier) :]
+        seq = base + pl.program_id(0)
         length = len_at[seq]
 
         def turn(x, at):
@@ -500,132 +827,168 @@
                 dv_ref[0, here, :] = dv_s[at, :].astype(jnp.bfloat16)
 
     def lanes(offset):
-        return pl.BlockSpec((1, half_rows, 128), lambda s, p, *_: (s, 0, offset + p))
+        return pl.BlockSpec((1, half_rows, 128), lambda s, p, *_: (base + s, 0, offset + p))
 
     table = pl.BlockSpec((seq_len, 128), lambda s, p, *_: (0, 0))
     side_in = [lanes(0), lanes(pairs), lanes(2 * pairs), lanes(0)]
     side_out = [lanes(0)] * 4
-    narrow = jax.ShapeDtypeStruct((seqs, half_rows, heads_wide), jnp.bfloat16)
+    narrow = jax.ShapeDtypeStruct((4, half_rows, heads_wide), jnp.bfloat16)
     work = seqs * pairs * 2 * seq_len * seq_len * 64
     result = pl.pallas_call(
         kernel,
         grid_spec=pltpu.PrefetchScalarGridSpec(
             num_scalar_prefetch=3,
             grid=(seqs, pairs),
-            in_specs=[table] * 3 + side_in + side_in,
+            in_specs=[table] * 3 + side_in + side_in + [pl.BlockSpec(memory_space=pl.ANY)] * len(earlier),
             out_specs=side_out + side_out,
             scratch_shapes=[pltpu.VMEM((seq_len, 128), jnp.bfloat16)] * 4
             + [pltpu.VMEM((seq_len, 128), jnp.float32)] * 4,
         ),
         out_shape=[narrow] * 8,
+        input_output_aliases={14 + i: i for i in range(len(earlier))},
         compiler_params=pltpu.CompilerParams(
             dimension_semantics=("arbitrary", "arbitrary"), vmem_limit_bytes=56 * 1024 * 1024
         ),
-        cost_estimate=pl.CostEstimate(
-            flops=12 * work, transcendentals=work // 64, bytes_accessed=2 * 8 * seqs * seq_len * heads_wide
+        cost_estimate=hint(
+            flops=36 * work, transcendentals=work // 64, bytes_accessed=2 * 8 * seqs * seq_len * heads_wide
         ),
     )(deal_own, deal_oth, lengths, *tables, joined_own, joined_own, joined_own, datt_own,
-      joined_oth, joined_oth, joined_oth, datt_oth)
-    return result[:4], result[4:]
+      joined_oth, joined_oth, joined_oth, datt_oth, *earlier)
+    return result
 
 
 def plane_body(
     tokens, cotangent, lengths, deal, ln_gain, ln_bias, w_qkv, b_qkv, w_out, b_out, w_up, b_up, w_down, b_down
 ):
-    shards = lax.axis_size("fsdp")
     core = lax.axis_index("dp")
     place = lax.axis_index("ctx")
     shard = lax.axis_index("fsdp")
+    spot = 2 * shard + core
     _, micro, rows, width = tokens.shape
     blocks = deal.shape[2]
-    lined = lax.axis_size("ctx")
-    blk = rows * lined // blocks
-    hidden_units = w_down.shape[0] // 2
+    blk = rows * 4 // blocks
+    units = w_down.shape[0] // 2
     head_cols = w_out.shape[0] // 2
-    low = jnp.bfloat16
-    wide = jnp.float32
-
-    small = jnp.concatenate([ln_gain, ln_bias, b_qkv, b_out, b_up, b_down])
-    small = lax.all_gather(small, "fsdp", axis=0, tiled=False).astype(wide)
+
+    meta = jnp.concatenate([deal[0].reshape(-1), lengths[0] // 64, lengths[0] % 64]).astype(LOW)
+    theirs = swap_dp(meta)
+    meta = jnp.where(place // micro == core, meta, theirs)
+    turn = place % micro
+    meta = jnp.concatenate([
+        lax.dynamic_slice_in_dim(meta, turn * blocks, blocks), lax.dynamic_slice_in_dim(meta, micro * blocks + turn, 1),
+        lax.dynamic_slice_in_dim(meta, micro * (blocks + 1) + turn, 1),
+    ])
+    size = 2 * ln_gain.shape[0] + b_qkv.shape[0] + b_out.shape[0] + b_up.shape[0] + b_down.shape[0] + meta.shape[0]
+    small = jnp.concatenate([ln_gain, ln_bias, b_qkv, b_out, b_up, b_down, meta, jnp.zeros((-size % 512,), LOW)])
+
+    small = lax.all_gather(small, "fsdp", axis=0, tiled=False)
     bounds = [0]
-    for piece in (ln_gain, ln_bias, b_qkv, b_out, b_up, b_down):
+    for piece in (ln_gain, ln_bias, b_qkv, b_out, b_up, b_down, meta):
         bounds.append(bounds[-1] + piece.shape[0])
-    gain, shift, bias_qkv, bias_out, bias_up, bias_down = (
-        small[:, a:b].reshape(-1) for a, b in zip(bounds[:-1], bounds[1:])
-    )
-    meta = jnp.concatenate([deal[0].reshape(-1), lengths[0]])
-    meta = lax.all_gather(meta, ("dp", "fsdp"), axis=0, tiled=False).reshape(2, shards, -1)
-    meta = pick(meta, place // micro, 0)
-    plane_deal = pick(meta[:, : micro * blocks].reshape(shards, micro, blocks), place % micro, 1)
-    plane_len = pick(meta[:, micro * blocks :], place % micro, 1)
-    plane_deal = plane_deal.reshape(shards, lined, 2)
-    deal_own = pick(plane_deal, core, 2)
-    deal_oth = pick(plane_deal, 1 - core, 2)
-
+    gain, shift, bias_qkv, bias_out, bias_up, bias_down, meta = (small[:, a:b] for a, b in zip(bounds[:-1], bounds[1:]))
+    gain, shift = gain.astype(WIDE).reshape(-1), shift.astype(WIDE).reshape(-1)
     own_blocks = lax.dynamic_slice_in_dim(deal[0], 2 * place, 2, axis=1)
     local_pos = (own_blocks[:, :, None] * blk + jnp.arange(blk, dtype=jnp.int32)).reshape(micro, rows)
     valid = (local_pos < lengths[0][:, None])[:, :, None]
-    inputs = tokens[0].astype(wide)
+    inputs = tokens[0].astype(WIDE)
     centered = inputs - jnp.mean(inputs, axis=-1, keepdims=True)
     inv_std = lax.rsqrt(jnp.mean(centered * centered, axis=-1, keepdims=True) + EPS)
-    hidden_home = (centered * inv_std * gain + shift).astype(low)
-    gout_home = jnp.where(valid, cotangent[0], jnp.zeros((), low))
-
-    up_w = columns_of(w_up, 1, core, shards)
-    hidden = to_plane(hidden_home, core, blk)
-    qkv_w = columns_of(w_qkv, 3, core, shards)
-    gout = to_plane(gout_home, core, blk)
-    down_w = lax.dynamic_slice_in_dim(w_down, core * hidden_units, hidden_units, 0)
+    hidden_home = (centered * inv_std * gain + shift).astype(LOW)
+    gout_home = jnp.where(valid, cotangent[0], jnp.zeros((), LOW))
+
+    h_received = for_other(after(hidden_home, small), core, blk)
+    up_sent = columns_sent([after(piece, small) for piece in columns_cut(w_up, 1, core, shard)])
+    g_received = for_other(after(gout_home, h_received), core, blk)
+    h_first, h_rest = slots_of(hidden_home, h_received, core, place, blk)
+    h_pieces = spread_first(after(h_first, *[piece for _, _, piece in up_sent]))
+    early = [piece for _, _, piece in h_pieces]
+    h_rest = jnp.concatenate(h_rest)
+    g_first, g_rest = slots_of(gout_home, after(g_received, h_rest), core, place, blk)
+    h_pieces = h_pieces + spread_rest(after(h_rest, *early), blk)
+    hidden_own = placed(h_pieces, shard, 4 * blk)
+    hidden = (hidden_own, swap_dp(hidden_own))
+    up_w = placed(up_sent, shard, w_up.shape[0])
+    g_pieces = spread_first(after(g_first, *early))
+    g_pieces = g_pieces + spread_rest(after(jnp.concatenate(g_rest), hidden_own, g_pieces[0][2]), blk)
+
+    bias_ends = (bias_out.astype(WIDE) + bias_down.astype(WIDE)).reshape(-1)
+    meta = meta.astype(jnp.int32)
+    plane_len = meta[:, blocks] * 64 + meta[:, blocks + 1]
+    plane_deal = meta[:, :blocks].reshape(4, 4, 2)[:, (place - jnp.arange(4, dtype=jnp.int32)) % 4]
+    deal_own = pick(plane_deal, core, 2)
+    deal_oth = pick(plane_deal, 1 - core, 2)
+    up_b = lax.dynamic_slice_in_dim(bias_up.reshape(-1), spot * units, units).astype(WIDE)
+    qkv_b = pick(bias_qkv.reshape(3, 8, head_cols), spot, 1).reshape(-1).astype(WIDE)
+
+    acts, slopes, dups, datts = [], [], [], []
+    for h in hidden:
+        act, slope = up_call(h, up_w, up_b)
+        acts.append(act)
+        slopes.append(slope)
+    gout_own = placed(g_pieces, shard, 4 * blk, acts[1])
+    gout = (gout_own, swap_dp(gout_own))
+    qkv_sent = columns_sent([after(piece, gout_own) for piece in columns_cut(w_qkv, 3, core, shard)])
+    qkv_w = placed(qkv_sent, shard, w_qkv.shape[0])
+    tables = rope_tables(8 * blk)
+    down_w = lax.dynamic_slice_in_dim(w_down, core * units, units, 0)
     out_w = lax.dynamic_slice_in_dim(w_out, core * head_cols, head_cols, 0)
-    up_b = lax.dynamic_slice_in_dim(bias_up, (2 * shard + core) * hidden_units, hidden_units)
-    qkv_b = pick(bias_qkv.reshape(3, 2 * shards, head_cols), 2 * shard + core, 1).reshape(-1)
-
-    acts, dups, joins, datts = [], [], [], []
-    for h, g in zip(hidden, gout):
-        upward = jnp.dot(h, up_w, preferred_element_type=wide) + up_b
-        act, slope = gelu_pair(upward)
-        acts.append(act.astype(low))
-        joins.append((jnp.dot(h, qkv_w, preferred_element_type=wide) + qkv_b).astype(low))
-        dups.append((contract_cols(g, down_w) * slope.astype(low).astype(wide)).astype(low))
-        datts.append(contract_cols(g, out_w).astype(low))
-
-    def both(first, second):
-        return (contract_rows(first[0], second[0]) + contract_rows(first[1], second[1])).astype(low)
-
-    g_down = both(acts, gout)
-    g_up = both(hidden, dups)
-    g_up = lax.all_to_all(g_up, "fsdp", 0, 0, tiled=True)
-    t_down = sum_ctx(g_down, place)
-    t_up = sum_ctx(g_up, place)
-
-    per_seq = (shards, lined * blk, -1)
-    side_own, side_oth = attention_call(
-        deal_own, deal_oth, plane_len,
-        joins[0].reshape(per_seq), joins[1].reshape(per_seq),
-        datts[0].reshape(per_seq), datts[1].reshape(per_seq), blk,
-    )
-    flat = lambda piece: piece.reshape(shards * lined * blk, -1)
-    atts = [flat(side_own[0]), flat(side_oth[0])]
-    dfused = [jnp.concatenate([flat(piece) for piece in side[1:]], axis=1) for side in (side_own, side_oth)]
-
-    g_out = both(atts, gout)
-    g_qkv = both(hidden, dfused)
-    g_qkv = lax.all_to_all(g_qkv, "fsdp", 0, 0, tiled=True)
-    t_out = sum_ctx(g_out, place)
-    t_qkv = sum_ctx(g_qkv, place)
-
-    def forward_part(side):
-        return jnp.dot(acts[side], down_w, preferred_element_type=wide) + jnp.dot(
-            atts[side], out_w, preferred_element_type=wide
-        )
-
-    def backward_part(side):
-        return contract_cols(dups[side], up_w) + contract_cols(dfused[side], qkv_w)
-
-    mixed = to_home(forward_part(0), forward_part(1).astype(low), core, micro, blk)
-    d_hidden = to_home(backward_part(0), backward_part(1).astype(low), core, micro, blk).astype(wide)
-
-    result = jnp.where(valid, inputs + mixed.astype(wide) + bias_out + bias_down, 0.0).astype(low)
+
+    def scatter(grad):
+        return lax.psum_scatter(grad, "ctx", scatter_dimension=0, tiled=True)
+
+    def gather(piece):
+        return lax.all_gather(piece, "ctx", axis=0, tiled=True)
+
+    def exchange(piece):
+        return lax.all_to_all(piece[0], "fsdp", 0, 0, tiled=True)
+
+    g_down = grad_call(acts, [gout])[0]
+    t_down = gather(scatter(g_down))
+    for g, slope in zip((after(gout[0], g_down), gout[1]), slopes):
+        dup, datt = down_back_call(g, slope, down_w, out_w)
+        dups.append(dup)
+        datts.append(datt)
+    g_up, s_up = grad_call((after(hidden[0], *dups), hidden[1]), [dups], sums=True, dealt=True)
+    x_up = exchange(scatter(g_up))
+    t_up = gather(x_up[None])
+    joins = [join_call(after(h, g_up), qkv_w, qkv_b) for h in hidden]
+
+    per_seq = (4, 4 * blk, -1)
+    shaped = [piece.reshape(per_seq) for piece in (joins[0], joins[1], datts[0], datts[1])]
+    sides = attention_call(deal_own, deal_oth, plane_len, *shaped, tables, blk, 0, 4)
+    sides = [piece.reshape(16 * blk, -1) for piece in sides]
+    atts = [sides[0], sides[4]]
+    turned = [sides[1:4], sides[5:8]]
+
+    g_qkv, s_q, s_k, s_v = grad_call(
+        hidden, [(turned[0][i], turned[1][i]) for i in range(3)], sums=True, dealt=True
+    )
+    x_qkv = exchange(scatter(g_qkv))
+    t_qkv = gather(x_qkv[None])
+    b_oth = backward_call(dups[1], after(turned[1], g_qkv, t_down, x_up), up_w, qkv_w)
+    o = grad_call(atts, [(after(gout[0], b_oth), gout[1])])[0]
+    in_o = inward(o)
+    b_total = backward_call(after(dups[0], o), turned[0], up_w, qkv_w, swap_dp(b_oth))
+    d_hidden, d_hop = collect(b_total, shard)
+    f_oth = forward_call(after(acts[1], b_total, in_o), atts[1], down_w, out_w)
+    o = o + in_o
+    ac_o = across(o)
+    o_down = rows_out(core, shard, t_down, after(swap_dp(t_down), f_oth))
+    f_total = forward_call(after(acts[0], o_down, ac_o, *d_hop), atts[0], down_w, out_w, swap_dp(f_oth))
+    o = o + ac_o
+    out_o = outward(o)
+    t_out = line_end(o, out_o, place)
+    mixed, _ = collect(f_total, shard)
+    t_up = after(t_up, f_total)
+    o_up = cols_out(core, shard, t_up, swap_dp(t_up), 1)
+    d_hidden = to_home(d_hidden, core, place, blk).astype(WIDE)
+    mixed = to_home(mixed, core, place, blk)
+    sums_tp = line_sum(jnp.concatenate([s_up, s_q, s_k, s_v], axis=1), place)
+    tails = lax.all_gather(sums_tp, ("fsdp", "dp"), axis=0, tiled=True)
+    o_qkv = cols_out(core, shard, t_qkv, swap_dp(t_qkv), 3)
+    o_out = rows_out(core, shard, t_out, swap_dp(t_out))
+
+    result = jnp.where(valid, inputs + mixed.astype(WIDE) + bias_ends, 0.0).astype(LOW)
     normed = centered * inv_std
     d_norm = d_hidden * gain
     d_inputs = inv_std * (
@@ -633,45 +996,18 @@
         - jnp.mean(d_norm, axis=-1, keepdims=True)
         - normed * jnp.mean(d_norm * normed, axis=-1, keepdims=True)
     )
-    back = (gout_home.astype(wide) + d_inputs).astype(low)
-
-    def column_sum(pair):
-        return sum(jnp.sum(piece.astype(wide), axis=0) for piece in pair)
-
-    spot = 2 * shard + core
-    s_up = lax.dynamic_update_slice_in_dim(
-        jnp.zeros((2 * shards * hidden_units,), wide), column_sum(dups), spot * hidden_units, 0
-    )
-    s_qkv = lax.dynamic_update_slice(
-        jnp.zeros((3, 2 * shards, head_cols), wide),
-        column_sum(dfused).reshape(3, 1, head_cols), (0, spot, 0),
-    ).reshape(-1)
-    s_gout = jnp.sum(gout_home.astype(wide), axis=(0, 1))
-    s_gain = jnp.sum(d_hidden * normed, axis=(0, 1))
-    s_shift = jnp.sum(d_hidden, axis=(0, 1))
-    sums = lax.psum(jnp.concatenate([s_gain, s_shift, s_gout, s_up, s_qkv]), ("dp", "ctx", "fsdp"))
-    at = 0
-    pieces = []
-    for size in (width, width, width, s_up.shape[0], s_qkv.shape[0]):
-        part = sums[at : at + size]
-        pieces.append(lax.dynamic_slice_in_dim(part, shard * (size // shards), size // shards))
-        at += size
-    d_gain, d_shift, d_row, d_bup, d_bqkv = pieces
-
-    def rows_out(mine):
-        pair = by_core(core, mine, swap_dp(mine), 0)
-        return pair.reshape(-1, mine.shape[1]).astype(wide)
-
-    def cols_out(mine, parts):
-        local = mine.shape[0] // shards
-        pair = by_core(core, mine, swap_dp(mine), 0)
-        pair = pair.reshape(2, shards, local, parts, -1).transpose(2, 3, 1, 0, 4)
-        return pair.reshape(local, -1).astype(wide)
-
-    return (
-        result[None], back[None], d_gain, d_shift, cols_out(t_qkv, 3), d_bqkv,
-        rows_out(t_out), d_row, cols_out(t_up, 1), d_bup, rows_out(t_down), d_row,
-    )
+    back = (gout_home.astype(WIDE) + d_inputs).astype(LOW)
+
+    d_bup = lax.dynamic_slice(tails, (2 * shard, 0), (2, units)).reshape(-1)
+    d_bqkv = tails[:, units:].reshape(8, 3, head_cols).transpose(1, 0, 2).reshape(-1)
+    d_bqkv = lax.dynamic_slice_in_dim(d_bqkv, shard * b_qkv.shape[0], b_qkv.shape[0])
+    sums = jnp.stack([
+        jnp.sum(d_hidden * normed, axis=(0, 1)), jnp.sum(d_hidden, axis=(0, 1)), jnp.sum(gout_home.astype(WIDE), axis=(0, 1)),
+    ])
+    sums = every_sum(sums, place)
+    sums = lax.dynamic_slice_in_dim(sums, shard * ln_gain.shape[0], ln_gain.shape[0], 1)
+
+    return result[None], back[None], sums[0], sums[1], o_qkv, d_bqkv, o_out, sums[2], o_up, d_bup, o_down, sums[2]
 
 
 def plane_fits(mesh, shapes):
@@ -683,7 +1019,7 @@
     heads = width // HEAD_DIM
     return (
         dp == 2
-        and dp * micro == ctx
+        and dp * micro == ctx == fsdp == 4
         and tokens.shape[0] == dp * fsdp
         and blocks == dp * ctx
         and heads % (2 * dp * fsdp) == 0

time: 1570 us -> 1080 us (0.69)
  matrix products: 312 us -> 0 us
  Pallas kernels: 70.9 us -> 377 us
  waiting for transfers between devices: 659 us -> 411 us
  blocking collectives: 155 us -> 18.4 us
  other arithmetic: 135 us -> 70.6 us
  local copies, waits for them, and re-layouts: 144 us -> 90.1 us
  starting transfers between devices: 65 us -> 86.7 us
    dot_general x24 -> x0, matrix products: 312 us -> none  [the longest x8 111 us: contract_cols(): lax.dot_general(left, right, (((1,), (1,)), ((), ())), preferred_element_...]
    pallas_call x0 -> x18, Pallas kernels: none -> 307 us  [the longest x10 168 us: row_call(): pl.pallas_call(body, grid=(count // tile,), in_specs=[rows_spec(a.shape[1...]
    psum x1 -> x0, waiting for transfers between devices: 113 us -> none  [plane_body(): lax.psum(jnp.concatenate([s_gain, s_shift, s_gout, s_up, s_qkv]), ('dp',...]
    all_gather x2 -> x3, waiting for transfers between devices: 118 us -> 6.3 us  [gather(): return lax.all_gather(piece, 'ctx', axis=0, tiled=True)]
    all_to_all x2 -> x0, blocking collectives: 105 us -> none  [to_plane(): dealt = lax.all_to_all(lined, 'ctx', 0, 0, tiled=True)]
    ppermute x12 -> x53, waiting for transfers between devices: 403 us -> 336 us  [the longest x38 249 us: swap_shard(): return lax.ppermute(value, 'fsdp', [(i, i ^ bits) for i in range(4)])]
    unnamed x120 -> x114, local copies, waits for them, and re-layouts: 62.6 us -> 19.9 us
    unnamed x1 -> x0, blocking collectives: 39.5 us -> none
  transfers between devices with their start and end apart: 35 -> 77, of which waited for: 10 -> 34; matrix products, arithmetic and copies ran while one was open for 32% -> 12% of each run, Pallas kernels for 5% -> 31%
where the time goes in v2:
time: 1080 us; the launch traced here: 1070 us
  waiting for transfers between devices  411 us (38%)
  Pallas kernels  377 us (35%)
  local copies, waits for them, and re-layouts  90.1 us (8%)
  starting transfers between devices  86.7 us (8%)
  other arithmetic  70.6 us (7%)
  blocking collectives  18.4 us (2%)
  between operations  15.6 us (1%)
    ppermute x38, waiting for transfers between devices, swap_shard(): return lax.ppermute(value, 'fsdp', [(i, i ^ bits) for i in range(4)])  249 us
    pallas_call x10, Pallas kernels, row_call(): pl.pallas_call(body, grid=(count // tile,), in_specs=[rows_spec(a.shape[1...  168 us
    pallas_call x4, Pallas kernels, grad_call(): pl.pallas_call(body, grid=(2 * steps,), in_specs=specs, out_specs=[fixed(...  86.8 us
    pallas_call x1, Pallas kernels, attention_call(): pl.pallas_call(kernel, grid_spec=pltpu.PrefetchScalarGridSpec(num_scalar_...  70.5 us
    all_to_all x2, waiting for transfers between devices, to_home(): lax.all_to_all(lined.reshape(4, blk, width), 'ctx', 0, 0, tiled=True)  42.5 us
    ppermute x38, starting transfers between devices, swap_shard(): return lax.ppermute(value, 'fsdp', [(i, i ^ bits) for i in range(4)])  40.6 us
    ppermute x6, waiting for transfers between devices, shift_ctx(): return lax.ppermute(value, 'ctx', [(i, (i + steps) % 4) for i in range(4)])  39.4 us
    ppermute x3, waiting for transfers between devices, inward(): return lax.ppermute(value, 'ctx', [(0, 1), (3, 2)])  33.2 us
  transfers between devices with their start and end apart: 77, of which 34 were waited for; matrix products, arithmetic and copies ran while one was open for 12% of the time, Pallas kernels for 31%

profile of v2, /device:TPU:0, one launch (start us, length us, event | category | flops | bytes accessed | tf_op | source)
XLA Modules:
  0.0 1069.3 jit_solution(10717150427523440582)
XLA Ops:
  48.5 14.7 %collective-permute-done.2 = bf16[512,1024]{1,0:T(8,128)(2,1)S(1)} collective-permute-done((bf16[512,1024]{1,0:T(8,128)(2,1)S(1)}, bf16[512,1024]{1,0:T(8,128)(2,1)S(1)}, u32[]{:S(2)}, u32[]{:S(2)}) %collective-permute-start.2) | collective-permute-done | bytes 1048608 | tf_op jit(solution)/shard_map/ppermute | solution.py:355
  208.2 32.2 %collective-permute-done.23 = bf16[128,2048]{1,0:T(8,128)(2,1)S(1)} collective-permute-done((bf16[128,2048]{1,0:T(8,128)(2,1)S(1)}, bf16[128,2048]{1,0:T(8,128)(2,1)S(1)}, u32[]{:S(2)}, u32[]{:S(2)}) %collective-permute-start.23) | collective-permute-done | bytes 524320 | tf_op jit(solution)/shard_map/ppermute | solution.py:359
  241.9 18.1 %shard_map.230 = (bf16[2048,1024]{1,0:T(8,128)(2,1)}, bf16[2048,1024]{1,0:T(8,128)(2,1)}) custom-call(bf16[2048,2048]{1,0:T(8,128)(2,1)} %collective-permute-done.17.rows_ref.refs_1_, bf16[2048,1024]{1,0:T(8,128)(2,1)} %copy-done.13, f32[1,1024]{1,0:T(1,128)} %bitcast.219), custom_call_target="tpu_custom_call" | custom-call | flops 15461881856 | bytes 20975616 | tf_op jit(solution)/shard_map/pallas_call | solution.py:569
  267.0 15.9 %collective-permute-done.25 = bf16[192,2048]{1,0:T(8,128)(2,1)S(1)} collective-permute-done((bf16[192,2048]{1,0:T(8,128)(2,1)S(1)}, bf16[192,2048]{1,0:T(8,128)(2,1)S(1)}, u32[]{:S(2)}, u32[]{:S(2)}) %collective-permute-start.25) | collective-permute-done | bytes 786464 | tf_op jit(solution)/shard_map/ppermute | solution.py:355
  321.7 18.0 %shard_map.229 = (bf16[2048,1024]{1,0:T(8,128)(2,1)}, bf16[2048,1024]{1,0:T(8,128)(2,1)}) custom-call(bf16[2048,2048]{1,0:T(8,128)(2,1)} %constant_dynamic-update-slice_fusion.20.rows_ref.refs_0_, bf16[2048,1024]{1,0:T(8,128)(2,1)} %copy-done.13, f32[1,1024]{1,0:T(1,128)} %bitcast.220), custom_call_target="tpu_custom_call" | custom-call | flops 15461881856 | bytes 20975616 | tf_op jit(solution)/shard_map/pallas_call | solution.py:569
  339.7 25.4 %shard_map.231 = bf16[1024,2048]{1,0:T(8,128)(2,1)} custom-call(bf16[2048,1024]{1,0:T(8,128)(2,1)} %get-tuple-element.108.refs_0_, bf16[2048,1024]{1,0:T(8,128)(2,1)} %get-tuple-element.106.refs_1_.refs_0_, bf16[2048,2048]{1,0:T(8,128)(2,1)} %constant_dynamic-update-slice_fusion.4.refs_2_.rows_ref, bf16[2048,2048]{1,0:T(8,128)(2,1)} %collective-permute-done.31.refs_3_.rows_ref), custom_call_target="tpu_custom_call" | custom-call | flops 30923763712 | bytes 25165824 | tf_op jit(solution)/shard_map/pallas_call | solution.py:722
  371.1 17.2 %shard_map.232 = (bf16[2048,1024]{1,0:T(8,128)(2,1)}, bf16[2048,256]{1,0:T(8,128)(2,1)}) custom-call(bf16[2048,2048]{1,0:T(8,128)(2,1)} %constant_dynamic-update-slice_fusion.4.refs_2_.rows_ref, bf16[2048,1024]{1,0:T(8,128)(2,1)} %get-tuple-element.78.slope_ref, bf16[1024,2048]{1,0:T(8,128)(2,1)} %constant_dynamic-slice_fusion.29.down_ref.refs_2_.refs_3_, ...), custom_call_target="tpu_custom_call" | custom-call | flops 19327352832 | bytes 23068672 | tf_op jit(solution)/shard_map/pallas_call | solution.py:569
  388.2 16.9 %shard_map.233 = (bf16[2048,1024]{1,0:T(8,128)(2,1)}, bf16[2048,256]{1,0:T(8,128)(2,1)}) custom-call(bf16[2048,2048]{1,0:T(8,128)(2,1)} %collective-permute-done.31.refs_3_.rows_ref, bf16[2048,1024]{1,0:T(8,128)(2,1)} %get-tuple-element.80.slope_ref, bf16[1024,2048]{1,0:T(8,128)(2,1)} %constant_dynamic-slice_fusion.29.down_ref.refs_2_.refs_3_, ...), custom_call_target="tpu_custom_call" | custom-call | flops 19327352832 | bytes 23068672 | tf_op jit(solution)/shard_map/pallas_call | solution.py:569
  405.1 26.5 %shard_map.234 = (bf16[4,4,128,1024]{3,2,1,0:T(8,128)(2,1)}, f32[1,1024]{1,0:T(1,128)}) custom-call(bf16[2048,2048]{1,0:T(8,128)(2,1)} %constant_dynamic-update-slice_fusion.20.rows_ref.refs_0_, bf16[2048,2048]{1,0:T(8,128)(2,1)} %collective-permute-done.17.rows_ref.refs_1_, bf16[2048,1024]{1,0:T(8,128)(2,1)} %get-tuple-element.105.refs_2_.refs_0_, ...), custom_call_target="tpu_custom_call" | custom-call | flops 30923763712 | bytes 25165824 | tf_op jit(solution)/shard_map/pallas_call | solution.py:722
  461.2 16.4 %collective-permute-done.34 = bf16[512,768]{1,0:T(8,128)(2,1)S(1)} collective-permute-done((bf16[512,768]{1,0:T(8,128)(2,1)}, bf16[512,768]{1,0:T(8,128)(2,1)S(1)}, u32[]{:S(2)}, u32[]{:S(2)}) %collective-permute-start.34) | collective-permute-done | bytes 786464 | tf_op jit(solution)/shard_map/ppermute | solution.py:355
  501.0 70.5 %shard_map.237 = (bf16[4,512,256]{2,1,0:T(8,128)(2,1)}, bf16[4,512,256]{2,1,0:T(8,128)(2,1)}, bf16[4,512,256]{2,1,0:T(8,128)(2,1)}, bf16[4,512,256]{2,1,0:T(8,12...) custom-call(s32[4,4]{1,0:T(4,128)} %bitcast.223, ...), custom_call_target="tpu_custom_call" | custom-call | flops 69578473472 | bytes 16777216 | tf_op jit(solution)/shard_map/pallas_call | solution.py:837
  575.2 21.6 %shard_map.238 = (bf16[4,4,128,768]{3,2,1,0:T(8,128)(2,1)}, f32[1,256]{1,0:T(1,128)}, f32[1,256]{1,0:T(1,128)}, f32[1,256]{1,0:T(1,128)}) custom-call(bf16[2048,2048]{1,0:T(8,128)(2,1)} %constant_dynamic-update-slice_fusion.20.rows_ref.refs_0_, bf16[2048,2048]{1,0:T(8,128)(2,1)} %collective-permute-done.17.rows_ref.refs_1_, bf16[2048,256]{1,0:T(8,128)(2,1)} %bitcast.239, ...), custom_call_target="tpu_custom_call" | custom-call | flops 23192823808 | bytes 23068672 | tf_op jit(solution)/shard_map/pallas_call | solution.py:722
  603.1 21.2 %shard_map.239 = bf16[2048,2048]{1,0:T(8,128)(2,1)} custom-call(bf16[2048,1024]{1,0:T(8,128)(2,1)} %get-tuple-element.81.refs_3_.refs_0_, bf16[2048,256]{1,0:T(8,128)(2,1)} %bitcast.246, bf16[2048,256]{1,0:T(8,128)(2,1)} %bitcast.248, bf16[2048,256]{1,0:T(8,128)(2,1)} %bitcast.250, bf16[2048,1024]{1,0:T(8,128)(2,1)} %copy-done.13, bf16[2048,768]{1,0:T(8,128)(2,1)} %copy-done.16), custom_call_target="tpu_custom_call" | custom-call | flops 27058294784 | bytes 23068672 | tf_op jit(solution)/shard_map/pallas_call | solution.py:569
  638.9 22.2 %shard_map.241 = bf16[2048,2048]{1,0:T(8,128)(2,1)} custom-call(bf16[2048,1024]{1,0:T(8,128)(2,1)} %get-tuple-element.105.refs_2_.refs_0_, bf16[2048,256]{1,0:T(8,128)(2,1)} %bitcast.240, bf16[2048,256]{1,0:T(8,128)(2,1)} %bitcast.242, bf16[2048,256]{1,0:T(8,128)(2,1)} %bitcast.244, bf16[2048,2048]{1,0:T(8,128)(2,1)} %collective-permute-done.36.refs_4_, ...), custom_call_target="tpu_custom_call" | custom-call | flops 27058294784 | bytes 31457280 | tf_op jit(solution)/shard_map/pallas_call | solution.py:569
  661.1 23.9 %collective-permute-done.37 = bf16[256,2048]{1,0:T(8,128)(2,1)S(1)} collective-permute-done((bf16[256,2048]{1,0:T(8,128)(2,1)}, bf16[256,2048]{1,0:T(8,128)(2,1)S(1)}, u32[]{:S(2)}, u32[]{:S(2)}) %collective-permute-start.37) | collective-permute-done | bytes 1048608 | tf_op jit(solution)/shard_map/ppermute | solution.py:453
  685.1 16.2 %shard_map.242 = bf16[2048,2048]{1,0:T(8,128)(2,1)} custom-call(bf16[2048,1024]{1,0:T(8,128)(2,1)} %get-tuple-element.106.refs_1_.refs_0_, bf16[2048,256]{1,0:T(8,128)(2,1)} %bitcast.238, bf16[1024,2048]{1,0:T(8,128)(2,1)} %constant_dynamic-slice_fusion.29.down_ref.refs_2_.refs_3_, bf16[256,2048]{1,0:T(8,128)(2,1)} %constant_dynamic-slice_fusion.28.out_w_ref.refs_3_.refs_4_), custom_call_target="tpu_custom_call" | custom-call | flops 19327352832 | bytes 18874368 | tf_op jit(solution)/shard_map/pallas_call | solution.py:569
  729.3 22.0 %collective-permute-done.40 = bf16[256,2048]{1,0:T(8,128)(2,1)} collective-permute-done((bf16[256,2048]{1,0:T(8,128)(2,1)}, bf16[256,2048]{1,0:T(8,128)(2,1)}, u32[]{:S(2)}, u32[]{:S(2)}) %collective-permute-start.40) | collective-permute-done | bytes 1048608 | tf_op jit(solution)/shard_map/ppermute | solution.py:355
  777.7 22.5 %collective-permute-done.51 = bf16[256,2048]{1,0:T(8,128)(2,1)} collective-permute-done((bf16[256,2048]{1,0:T(8,128)(2,1)}, bf16[256,2048]{1,0:T(8,128)(2,1)}, u32[]{:S(2)}, u32[]{:S(2)}) %collective-permute-start.51) | collective-permute-done | bytes 1048608 | tf_op jit(solution)/shard_map/ppermute | solution.py:355
  805.3 16.6 %shard_map.244 = bf16[2048,2048]{1,0:T(8,128)(2,1)} custom-call(bf16[2048,1024]{1,0:T(8,128)(2,1)} %get-tuple-element.108.refs_0_, bf16[2048,256]{1,0:T(8,128)(2,1)} %bitcast.234, bf16[2048,2048]{1,0:T(8,128)(2,1)} %collective-permute-done.41.refs_2_, bf16[1024,2048]{1,0:T(8,128)(2,1)} %constant_dynamic-slice_fusion.29.down_ref.refs_2_.refs_3_, ...), custom_call_target="tpu_custom_call" | custom-call | flops 19327352832 | bytes 27262976 | tf_op jit(solution)/shard_map/pallas_call | solution.py:569
  846.9 17.1 %collective-permute-done.47 = bf16[256,2048]{1,0:T(8,128)(2,1)S(1)} collective-permute-done((bf16[256,2048]{1,0:T(8,128)(2,1)}, bf16[256,2048]{1,0:T(8,128)(2,1)S(1)}, u32[]{:S(2)}, u32[]{:S(2)}) %collective-permute-start.47) | collective-permute-done | bytes 1048608 | tf_op jit(solution)/shard_map/ppermute | solution.py:355
  867.9 22.5 %collective-permute-done.46 = bf16[256,2048]{1,0:T(8,128)(2,1)S(1)} collective-permute-done((bf16[256,2048]{1,0:T(8,128)(2,1)S(1)}, bf16[256,2048]{1,0:T(8,128)(2,1)S(1)}, u32[]{:S(2)}, u32[]{:S(2)}) %collective-permute-start.46) | collective-permute-done | bytes 1048608 | tf_op jit(solution)/shard_map/ppermute | solution.py:355
  912.3 18.4 %all-to-all-done.2 = bf16[4,128,2048]{2,1,0:T(8,128)(2,1)S(1)} async-done(((bf16[4,128,2048]{2,1,0:T(8,128)(2,1)}), bf16[4,128,2048]{2,1,0:T(8,128)(2,1)S(1)}, u32[]{:S(2)}, u32[]{:S(2)}) %all-to-all-start.2) | async-done | bytes 2097184 | tf_op jit(solution)/shard_map/all_to_all | solution.py:431
  967.6 24.0 %all-to-all-done.1 = bf16[4,128,2048]{2,1,0:T(8,128)(2,1)} async-done(((bf16[4,128,2048]{2,1,0:T(8,128)(2,1)}), bf16[4,128,2048]{2,1,0:T(8,128)(2,1)}, u32[]{:S(2)}, u32[]{:S(2)}) %all-to-all-start.1) | async-done | bytes 2097184 | tf_op jit(solution)/shard_map/all_to_all | solution.py:431
  1005.8 19.1 %shard_map.245 = f32[512,6144]{1,0:T(8,128)} custom-call(s32[2]{0:T(128)} %pad_add_fusion.where, bf16[4,4,128,768]{3,2,1,0:T(8,128)(2,1)} %bitcast.188, bf16[4,4,128,768]{3,2,1,0:T(8,128)(2,1)} %collective-permute-done.60.oth_ref), custom_call_target="tpu_custom_call" | custom-call | bytes 18874368 | tf_op jit(solution)/shard_map/pallas_call | solution.py:534
  (411 shorter events, 514.8 us)
Async XLA Ops:
  7.3 493.8 %reduce-scatter.4.cloned.1.call-start = ((), (), s32[]{:S(2)}) async-start(), calls=%async_computation.7 | async-start | bytes 5242880 | tf_op jit(solution)/shard_map/reduce_scatter | solution.py:937
  38.7 48.1 %collective-permute-start.3 = (bf16[512,1024]{1,0:T(8,128)(2,1)}, bf16[512,1024]{1,0:T(8,128)(2,1)}, u32[]{:S(2)}, u32[]{:S(2)}) collective-permute-start(bf16[512,1024]{1,0:T(8,128)(2,1)} %get-tuple-element.66), channel_id=1, source_target_pairs={{0,2},{1,3},{2,0},{3,1},{4,6},{5,7},{6,4},{7,5},{8,10},{9,11},{10,... | collective-permute-start | bytes 3145736 | tf_op jit(solution)/shard_map/ppermute | solution.py:355
  39.2 47.5 %collective-permute-start.4 = (bf16[512,1024]{1,0:T(8,128)(2,1)}, bf16[512,1024]{1,0:T(8,128)(2,1)}, u32[]{:S(2)}, u32[]{:S(2)}) collective-permute-start(bf16[512,1024]{1,0:T(8,128)(2,1)} %get-tuple-element.67), channel_id=1, source_target_pairs={{0,3},{1,2},{2,1},{3,0},{4,7},{5,6},{6,5},{7,4},{8,11},{9,10},{10,... | collective-permute-start | bytes 3145736 | tf_op jit(solution)/shard_map/ppermute | solution.py:355
  176.3 65.6 %collective-permute-start.17 = (bf16[2048,2048]{1,0:T(8,128)(2,1)}, bf16[2048,2048]{1,0:T(8,128)(2,1)}, u32[]{:S(2)}, u32[]{:S(2)}) collective-permute-start(bf16[2048,2048]{1,0:T(8,128)(2,1)} %constant_dynamic-update-slice_fusion.20.rows_ref.refs_0_), channel_id=1, source_target_pairs={{0,16},{16,0},{1,17},{17,1},{2,18},{18,2},{3,19},{19,3},{4,20},{20... | collective-permute-start | bytes 25165832 | tf_op jit(solution)/shard_map/ppermute | solution.py:351
  195.3 46.5 %collective-permute-start.22 = (bf16[128,2048]{1,0:T(8,128)(2,1)S(1)}, bf16[128,2048]{1,0:T(8,128)(2,1)S(1)}, u32[]{:S(2)}, u32[]{:S(2)}) collective-permute-start(bf16[128,2048]{1,0:T(8,128)(2,1)S(1)} %get-tuple-element.166), channel_id=1, source_target_pairs={{0,4},{4,8},{8,12},{12,0},{1,5},{5,9},{9,13},{13,1},{2,6},{6,10},{... | collective-permute-start | bytes 1572872 | tf_op jit(solution)/shard_map/ppermute | solution.py:359
  207.7 53.2 %collective-permute-start.20 = (bf16[128,2048]{1,0:T(8,128)(2,1)S(1)}, bf16[128,2048]{1,0:T(8,128)(2,1)S(1)}, u32[]{:S(2)}, u32[]{:S(2)}) collective-permute-start(bf16[128,2048]{1,0:T(8,128)(2,1)S(1)} %get-tuple-element.75), channel_id=1, source_target_pairs={{0,2},{1,3},{2,0},{3,1},{4,6},{5,7},{6,4},{7,5},{8,10},{9,11},{10,... | collective-permute-start | bytes 1572872 | tf_op jit(solution)/shard_map/ppermute | solution.py:355
  365.1 206.4 %reduce-scatter.6.cloned.1.call-start = ((), (), s32[]{:S(2)}) async-start(), calls=%async_computation.9 | async-start | bytes 5242880 | tf_op jit(solution)/shard_map/reduce_scatter | solution.py:937
  431.7 171.4 %all-gather.8.cloned.1.call-start = ((), (), s32[]{:S(2)}) async-start(), calls=%async_computation.8 | async-start | bytes 5242880 | tf_op jit(solution)/shard_map/all_gather | solution.py:940
  575.1 130.3 %reduce-scatter.8.cloned.1.call-start = ((), (), s32[]{:S(2)}) async-start(), calls=%async_computation.10 | async-start | bytes 3932160 | tf_op jit(solution)/shard_map/reduce_scatter | solution.py:937
  637.6 47.5 %collective-permute-start.37 = (bf16[256,2048]{1,0:T(8,128)(2,1)}, bf16[256,2048]{1,0:T(8,128)(2,1)S(1)}, u32[]{:S(2)}, u32[]{:S(2)}) collective-permute-start(bf16[256,2048]{1,0:T(8,128)(2,1)} %shard_map.240), channel_id=1, source_target_pairs={{0,4},{12,8},{1,5},{13,9},{2,6},{14,10},{3,7},{15,11},{16,20},{28,... | collective-permute-start | bytes 3145736 | tf_op jit(solution)/shard_map/ppermute | solution.py:453
  701.3 104.1 %collective-permute-start.41 = (bf16[2048,2048]{1,0:T(8,128)(2,1)}, bf16[2048,2048]{1,0:T(8,128)(2,1)}, u32[]{:S(2)}, u32[]{:S(2)}) collective-permute-start(bf16[2048,2048]{1,0:T(8,128)(2,1)} %shard_map.242), channel_id=1, source_target_pairs={{0,16},{16,0},{1,17},{17,1},{2,18},{18,2},{3,19},{19,3},{4,20},{20... | collective-permute-start | bytes 25165832 | tf_op jit(solution)/shard_map/ppermute | solution.py:351
  709.1 199.1 %all-gather.10.cloned.1.call-start = ((), (), s32[]{:S(2)}) async-start(), calls=%async_computation.11 | async-start | bytes 3932160 | tf_op jit(solution)/shard_map/all_gather | solution.py:940
  709.1 46.5 %collective-permute-start.32 = (bf16[1024,2048]{1,0:T(8,128)(2,1)}, bf16[1024,2048]{1,0:T(8,128)(2,1)}, u32[]{:S(2)}, u32[]{:S(2)}) collective-permute-start(bf16[1024,2048]{1,0:T(8,128)(2,1)} %all-gather.8.cloned.1.call-done.own_ref), channel_id=1, source_target_pairs={{0,16},{16,0},{1,17},{17,1},{2,18},{18,2},{3,19},{19,3},{4,20},{20... | collective-permute-start | bytes 12582920 | tf_op jit(solution)/shard_map/ppermute | solution.py:351
  720.7 226.5 %all-gather.12.cloned.1.call-start = ((), (), s32[]{:S(2)}) async-start(), calls=%async_computation.12 | async-start | bytes 5242880 | tf_op jit(solution)/shard_map/all_gather | solution.py:940
  728.8 48.9 %collective-permute-start.52 = (bf16[256,2048]{1,0:T(8,128)(2,1)S(1)}, bf16[256,2048]{1,0:T(8,128)(2,1)}, u32[]{:S(2)}, u32[]{:S(2)}) collective-permute-start(bf16[256,2048]{1,0:T(8,128)(2,1)S(1)} %get-tuple-element.122), channel_id=1, source_target_pairs={{0,2},{1,3},{2,0},{3,1},{4,6},{5,7},{6,4},{7,5},{8,10},{9,11},{10,... | collective-permute-start | bytes 3145736 | tf_op jit(solution)/shard_map/ppermute | solution.py:355
  771.4 55.4 %collective-permute-start.49 = (bf16[256,2048]{1,0:T(8,128)(2,1)}, bf16[256,2048]{1,0:T(8,128)(2,1)S(1)}, u32[]{:S(2)}, u32[]{:S(2)}) collective-permute-start(bf16[256,2048]{1,0:T(8,128)(2,1)} %get-tuple-element.123), channel_id=1, source_target_pairs={{0,1},{1,0},{2,3},{3,2},{4,5},{5,4},{6,7},{7,6},{8,9},{9,8},{10,11... | collective-permute-start | bytes 3145736 | tf_op jit(solution)/shard_map/ppermute | solution.py:355
  832.5 98.3 %all-to-all-start.2 = ((bf16[4,128,2048]{2,1,0:T(8,128)(2,1)}), bf16[4,128,2048]{2,1,0:T(8,128)(2,1)S(1)}, u32[]{:S(2)}, u32[]{:S(2)}) async-start(bf16[4,128,2048]{2,1,0:T(8,128)(2,1)} %bitcast.179), calls=%async_computation.4 | async-start | bytes 4194304 | tf_op jit(solution)/shard_map/all_to_all | solution.py:431
  846.7 84.2 %collective-permute-start.42 = (bf16[256,2048]{1,0:T(8,128)(2,1)}, bf16[256,2048]{1,0:T(8,128)(2,1)}, u32[]{:S(2)}, u32[]{:S(2)}) collective-permute-start(bf16[256,2048]{1,0:T(8,128)(2,1)} %get-tuple-element.131), channel_id=1, source_target_pairs={{0,1},{1,0},{2,3},{3,2},{4,5},{5,4},{6,7},{7,6},{8,9},{9,8},{10,11... | collective-permute-start | bytes 3145736 | tf_op jit(solution)/shard_map/ppermute | solution.py:355
  908.2 97.5 %collective-permute-start.60 = (bf16[4,4,128,768]{3,2,1,0:T(8,128)(2,1)}, bf16[4,4,128,768]{3,2,1,0:T(8,128)(2,1)}, u32[]{:S(2)}, u32[]{:S(2)}) collective-permute-start(bf16[4,4,128,768]{3,2,1,0:T(8,128)(2,1)} %bitcast.187), channel_id=1, source_target_pairs={{0,16},{16,0},{1,17},{17,1},{2,18},{18,2},{3,19},{19,3},{4,20},{20... | collective-permute-start | bytes 9437192 | tf_op jit(solution)/shard_map/ppermute | solution.py:351
  910.9 53.6 %collective-permute-start.64 = (bf16[256,2048]{1,0:T(8,128)(2,1)}, bf16[256,2048]{1,0:T(8,128)(2,1)}, u32[]{:S(2)}, u32[]{:S(2)}) collective-permute-start(bf16[256,2048]{1,0:T(8,128)(2,1)} %add.731), channel_id=1, source_target_pairs={{4,0},{8,12},{5,1},{9,13},{6,2},{10,14},{7,3},{11,15},{20,16},{24,... | collective-permute-start | bytes 3145736 | tf_op jit(solution)/shard_map/ppermute | solution.py:461
  938.0 53.6 %all-to-all-start.1 = ((bf16[4,128,2048]{2,1,0:T(8,128)(2,1)}), bf16[4,128,2048]{2,1,0:T(8,128)(2,1)}, u32[]{:S(2)}, u32[]{:S(2)}) async-start(bf16[4,128,2048]{2,1,0:T(8,128)(2,1)} %bitcast.180), calls=%async_computation.3 | async-start | bytes 4194304 | tf_op jit(solution)/shard_map/all_to_all | solution.py:431
  947.2 91.3 %collective-permute-start.66 = (bf16[4,4,128,1024]{3,2,1,0:T(8,128)(2,1)}, bf16[4,4,128,1024]{3,2,1,0:T(8,128)(2,1)}, u32[]{:S(2)}, u32[]{:S(2)}) collective-permute-start(bf16[4,4,128,1024]{3,2,1,0:T(8,128)(2,1)} %bitcast.185), channel_id=1, source_target_pairs={{0,16},{16,0},{1,17},{17,1},{2,18},{18,2},{3,19},{19,3},{4,20},{20... | collective-permute-start | bytes 12582920 | tf_op jit(solution)/shard_map/ppermute | solution.py:351
  965.9 59.0 %collective-permute-start.65 = (bf16[256,2048]{1,0:T(8,128)(2,1)S(1)}, bf16[256,2048]{1,0:T(8,128)(2,1)S(1)}, u32[]{:S(2)}, u32[]{:S(2)}) collective-permute-start(bf16[256,2048]{1,0:T(8,128)(2,1)S(1)} %broadcast_select_fusion.own_ref), channel_id=1, source_target_pairs={{0,16},{16,0},{1,17},{17,1},{2,18},{18,2},{3,19},{19,3},{4,20},{20... | collective-permute-start | bytes 3145736 | tf_op jit(solution)/shard_map/ppermute | solution.py:351
  993.9 58.5 %collective-permute-start.48 = (bf16[2,128,2048]{2,1,0:T(8,128)(2,1)}, bf16[2,128,2048]{2,1,0:T(8,128)(2,1)S(1)}, u32[]{:S(2)}, u32[]{:S(2)}) collective-permute-start(bf16[2,128,2048]{2,1,0:T(8,128)(2,1)} %dynamic-slice_bitcast_fusion.1), channel_id=1, source_target_pairs={{0,16},{16,0},{1,17},{17,1},{2,18},{18,2},{3,19},{19,3},{4,20},{20... | collective-permute-start | bytes 3145736 | tf_op jit(solution)/shard_map/ppermute | solution.py:351
  (103 other events, 2656.6 us)
Sparse Core Ops, SparseCore 0:
  365.3 75.1 reduce-scatter.3
  442.9 77.2 reduce-scatter.5
  521.8 81.2 all-gather.7
  624.4 81.0 reduce-scatter.7
  720.8 84.5 all-gather.9
  806.8 124.2 all-gather.11

commit v3 on v2

--- a/solution.py
+++ b/solution.py
@@ -374,27 +374,10 @@
     return swap_dp(pick(rows.reshape(micro, 2, blk, width), 1 - core, 1))
 
 
-def slots_of(rows, received, core, place, blk):
+def deal_out(rows, received, core, blk):
     micro, _, width = rows.shape
-    split = rows.reshape(micro, 2, blk, width)
-    lined = by_core(core, pick(split, core, 1), received, 0).reshape(4, blk, width)
-    first = pick(lined, place, 0)
-    rest = [shift_ctx(pick(lined, (place + steps) % 4, 0), steps) for steps in (1, 2, 3)]
-    return first, rest
-
-
-def spread_first(rows):
-    return [(bits, 0, swap_shard(rows, bits)) for bits in (1, 2, 3)] + [(0, 0, rows)]
-
-
-def spread_rest(rows, start):
-    half = rows.shape[0] // 2
-    top, end = rows[:half], rows[half:]
-    x_top, y_end = swap_shard(top, 1), swap_shard(end, 2)
-    x_end, y_top = swap_shard(end, 1), swap_shard(top, 2)
-    d_top, d_end = swap_shard(x_top, 2), swap_shard(y_end, 1)
-    pairs = ((0, top, end), (1, x_top, x_end), (2, y_top, y_end), (3, d_top, d_end))
-    return [(bits, start, one) for bits, one, _ in pairs] + [(bits, start + half, two) for bits, _, two in pairs]
+    lined = by_core(core, pick(rows.reshape(micro, 2, blk, width), core, 1), received, 0).reshape(4, blk, width)
+    return lax.all_to_all(lined, "ctx", 0, 0, tiled=True).reshape(4 * blk, width)
 
 
 def placed(pieces, shard, size, *gates):
@@ -411,7 +394,7 @@
     return total.astype(LOW)
 
 
-def collect(total, shard):
+def collect(total, shard, *gates):
     size = total.shape[0] // 4
     half = size // 2
 
@@ -420,15 +403,14 @@
 
     via_x, via_y = swap_shard(part(3, 0), 1), swap_shard(part(3, 1), 2)
     x_top, y_end = swap_shard(part(1, 0), 1), swap_shard(part(2, 1), 2)
-    y_top = swap_shard(plus(part(2, 0), via_x), 2)
-    x_end = swap_shard(plus(part(1, 1), via_y), 1)
-    return jnp.concatenate([plus(part(0, 0), x_top, y_top), plus(part(0, 1), x_end, y_end)]), (via_x, via_y)
+    y_top = swap_shard(plus(part(2, 0), after(via_x, *gates)), 2)
+    x_end = swap_shard(plus(part(1, 1), after(via_y, *gates)), 1)
+    return jnp.concatenate([plus(part(0, 0), x_top, y_top), plus(part(0, 1), x_end, y_end)])
 
 
 def to_home(mine, core, place, blk):
     width = mine.shape[1]
-    lined = jnp.concatenate([lax.dynamic_slice_in_dim(mine, (place - j) % 4 * blk, blk, 0) for j in range(4)])
-    lined = lax.all_to_all(lined.reshape(4, blk, width), "ctx", 0, 0, tiled=True).reshape(2, 2, blk, width)
+    lined = lax.all_to_all(mine.reshape(4, blk, width), "ctx", 0, 0, tiled=True).reshape(2, 2, blk, width)
     kept = pick(lined, core, 0)
     received = swap_dp(pick(lined, 1 - core, 0))
     return by_core(core, kept, received, 1).reshape(2, 2 * blk, width)
@@ -514,9 +496,9 @@
     )
 
 
-def cols_out(core, shard, own, oth, parts):
+def cols_out(core, shard, own, oth, parts, held):
     lines, columns, rows, width = own.shape
-    width = width // parts
+    width = width // held
 
     def kernel(where, own_ref, oth_ref, out_ref):
         side = pl.program_id(2)
@@ -652,12 +634,12 @@
     return row_call(body, tiled, [up_w, qkv_w], [up_w.shape[0]], flops)[0]
 
 
-def grad_call(left, rights, left_part=(0, 1), right_part=(0, 1), sums=False, dealt=False, tile=512):
+def grad_call(left, rights, left_part=(0, 1), right_part=(0, 1), sums=False, dealt=False, flip=False, tile=512):
     steps = left[0].shape[0] // tile
     left_cols = left[0].shape[1] // left_part[1]
     right_cols = [pair[0].shape[1] // right_part[1] for pair in rights]
     count = len(rights)
-    piece = left_cols // 16
+    piece = (right_cols[0] if flip else left_cols) // 16
     made = 1 if dealt else count
 
     def body(*refs):
@@ -693,6 +675,11 @@
                 for grad, acc in zip(grads, accs):
                     grad[...] = acc[...].astype(LOW)
                 return
+            if flip:
+                for spot in range(16):
+                    part = accs[0][:, spot * piece : (spot + 1) * piece]
+                    grads[0][spot % 4, spot // 4] = part.T.astype(LOW)
+                return
             start = 0
             for acc, cols in zip(accs, right_cols):
                 for column in range(4):
@@ -715,7 +702,7 @@
     specs += [side_spec(cols, right_part[0], side) for side in (0, 1) for cols in right_cols]
     shapes = [jax.ShapeDtypeStruct((left_cols, cols), LOW) for cols in right_cols]
     if dealt:
-        shapes = [jax.ShapeDtypeStruct((4, 4, piece, sum(right_cols)), LOW)]
+        shapes = [jax.ShapeDtypeStruct((4, 4, piece, left_cols if flip else sum(right_cols)), LOW)]
     if sums:
         shapes += [jax.ShapeDtypeStruct((1, cols), WIDE) for cols in right_cols]
     rows = 2 * left[0].shape[0]
@@ -857,6 +844,38 @@
     return result
 
 
+def flipped_out(core, shard, own, oth, start):
+    lines, columns, rows, width = own.shape
+    width = width // 4
+
+    def kernel(where, own_ref, oth_ref, out_ref):
+        side = pl.program_id(1)
+
+        def write(ref):
+            for line in range(lines):
+                out_ref[:, line * rows : (line + 1) * rows] = ref[line, 0].astype(WIDE).T
+
+        @pl.when(side == 0)
+        def _():
+            write(own_ref)
+
+        @pl.when(side == 1)
+        def _():
+            write(oth_ref)
+
+    source = pl.BlockSpec((lines, 1, rows, width), lambda b, s, where: (0, b, 0, start))
+    target = pl.BlockSpec((width, lines * rows), lambda b, s, where: (where[0] ^ s, b))
+    return pl.pallas_call(
+        kernel,
+        grid_spec=pltpu.PrefetchScalarGridSpec(
+            num_scalar_prefetch=1, grid=(columns, 2), in_specs=[source, source], out_specs=target
+        ),
+        out_shape=jax.ShapeDtypeStruct((2 * width, lines * columns * rows), WIDE),
+        compiler_params=pltpu.CompilerParams(dimension_semantics=("arbitrary",) * 2),
+        cost_estimate=pl.CostEstimate(flops=0, transcendentals=0, bytes_accessed=3 * own.size),
+    )(jnp.stack([core, shard]).astype(jnp.int32), own, oth)
+
+
 def plane_body(
     tokens, cotangent, lengths, deal, ln_gain, ln_bias, w_qkv, b_qkv, w_out, b_out, w_up, b_up, w_down, b_down
 ):
@@ -899,22 +918,17 @@
     h_received = for_other(after(hidden_home, small), core, blk)
     up_sent = columns_sent([after(piece, small) for piece in columns_cut(w_up, 1, core, shard)])
     g_received = for_other(after(gout_home, h_received), core, blk)
-    h_first, h_rest = slots_of(hidden_home, h_received, core, place, blk)
-    h_pieces = spread_first(after(h_first, *[piece for _, _, piece in up_sent]))
-    early = [piece for _, _, piece in h_pieces]
-    h_rest = jnp.concatenate(h_rest)
-    g_first, g_rest = slots_of(gout_home, after(g_received, h_rest), core, place, blk)
-    h_pieces = h_pieces + spread_rest(after(h_rest, *early), blk)
-    hidden_own = placed(h_pieces, shard, 4 * blk)
+    h_dealt = deal_out(hidden_home, h_received, core, blk)
+    hidden_own = lax.all_gather(after(h_dealt, *[piece for _, _, piece in up_sent]), "fsdp", axis=0, tiled=True)
     hidden = (hidden_own, swap_dp(hidden_own))
     up_w = placed(up_sent, shard, w_up.shape[0])
-    g_pieces = spread_first(after(g_first, *early))
-    g_pieces = g_pieces + spread_rest(after(jnp.concatenate(g_rest), hidden_own, g_pieces[0][2]), blk)
+    g_dealt = deal_out(gout_home, after(g_received, h_dealt), core, blk)
+    gout_own = lax.all_gather(g_dealt, "fsdp", axis=0, tiled=True)
 
     bias_ends = (bias_out.astype(WIDE) + bias_down.astype(WIDE)).reshape(-1)
     meta = meta.astype(jnp.int32)
     plane_len = meta[:, blocks] * 64 + meta[:, blocks + 1]
-    plane_deal = meta[:, :blocks].reshape(4, 4, 2)[:, (place - jnp.arange(4, dtype=jnp.int32)) % 4]
+    plane_deal = meta[:, :blocks].reshape(4, 4, 2)
     deal_own = pick(plane_deal, core, 2)
     deal_oth = pick(plane_deal, 1 - core, 2)
     up_b = lax.dynamic_slice_in_dim(bias_up.reshape(-1), spot * units, units).astype(WIDE)
@@ -925,7 +939,7 @@
         act, slope = up_call(h, up_w, up_b)
         acts.append(act)
         slopes.append(slope)
-    gout_own = placed(g_pieces, shard, 4 * blk, acts[1])
+    gout_own = after(gout_own, *acts)
     gout = (gout_own, swap_dp(gout_own))
     qkv_sent = columns_sent([after(piece, gout_own) for piece in columns_cut(w_qkv, 3, core, shard)])
     qkv_w = placed(qkv_sent, shard, w_qkv.shape[0])
@@ -948,7 +962,8 @@
         dup, datt = down_back_call(g, slope, down_w, out_w)
         dups.append(dup)
         datts.append(datt)
-    g_up, s_up = grad_call((after(hidden[0], *dups), hidden[1]), [dups], sums=True, dealt=True)
+    waited = [piece for bits, _, piece in qkv_sent if bits]
+    g_up, s_up = grad_call((after(hidden[0], *dups, *waited), hidden[1]), [dups], sums=True, dealt=True)
     x_up = exchange(scatter(g_up))
     t_up = gather(x_up[None])
     joins = [join_call(after(h, g_up), qkv_w, qkv_b) for h in hidden]
@@ -960,35 +975,36 @@
     atts = [sides[0], sides[4]]
     turned = [sides[1:4], sides[5:8]]
 
+    g_out = grad_call(atts, [gout], dealt=True, flip=True)[0]
     g_qkv, s_q, s_k, s_v = grad_call(
-        hidden, [(turned[0][i], turned[1][i]) for i in range(3)], sums=True, dealt=True
-    )
-    x_qkv = exchange(scatter(g_qkv))
-    t_qkv = gather(x_qkv[None])
-    b_oth = backward_call(dups[1], after(turned[1], g_qkv, t_down, x_up), up_w, qkv_w)
-    o = grad_call(atts, [(after(gout[0], b_oth), gout[1])])[0]
-    in_o = inward(o)
-    b_total = backward_call(after(dups[0], o), turned[0], up_w, qkv_w, swap_dp(b_oth))
-    d_hidden, d_hop = collect(b_total, shard)
-    f_oth = forward_call(after(acts[1], b_total, in_o), atts[1], down_w, out_w)
-    o = o + in_o
-    ac_o = across(o)
-    o_down = rows_out(core, shard, t_down, after(swap_dp(t_down), f_oth))
-    f_total = forward_call(after(acts[0], o_down, ac_o, *d_hop), atts[0], down_w, out_w, swap_dp(f_oth))
-    o = o + ac_o
-    out_o = outward(o)
-    t_out = line_end(o, out_o, place)
-    mixed, _ = collect(f_total, shard)
-    t_up = after(t_up, f_total)
-    o_up = cols_out(core, shard, t_up, swap_dp(t_up), 1)
-    d_hidden = to_home(d_hidden, core, place, blk).astype(WIDE)
-    mixed = to_home(mixed, core, place, blk)
+        (after(hidden[0], g_out), hidden[1]), [(turned[0][i], turned[1][i]) for i in range(3)], sums=True, dealt=True
+    )
+    mine = scatter(jnp.concatenate([g_qkv, g_out], axis=3))[0]
+    qkv_cols = g_qkv.shape[3]
+    x_qkv = lax.all_to_all(mine[:, :, :qkv_cols], "fsdp", 0, 0, tiled=True)
+    t_mix = gather(jnp.concatenate([x_qkv, mine[:, :, qkv_cols:]], axis=2)[None])
     sums_tp = line_sum(jnp.concatenate([s_up, s_q, s_k, s_v], axis=1), place)
     tails = lax.all_gather(sums_tp, ("fsdp", "dp"), axis=0, tiled=True)
-    o_qkv = cols_out(core, shard, t_qkv, swap_dp(t_qkv), 3)
-    o_out = rows_out(core, shard, t_out, swap_dp(t_out))
-
-    result = jnp.where(valid, inputs + mixed.astype(WIDE) + bias_ends, 0.0).astype(LOW)
+    b_oth = backward_call(dups[1], after(turned[1], g_qkv, x_up), up_w, qkv_w)
+    f_oth = forward_call(after(acts[1], b_oth, t_down), atts[1], down_w, out_w)
+    b_total = backward_call(after(dups[0], f_oth), turned[0], up_w, qkv_w, swap_dp(b_oth))
+    f_total = forward_call(after(acts[0], b_total), atts[0], down_w, out_w, swap_dp(f_oth))
+    d_hidden = collect(b_total, shard, f_total)
+    mixed = collect(f_total, shard)
+    d_hidden = to_home(after(d_hidden, x_qkv), core, place, blk)
+    t_up = after(t_up, f_total, x_qkv)
+    o_up = cols_out(core, shard, t_up, after(swap_dp(t_up), tails), 1, 1)
+    o_down = rows_out(core, shard, t_down, after(swap_dp(t_down), o_up))
+    d_hidden = after(d_hidden, o_down).astype(WIDE)
+    mixed = to_home(mixed, core, place, blk)
+    t_mix = after(t_mix, o_down)
+    t_mix = (t_mix, swap_dp(t_mix))
+    o_qkv = cols_out(core, shard, *t_mix, 3, 4)
+    o_out = flipped_out(core, shard, *t_mix, 3)
+
+    inputs = after(tokens[0], f_total).astype(WIDE)
+    centered = inputs - jnp.mean(inputs, axis=-1, keepdims=True)
+    inv_std = lax.rsqrt(jnp.mean(centered * centered, axis=-1, keepdims=True) + EPS)
     normed = centered * inv_std
     d_norm = d_hidden * gain
     d_inputs = inv_std * (
@@ -998,6 +1014,8 @@
     )
     back = (gout_home.astype(WIDE) + d_inputs).astype(LOW)
 
+    mixed = after(mixed, o_qkv, o_out)
+    result = jnp.where(valid, inputs + mixed.astype(WIDE) + bias_ends, 0.0).astype(LOW)
     d_bup = lax.dynamic_slice(tails, (2 * shard, 0), (2, units)).reshape(-1)
     d_bqkv = tails[:, units:].reshape(8, 3, head_cols).transpose(1, 0, 2).reshape(-1)
     d_bqkv = lax.dynamic_slice_in_dim(d_bqkv, shard * b_qkv.shape[0], b_qkv.shape[0])

time: 1080 us -> 938 us (0.87)
  waiting for transfers between devices: 411 us -> 299 us
  blocking collectives: 18.4 us -> 71.8 us
  local copies, waits for them, and re-layouts: 90.1 us -> 43.8 us
  starting transfers between devices: 86.7 us -> 58.4 us
    ppermute x38 -> x20, waiting for transfers between devices: 249 us -> 103 us  [swap_shard(): return lax.ppermute(value, 'fsdp', [(i, i ^ bits) for i in range(4)])]
    all_gather x0 -> x2, waiting for transfers between devices: none -> 75.2 us  [the longest x1 47.2 us: plane_body(): gout_own = lax.all_gather(g_dealt, 'fsdp', axis=0, tiled=True)]
    all_to_all x0 -> x1, blocking collectives: none -> 53.2 us  [deal_out(): lax.all_to_all(lined, 'ctx', 0, 0, tiled=True).reshape(4 * blk, width)]
    ppermute x6 -> x0, waiting for transfers between devices: 39.4 us -> none  [shift_ctx(): return lax.ppermute(value, 'ctx', [(i, (i + steps) % 4) for i in range(4)])]
    all_gather x3, waiting for transfers between devices: 6.3 us -> 43.8 us  [gather(): return lax.all_gather(piece, 'ctx', axis=0, tiled=True)]
    dynamic_update_slice x30 -> x8, local copies, waits for them, and re-layouts: 28.8 us -> 1.9 us  [placed(): lax.dynamic_update_slice(whole, piece, ((shard ^ bits) * size + start, 0))]
    ppermute x3 -> x2, waiting for transfers between devices: 33.2 us -> 13.7 us  [inward(): return lax.ppermute(value, 'ctx', [(0, 1), (3, 2)])]
    ppermute x38 -> x20, starting transfers between devices: 40.6 us -> 23.7 us  [swap_shard(): return lax.ppermute(value, 'fsdp', [(i, i ^ bits) for i in range(4)])]
  transfers between devices with their start and end apart: 77 -> 52, of which waited for: 34 -> 26; matrix products, arithmetic and copies ran while one was open for 12% -> 9% of each run, Pallas kernels for 31% -> 35%
where the time goes in v3:
time: 938 us; the launch traced here: 931 us
  Pallas kernels  379 us (40%)
  waiting for transfers between devices  299 us (32%)
  blocking collectives  71.8 us (8%)
  other arithmetic  63 us (7%)
  starting transfers between devices  58.4 us (6%)
  local copies, waits for them, and re-layouts  43.8 us (5%)
  between operations  15.3 us (2%)
    pallas_call x10, Pallas kernels, row_call(): pl.pallas_call(body, grid=(count // tile,), in_specs=[rows_spec(a.shape[1...  167 us
    ppermute x20, waiting for transfers between devices, swap_shard(): return lax.ppermute(value, 'fsdp', [(i, i ^ bits) for i in range(4)])  103 us
    pallas_call x4, Pallas kernels, grad_call(): pl.pallas_call(body, grid=(2 * steps,), in_specs=specs, out_specs=[fixed(...  86.8 us
    pallas_call x1, Pallas kernels, attention_call(): pl.pallas_call(kernel, grid_spec=pltpu.PrefetchScalarGridSpec(num_scalar_...  70.5 us
    all_to_all x1, blocking collectives, deal_out(): lax.all_to_all(lined, 'ctx', 0, 0, tiled=True).reshape(4 * blk, width)  53.2 us
    all_gather x1, waiting for transfers between devices, plane_body(): gout_own = lax.all_gather(g_dealt, 'fsdp', axis=0, tiled=True)  47.2 us
    all_gather x3, waiting for transfers between devices, gather(): return lax.all_gather(piece, 'ctx', axis=0, tiled=True)  43.8 us
    pallas_call x2, Pallas kernels, cols_out(): pl.pallas_call(kernel, grid_spec=pltpu.PrefetchScalarGridSpec(num_scalar_...  33.2 us
  transfers between devices with their start and end apart: 52, of which 26 were waited for; matrix products, arithmetic and copies ran while one was open for 9% of the time, Pallas kernels for 35%

profile of v3, /device:TPU:0, one launch (start us, length us, event | category | flops | bytes accessed | tf_op | source)
XLA Modules:
  0.0 930.7 jit_solution(12250884494402622324)
XLA Ops:
  44.4 22.6 %collective-permute-done.2 = bf16[512,1024]{1,0:T(8,128)(2,1)S(1)} collective-permute-done((bf16[512,1024]{1,0:T(8,128)(2,1)S(1)}, bf16[512,1024]{1,0:T(8,128)(2,1)S(1)}, u32[]{:S(2)}, u32[]{:S(2)}) %collective-permute-start.2) | collective-permute-done | bytes 1048608 | tf_op jit(solution)/shard_map/ppermute | solution.py:355
  66.9 22.6 %collective-permute-done.3 = bf16[512,1024]{1,0:T(8,128)(2,1)S(1)} collective-permute-done((bf16[512,1024]{1,0:T(8,128)(2,1)S(1)}, bf16[512,1024]{1,0:T(8,128)(2,1)S(1)}, u32[]{:S(2)}, u32[]{:S(2)}) %collective-permute-start.3) | collective-permute-done | bytes 1048608 | tf_op jit(solution)/shard_map/ppermute | solution.py:355
  97.0 53.2 %all_to_all.30 = bf16[4,128,2048]{2,1,0:T(8,128)(2,1)} all-to-all(bf16[4,128,2048]{2,1,0:T(8,128)(2,1)S(1)} %bitcast.166), channel_id=1, replica_groups=mesh['dp'=2,'ctx'=4,'fsdp'=4] {'ctx'}, dimensions={0} | all-to-all | bytes 4194304 | tf_op jit(solution)/shard_map/all_to_all | solution.py:380
  150.5 28.0 %all-gather.10.cloned.1.call-done.rows_ref.refs_0_ = bf16[2048,2048]{1,0:T(8,128)(2,1)} async-done(((bf16[512,2048]{1,0:T(8,128)(2,1)}), bf16[2048,2048]{1,0:T(8,128)(2,1)}) %all-gather.10.cloned.1.call-update) | async-done | bytes 8388624 | tf_op jit(solution)/shard_map/all_gather | solution.py:922
  184.4 18.3 %shard_map.229 = (bf16[2048,1024]{1,0:T(8,128)(2,1)}, bf16[2048,1024]{1,0:T(8,128)(2,1)}) custom-call(bf16[2048,2048]{1,0:T(8,128)(2,1)} %all-gather.10.cloned.1.call-done.rows_ref.refs_0_, bf16[2048,1024]{1,0:T(8,128)(2,1)} %copy-done.8, f32[1,1024]{1,0:T(1,128)} %bitcast.201), custom_call_target="tpu_custom_call" | custom-call | flops 15461881856 | bytes 20975616 | tf_op jit(solution)/shard_map/pallas_call | solution.py:551
  202.7 18.0 %shard_map.230 = (bf16[2048,1024]{1,0:T(8,128)(2,1)}, bf16[2048,1024]{1,0:T(8,128)(2,1)}) custom-call(bf16[2048,2048]{1,0:T(8,128)(2,1)} %collective-permute-done.6.rows_ref.refs_1_, bf16[2048,1024]{1,0:T(8,128)(2,1)} %copy-done.8, f32[1,1024]{1,0:T(1,128)} %bitcast.202), custom_call_target="tpu_custom_call" | custom-call | flops 15461881856 | bytes 20975616 | tf_op jit(solution)/shard_map/pallas_call | solution.py:551
  220.7 47.2 %all-gather.12.cloned.1.call-done.refs_2_.rows_ref = bf16[2048,2048]{1,0:T(8,128)(2,1)} async-done(((bf16[512,2048]{1,0:T(8,128)(2,1)}), bf16[2048,2048]{1,0:T(8,128)(2,1)}) %all-gather.12.cloned.1.call-update) | async-done | bytes 8388624 | tf_op jit(solution)/shard_map/all_gather | solution.py:926
  281.5 25.4 %shard_map.231 = bf16[1024,2048]{1,0:T(8,128)(2,1)} custom-call(bf16[2048,1024]{1,0:T(8,128)(2,1)} %get-tuple-element.109.refs_0_, bf16[2048,1024]{1,0:T(8,128)(2,1)} %get-tuple-element.107.refs_1_.refs_0_, bf16[2048,2048]{1,0:T(8,128)(2,1)} %all-gather.12.cloned.1.call-done.refs_2_.rows_ref, bf16[2048,2048]{1,0:T(8,128)(2,1)} %collective-permute-done.7.refs_3_.rows_ref), custom_call_target="tpu_custom_call" | custom-call | flops 30923763712 | bytes 25165824 | tf_op jit(solution)/shard_map/pallas_call | solution.py:709
  318.9 16.8 %shard_map.232 = (bf16[2048,1024]{1,0:T(8,128)(2,1)}, bf16[2048,256]{1,0:T(8,128)(2,1)}) custom-call(bf16[2048,2048]{1,0:T(8,128)(2,1)} %all-gather.12.cloned.1.call-done.refs_2_.rows_ref, bf16[2048,1024]{1,0:T(8,128)(2,1)} %get-tuple-element.80.slope_ref, bf16[1024,2048]{1,0:T(8,128)(2,1)} %constant_dynamic-slice_fusion.29.down_ref.refs_2_.refs_3_, ...), custom_call_target="tpu_custom_call" | custom-call | flops 19327352832 | bytes 23068672 | tf_op jit(solution)/shard_map/pallas_call | solution.py:551
  335.7 16.8 %shard_map.233 = (bf16[2048,1024]{1,0:T(8,128)(2,1)}, bf16[2048,256]{1,0:T(8,128)(2,1)}) custom-call(bf16[2048,2048]{1,0:T(8,128)(2,1)} %collective-permute-done.7.refs_3_.rows_ref, bf16[2048,1024]{1,0:T(8,128)(2,1)} %get-tuple-element.82.slope_ref, bf16[1024,2048]{1,0:T(8,128)(2,1)} %constant_dynamic-slice_fusion.29.down_ref.refs_2_.refs_3_, ...), custom_call_target="tpu_custom_call" | custom-call | flops 19327352832 | bytes 23068672 | tf_op jit(solution)/shard_map/pallas_call | solution.py:551
  352.8 26.8 %shard_map.234 = (bf16[4,4,128,1024]{3,2,1,0:T(8,128)(2,1)}, f32[1,1024]{1,0:T(1,128)}) custom-call(bf16[2048,2048]{1,0:T(8,128)(2,1)} %all-gather.10.cloned.1.call-done.rows_ref.refs_0_, bf16[2048,2048]{1,0:T(8,128)(2,1)} %collective-permute-done.6.rows_ref.refs_1_, bf16[2048,1024]{1,0:T(8,128)(2,1)} %get-tuple-element.108.refs_2_.refs_0_, ...), custom_call_target="tpu_custom_call" | custom-call | flops 30923763712 | bytes 25165824 | tf_op jit(solution)/shard_map/pallas_call | solution.py:709
  410.5 70.5 %shard_map.237 = (bf16[4,512,256]{2,1,0:T(8,128)(2,1)}, bf16[4,512,256]{2,1,0:T(8,128)(2,1)}, bf16[4,512,256]{2,1,0:T(8,128)(2,1)}, bf16[4,512,256]{2,1,0:T(8,12...) custom-call(s32[4,4]{1,0:T(4,128)} %bitcast.205, ...), custom_call_target="tpu_custom_call" | custom-call | flops 69578473472 | bytes 16777216 | tf_op jit(solution)/shard_map/pallas_call | solution.py:824
  497.9 21.4 %shard_map.239 = (bf16[4,4,128,768]{3,2,1,0:T(8,128)(2,1)}, f32[1,256]{1,0:T(1,128)}, f32[1,256]{1,0:T(1,128)}, f32[1,256]{1,0:T(1,128)}) custom-call(bf16[2048,2048]{1,0:T(8,128)(2,1)} %all-gather.10.cloned.1.call-done.rows_ref.refs_0_, bf16[2048,2048]{1,0:T(8,128)(2,1)} %collective-permute-done.6.rows_ref.refs_1_, bf16[2048,256]{1,0:T(8,128)(2,1)} %bitcast.219, ...), custom_call_target="tpu_custom_call" | custom-call | flops 23192823808 | bytes 23068672 | tf_op jit(solution)/shard_map/pallas_call | solution.py:709
  523.9 21.6 %shard_map.240 = bf16[2048,2048]{1,0:T(8,128)(2,1)} custom-call(bf16[2048,1024]{1,0:T(8,128)(2,1)} %get-tuple-element.83.refs_3_.refs_0_, bf16[2048,256]{1,0:T(8,128)(2,1)} %bitcast.228, bf16[2048,256]{1,0:T(8,128)(2,1)} %bitcast.230, bf16[2048,256]{1,0:T(8,128)(2,1)} %bitcast.232, bf16[2048,1024]{1,0:T(8,128)(2,1)} %copy-done.8, bf16[2048,768]{1,0:T(8,128)(2,1)} %copy-done.10), custom_call_target="tpu_custom_call" | custom-call | flops 27058294784 | bytes 23068672 | tf_op jit(solution)/shard_map/pallas_call | solution.py:551
  546.6 15.8 %shard_map.241 = bf16[2048,2048]{1,0:T(8,128)(2,1)} custom-call(bf16[2048,1024]{1,0:T(8,128)(2,1)} %get-tuple-element.107.refs_1_.refs_0_, bf16[2048,256]{1,0:T(8,128)(2,1)} %bitcast.226, bf16[1024,2048]{1,0:T(8,128)(2,1)} %constant_dynamic-slice_fusion.29.down_ref.refs_2_.refs_3_, bf16[256,2048]{1,0:T(8,128)(2,1)} %constant_dynamic-slice_fusion.28.out_w_ref.refs_3_.refs_4_), custom_call_target="tpu_custom_call" | custom-call | flops 19327352832 | bytes 18874368 | tf_op jit(solution)/shard_map/pallas_call | solution.py:551
  562.4 21.9 %shard_map.242 = bf16[2048,2048]{1,0:T(8,128)(2,1)} custom-call(bf16[2048,1024]{1,0:T(8,128)(2,1)} %get-tuple-element.108.refs_2_.refs_0_, bf16[2048,256]{1,0:T(8,128)(2,1)} %bitcast.220, bf16[2048,256]{1,0:T(8,128)(2,1)} %bitcast.222, bf16[2048,256]{1,0:T(8,128)(2,1)} %bitcast.224, bf16[2048,2048]{1,0:T(8,128)(2,1)} %collective-permute-done.11.refs_4_, ...), custom_call_target="tpu_custom_call" | custom-call | flops 27058294784 | bytes 31457280 | tf_op jit(solution)/shard_map/pallas_call | solution.py:551
  591.5 16.6 %shard_map.243 = bf16[2048,2048]{1,0:T(8,128)(2,1)} custom-call(bf16[2048,1024]{1,0:T(8,128)(2,1)} %get-tuple-element.109.refs_0_, bf16[2048,256]{1,0:T(8,128)(2,1)} %bitcast.216, bf16[2048,2048]{1,0:T(8,128)(2,1)} %collective-permute-done.12.refs_2_, bf16[1024,2048]{1,0:T(8,128)(2,1)} %constant_dynamic-slice_fusion.29.down_ref.refs_2_.refs_3_, ...), custom_call_target="tpu_custom_call" | custom-call | flops 19327352832 | bytes 27262976 | tf_op jit(solution)/shard_map/pallas_call | solution.py:551
  675.4 16.1 %collective-permute-done.30 = bf16[256,2048]{1,0:T(8,128)(2,1)} collective-permute-done((bf16[256,2048]{1,0:T(8,128)(2,1)}, bf16[256,2048]{1,0:T(8,128)(2,1)}, u32[]{:S(2)}, u32[]{:S(2)}) %collective-permute-start.30) | collective-permute-done | bytes 1048608 | tf_op jit(solution)/shard_map/ppermute | solution.py:355
  700.3 20.7 %all-gather.18.cloned.1.call-done = bf16[16,128,1024]{2,1,0:T(8,128)(2,1)} async-done(((bf16[4,128,1024]{2,1,0:T(8,128)(2,1)}), bf16[16,128,1024]{2,1,0:T(8,128)(2,1)}) %all-gather.18.cloned.1.call-update) | async-done | bytes 4194320 | tf_op jit(solution)/shard_map/all_gather | solution.py:954
  757.4 27.5 %all-to-all-done.5 = bf16[4,128,2048]{2,1,0:T(8,128)(2,1)S(1)} async-done(((bf16[4,128,2048]{2,1,0:T(8,128)(2,1)}), bf16[4,128,2048]{2,1,0:T(8,128)(2,1)S(1)}, u32[]{:S(2)}, u32[]{:S(2)}) %all-to-all-start.5) | async-done | bytes 2097184 | tf_op jit(solution)/shard_map/all_to_all | solution.py:413
  806.8 14.0 %shard_map.244 = f32[512,8192]{1,0:T(8,128)} custom-call(s32[2]{0:T(128)} %pad_add_fusion.where, bf16[4,4,128,1024]{3,2,1,0:T(8,128)(2,1)} %bitcast.171, bf16[4,4,128,1024]{3,2,1,0:T(8,128)(2,1)} %collective-permute-done.21.oth_ref), custom_call_target="tpu_custom_call" | custom-call | bytes 25165824 | tf_op jit(solution)/shard_map/pallas_call | solution.py:516
  820.9 14.0 %shard_map.245 = f32[2048,2048]{1,0:T(8,128)} custom-call(s32[2]{0:T(128)} %pad_add_fusion.where, bf16[1024,2048]{1,0:T(8,128)(2,1)} %all-gather.14.cloned.1.call-done.own_ref, bf16[1024,2048]{1,0:T(8,128)(2,1)} %collective-permute-done.20.oth_ref), custom_call_target="tpu_custom_call" | custom-call | bytes 25165824 | tf_op jit(solution)/shard_map/pallas_call | solution.py:478
  834.9 22.1 %all-gather.16.cloned.1.call-done = bf16[16,128,1024]{2,1,0:T(8,128)(2,1)} async-done(((bf16[4,128,1024]{2,1,0:T(8,128)(2,1)}), bf16[16,128,1024]{2,1,0:T(8,128)(2,1)}) %all-gather.16.cloned.1.call-update) | async-done | bytes 4194320 | tf_op jit(solution)/shard_map/all_gather | solution.py:954
  897.5 19.2 %shard_map.246 = f32[512,6144]{1,0:T(8,128)} custom-call(s32[2]{0:T(128)} %pad_add_fusion.where, bf16[4,4,128,1024]{3,2,1,0:T(8,128)(2,1)} %bitcast.158, bf16[4,4,128,1024]{3,2,1,0:T(8,128)(2,1)} %collective-permute-done.25.oth_ref), custom_call_target="tpu_custom_call" | custom-call | bytes 25165824 | tf_op jit(solution)/shard_map/pallas_call | solution.py:516
  (304 shorter events, 318.3 us)
Async XLA Ops:
  33.1 57.3 %all-to-all-start = ((bf16[4,128,2048]{2,1,0:T(8,128)(2,1)}), bf16[4,128,2048]{2,1,0:T(8,128)(2,1)}, u32[]{:S(2)}, u32[]{:S(2)}) async-start(bf16[4,128,2048]{2,1,0:T(8,128)(2,1)} %bitcast.164), calls=%async_computation | async-start | bytes 4194304 | tf_op jit(solution)/shard_map/all_to_all | solution.py:380
  38.0 140.5 %all-gather.10.cloned.1.call-start = ((), (), s32[]{:S(2)}) async-start(), calls=%async_computation.9 | async-start | bytes 10485760 | tf_op jit(solution)/shard_map/all_gather | solution.py:922
  42.4 47.1 %collective-permute-start.3 = (bf16[512,1024]{1,0:T(8,128)(2,1)S(1)}, bf16[512,1024]{1,0:T(8,128)(2,1)S(1)}, u32[]{:S(2)}, u32[]{:S(2)}) collective-permute-start(bf16[512,1024]{1,0:T(8,128)(2,1)S(1)} %get-tuple-element.71), channel_id=1, source_target_pairs={{0,2},{1,3},{2,0},{3,1},{4,6},{5,7},{6,4},{7,5},{8,10},{9,11},{10,... | collective-permute-start | bytes 3145736 | tf_op jit(solution)/shard_map/ppermute | solution.py:355
  42.9 47.6 %collective-permute-start.4 = (bf16[512,1024]{1,0:T(8,128)(2,1)S(1)}, bf16[512,1024]{1,0:T(8,128)(2,1)}, u32[]{:S(2)}, u32[]{:S(2)}) collective-permute-start(bf16[512,1024]{1,0:T(8,128)(2,1)S(1)} %get-tuple-element.72), channel_id=1, source_target_pairs={{0,3},{1,2},{2,1},{3,0},{4,7},{5,6},{6,5},{7,4},{8,11},{9,10},{10,... | collective-permute-start | bytes 3145736 | tf_op jit(solution)/shard_map/ppermute | solution.py:355
  90.5 177.5 %all-gather.12.cloned.1.call-start = ((), (), s32[]{:S(2)}) async-start(), calls=%async_computation.10 | async-start | bytes 10485760 | tf_op jit(solution)/shard_map/all_gather | solution.py:926
  150.3 260.2 %reduce-scatter.6.cloned.1.call-start = ((), (), s32[]{:S(2)}) async-start(), calls=%async_computation.12 | async-start | bytes 5242880 | tf_op jit(solution)/shard_map/reduce_scatter | solution.py:951
  306.9 187.3 %reduce-scatter.4.cloned.1.call-start = ((), (), s32[]{:S(2)}) async-start(), calls=%async_computation.11 | async-start | bytes 5242880 | tf_op jit(solution)/shard_map/reduce_scatter | solution.py:951
  379.6 167.0 %all-gather.14.cloned.1.call-start = ((), (), s32[]{:S(2)}) async-start(), calls=%async_computation.13 | async-start | bytes 5242880 | tf_op jit(solution)/shard_map/all_gather | solution.py:954
  497.7 126.5 %reduce-scatter.8.cloned.1.call-start = ((), (), s32[]{:S(2)}) async-start(), calls=%async_computation.14 | async-start | bytes 5242880 | tf_op jit(solution)/shard_map/reduce_scatter | solution.py:951
  523.9 197.2 %all-gather.18.cloned.1.call-start = ((), (), s32[]{:S(2)}) async-start(), calls=%async_computation.16 | async-start | bytes 5242880 | tf_op jit(solution)/shard_map/all_gather | solution.py:954
  588.0 44.2 %collective-permute-start.29 = (bf16[256,2048]{1,0:T(8,128)(2,1)}, bf16[256,2048]{1,0:T(8,128)(2,1)}, u32[]{:S(2)}, u32[]{:S(2)}) collective-permute-start(bf16[256,2048]{1,0:T(8,128)(2,1)} %get-tuple-element.134), channel_id=1, source_target_pairs={{0,2},{1,3},{2,0},{3,1},{4,6},{5,7},{6,4},{7,5},{8,10},{9,11},{10,... | collective-permute-start | bytes 3145736 | tf_op jit(solution)/shard_map/ppermute | solution.py:355
  591.0 47.4 %collective-permute-start.26 = (bf16[256,2048]{1,0:T(8,128)(2,1)S(1)}, bf16[256,2048]{1,0:T(8,128)(2,1)}, u32[]{:S(2)}, u32[]{:S(2)}) collective-permute-start(bf16[256,2048]{1,0:T(8,128)(2,1)S(1)} %get-tuple-element.132), channel_id=1, source_target_pairs={{0,1},{1,0},{2,3},{3,2},{4,5},{5,4},{6,7},{7,6},{8,9},{9,8},{10,11... | collective-permute-start | bytes 3145736 | tf_op jit(solution)/shard_map/ppermute | solution.py:355
  629.8 227.2 %all-gather.16.cloned.1.call-start = ((), (), s32[]{:S(2)}) async-start(), calls=%async_computation.15 | async-start | bytes 5242880 | tf_op jit(solution)/shard_map/all_gather | solution.py:954
  630.1 45.3 %collective-permute-start.31 = (bf16[256,2048]{1,0:T(8,128)(2,1)S(1)}, bf16[256,2048]{1,0:T(8,128)(2,1)}, u32[]{:S(2)}, u32[]{:S(2)}) collective-permute-start(bf16[256,2048]{1,0:T(8,128)(2,1)S(1)} %get-tuple-element.133), channel_id=1, source_target_pairs={{0,2},{1,3},{2,0},{3,1},{4,6},{5,7},{6,4},{7,5},{8,10},{9,11},{10,... | collective-permute-start | bytes 3145736 | tf_op jit(solution)/shard_map/ppermute | solution.py:355
  653.3 38.2 %collective-permute-start.30 = (bf16[256,2048]{1,0:T(8,128)(2,1)}, bf16[256,2048]{1,0:T(8,128)(2,1)}, u32[]{:S(2)}, u32[]{:S(2)}) collective-permute-start(bf16[256,2048]{1,0:T(8,128)(2,1)} %get-tuple-element.131), channel_id=1, source_target_pairs={{0,1},{1,0},{2,3},{3,2},{4,5},{5,4},{6,7},{7,6},{8,9},{9,8},{10,11... | collective-permute-start | bytes 3145736 | tf_op jit(solution)/shard_map/ppermute | solution.py:355
  656.9 66.8 %collective-permute-start.13 = (bf16[256,2048]{1,0:T(8,128)(2,1)}, bf16[256,2048]{1,0:T(8,128)(2,1)}, u32[]{:S(2)}, u32[]{:S(2)}) collective-permute-start(bf16[256,2048]{1,0:T(8,128)(2,1)} %get-tuple-element.138), channel_id=1, source_target_pairs={{0,1},{1,0},{2,3},{3,2},{4,5},{5,4},{6,7},{7,6},{8,9},{9,8},{10,11... | collective-permute-start | bytes 3145736 | tf_op jit(solution)/shard_map/ppermute | solution.py:355
  657.5 64.1 %collective-permute-start.16 = (bf16[256,2048]{1,0:T(8,128)(2,1)}, bf16[256,2048]{1,0:T(8,128)(2,1)}, u32[]{:S(2)}, u32[]{:S(2)}) collective-permute-start(bf16[256,2048]{1,0:T(8,128)(2,1)} %get-tuple-element.140), channel_id=1, source_target_pairs={{0,2},{1,3},{2,0},{3,1},{4,6},{5,7},{6,4},{7,5},{8,10},{9,11},{10,... | collective-permute-start | bytes 3145736 | tf_op jit(solution)/shard_map/ppermute | solution.py:355
  671.9 51.8 %collective-permute-start.15 = (bf16[256,2048]{1,0:T(8,128)(2,1)}, bf16[256,2048]{1,0:T(8,128)(2,1)}, u32[]{:S(2)}, u32[]{:S(2)}) collective-permute-start(bf16[256,2048]{1,0:T(8,128)(2,1)} %add_convert_fusion.7), channel_id=1, source_target_pairs={{0,2},{1,3},{2,0},{3,1},{4,6},{5,7},{6,4},{7,5},{8,10},{9,11},{10,... | collective-permute-start | bytes 3145736 | tf_op jit(solution)/shard_map/ppermute | solution.py:355
  695.5 89.4 %all-to-all-start.5 = ((bf16[4,128,2048]{2,1,0:T(8,128)(2,1)}), bf16[4,128,2048]{2,1,0:T(8,128)(2,1)S(1)}, u32[]{:S(2)}, u32[]{:S(2)}) async-start(bf16[4,128,2048]{2,1,0:T(8,128)(2,1)} %bitcast.162), calls=%async_computation.8 | async-start | bytes 4194304 | tf_op jit(solution)/shard_map/all_to_all | solution.py:413
  721.1 85.8 %collective-permute-start.21 = (bf16[4,4,128,1024]{3,2,1,0:T(8,128)(2,1)}, bf16[4,4,128,1024]{3,2,1,0:T(8,128)(2,1)}, u32[]{:S(2)}, u32[]{:S(2)}) collective-permute-start(bf16[4,4,128,1024]{3,2,1,0:T(8,128)(2,1)} %bitcast.170), channel_id=1, source_target_pairs={{0,16},{16,0},{1,17},{17,1},{2,18},{18,2},{3,19},{19,3},{4,20},{20... | collective-permute-start | bytes 12582920 | tf_op jit(solution)/shard_map/ppermute | solution.py:351
  721.1 99.8 %collective-permute-start.20 = (bf16[1024,2048]{1,0:T(8,128)(2,1)}, bf16[1024,2048]{1,0:T(8,128)(2,1)}, u32[]{:S(2)}, u32[]{:S(2)}) collective-permute-start(bf16[1024,2048]{1,0:T(8,128)(2,1)} %all-gather.14.cloned.1.call-done.own_ref), channel_id=1, source_target_pairs={{0,16},{16,0},{1,17},{17,1},{2,18},{18,2},{3,19},{19,3},{4,20},{20... | collective-permute-start | bytes 12582920 | tf_op jit(solution)/shard_map/ppermute | solution.py:351
  745.8 50.6 %collective-permute-start.24 = (f32[1,1792]{1,0:T(1,128)S(1)}, f32[1,1792]{1,0:T(1,128)S(1)}, u32[]{:S(2)}, u32[]{:S(2)}) collective-permute-start(f32[1,1792]{1,0:T(1,128)S(1)} %add.482), channel_id=1, source_target_pairs={{4,0},{8,12},{5,1},{9,13},{6,2},{10,14},{7,3},{11,15},{20,16},{24,... | collective-permute-start | bytes 21512 | tf_op jit(solution)/shard_map/ppermute | solution.py:443
  786.2 79.3 %all-to-all-start.3 = ((bf16[4,128,2048]{2,1,0:T(8,128)(2,1)}), bf16[4,128,2048]{2,1,0:T(8,128)(2,1)}, u32[]{:S(2)}, u32[]{:S(2)}) async-start(bf16[4,128,2048]{2,1,0:T(8,128)(2,1)} %bitcast.163), calls=%async_computation.5 | async-start | bytes 4194304 | tf_op jit(solution)/shard_map/all_to_all | solution.py:413
  796.4 60.7 %collective-permute-start.32 = (bf16[2,128,2048]{2,1,0:T(8,128)(2,1)}, bf16[2,128,2048]{2,1,0:T(8,128)(2,1)S(1)}, u32[]{:S(2)}, u32[]{:S(2)}) collective-permute-start(bf16[2,128,2048]{2,1,0:T(8,128)(2,1)} %dynamic-slice_bitcast_fusion), channel_id=1, source_target_pairs={{0,16},{16,0},{1,17},{17,1},{2,18},{18,2},{3,19},{19,3},{4,20},{20... | collective-permute-start | bytes 3145736 | tf_op jit(solution)/shard_map/ppermute | solution.py:351
  (65 other events, 1563.3 us)
Sparse Core Ops, SparseCore 0:
  90.6 87.8 all-gather.9
  180.3 87.5 all-gather.11
  307.0 76.7 reduce-scatter.5
  386.6 77.2 reduce-scatter.3
  465.3 81.2 all-gather.13
  548.8 75.2 reduce-scatter.7
  625.8 95.2 all-gather.17
  722.7 134.2 all-gather.15

commit v4 on v3

--- a/solution.py
+++ b/solution.py
@@ -374,10 +374,20 @@
     return swap_dp(pick(rows.reshape(micro, 2, blk, width), 1 - core, 1))
 
 
-def deal_out(rows, received, core, blk):
+def line_up(rows, received, core, blk):
     micro, _, width = rows.shape
-    lined = by_core(core, pick(rows.reshape(micro, 2, blk, width), core, 1), received, 0).reshape(4, blk, width)
-    return lax.all_to_all(lined, "ctx", 0, 0, tiled=True).reshape(4 * blk, width)
+    return by_core(core, pick(rows.reshape(micro, 2, blk, width), core, 1), received, 0).reshape(4, blk, width)
+
+
+def deal_out(lined):
+    return lax.all_to_all(lined, "ctx", 0, 0, tiled=True).reshape(-1, lined.shape[2])
+
+
+def normed_rows(rows):
+    inputs = rows.astype(WIDE)
+    centered = inputs - jnp.mean(inputs, axis=-1, keepdims=True)
+    inv_std = lax.rsqrt(jnp.mean(centered * centered, axis=-1, keepdims=True) + EPS)
+    return inputs, centered * inv_std, inv_std
 
 
 def placed(pieces, shard, size, *gates):
@@ -496,32 +506,32 @@
     )
 
 
-def cols_out(core, shard, own, oth, parts, held):
-    lines, columns, rows, width = own.shape
+def cols_half(core, shard, half, side, parts, held, earlier=()):
+    lines, columns, rows, width = half.shape
     width = width // held
 
-    def kernel(where, own_ref, oth_ref, out_ref):
-        side = pl.program_id(2)
-
-        @pl.when(side == 0)
-        def _():
-            out_ref[...] = own_ref[...].reshape(lines * rows, width).astype(WIDE)
-
-        @pl.when(side == 1)
-        def _():
-            out_ref[...] = oth_ref[...].reshape(lines * rows, width).astype(WIDE)
-
-    source = pl.BlockSpec((lines, 1, rows, width), lambda b, t, s, where: (0, b, 0, t))
-    target = pl.BlockSpec((lines * rows, width), lambda b, t, s, where: (0, t * 8 + 2 * b + (where[0] ^ s)))
+    def kernel(where, half_ref, *rest):
+        rest[-1][...] = half_ref[...].reshape(lines * rows, width).astype(WIDE)
+
     return pl.pallas_call(
         kernel,
         grid_spec=pltpu.PrefetchScalarGridSpec(
-            num_scalar_prefetch=1, grid=(columns, parts, 2), in_specs=[source, source], out_specs=target
+            num_scalar_prefetch=1,
+            grid=(columns, parts),
+            in_specs=[pl.BlockSpec((lines, 1, rows, width), lambda b, t, where: (0, b, 0, t))]
+            + [pl.BlockSpec(memory_space=pl.ANY)] * len(earlier),
+            out_specs=pl.BlockSpec((lines * rows, width), lambda b, t, where: (0, t * 8 + 2 * b + (where[0] ^ side))),
         ),
         out_shape=jax.ShapeDtypeStruct((lines * rows, 2 * columns * parts * width), WIDE),
-        compiler_params=pltpu.CompilerParams(dimension_semantics=("arbitrary",) * 3),
-        cost_estimate=pl.CostEstimate(flops=0, transcendentals=0, bytes_accessed=12 * own.size),
-    )(jnp.stack([core, shard]).astype(jnp.int32), own, oth)
+        input_output_aliases={2: 0} if earlier else {},
+        compiler_params=pltpu.CompilerParams(dimension_semantics=("arbitrary",) * 2),
+        cost_estimate=pl.CostEstimate(flops=0, transcendentals=0, bytes_accessed=6 * half.size),
+    )(jnp.stack([core, shard]).astype(jnp.int32), half, *earlier)
+
+
+def cols_out(core, shard, own, oth, parts, held):
+    first = cols_half(core, shard, own, 0, parts, held)
+    return cols_half(core, shard, oth, 1, parts, held, (first,))
 
 
 GELU_C = 0.7978845608028654
@@ -846,7 +856,6 @@
 
 def flipped_out(core, shard, own, oth, start):
     lines, columns, rows, width = own.shape
-    width = width // 4
 
     def kernel(where, own_ref, oth_ref, out_ref):
         side = pl.program_id(1)
@@ -889,6 +898,11 @@
     units = w_down.shape[0] // 2
     head_cols = w_out.shape[0] // 2
 
+    h_received = for_other(tokens[0], core, blk)
+    norm = lax.all_gather(jnp.stack([ln_gain, ln_bias]), "fsdp", axis=1, tiled=True).astype(WIDE)
+    gain, shift = norm[0], norm[1]
+    _, hidden_home, _ = normed_rows(line_up(tokens[0], h_received, core, blk))
+    hidden_home = (hidden_home * gain + shift).astype(LOW)
     meta = jnp.concatenate([deal[0].reshape(-1), lengths[0] // 64, lengths[0] % 64]).astype(LOW)
     theirs = swap_dp(meta)
     meta = jnp.where(place // micro == core, meta, theirs)
@@ -897,32 +911,27 @@
         lax.dynamic_slice_in_dim(meta, turn * blocks, blocks), lax.dynamic_slice_in_dim(meta, micro * blocks + turn, 1),
         lax.dynamic_slice_in_dim(meta, micro * (blocks + 1) + turn, 1),
     ])
-    size = 2 * ln_gain.shape[0] + b_qkv.shape[0] + b_out.shape[0] + b_up.shape[0] + b_down.shape[0] + meta.shape[0]
-    small = jnp.concatenate([ln_gain, ln_bias, b_qkv, b_out, b_up, b_down, meta, jnp.zeros((-size % 512,), LOW)])
-
-    small = lax.all_gather(small, "fsdp", axis=0, tiled=False)
+    size = b_qkv.shape[0] + b_out.shape[0] + b_up.shape[0] + b_down.shape[0] + meta.shape[0]
+    small = jnp.concatenate([b_qkv, b_out, b_up, b_down, meta, jnp.zeros((-size % 512,), LOW)])
+
+    up_sent = columns_sent([after(piece, hidden_home) for piece in columns_cut(w_up, 1, core, shard)])
+    waited = [piece for bits, _, piece in up_sent if bits]
+    small = lax.all_gather(after(small, *waited), "fsdp", axis=0, tiled=False)
     bounds = [0]
-    for piece in (ln_gain, ln_bias, b_qkv, b_out, b_up, b_down, meta):
+    for piece in (b_qkv, b_out, b_up, b_down, meta):
         bounds.append(bounds[-1] + piece.shape[0])
-    gain, shift, bias_qkv, bias_out, bias_up, bias_down, meta = (small[:, a:b] for a, b in zip(bounds[:-1], bounds[1:]))
-    gain, shift = gain.astype(WIDE).reshape(-1), shift.astype(WIDE).reshape(-1)
+    bias_qkv, bias_out, bias_up, bias_down, meta = (small[:, a:b] for a, b in zip(bounds[:-1], bounds[1:]))
     own_blocks = lax.dynamic_slice_in_dim(deal[0], 2 * place, 2, axis=1)
     local_pos = (own_blocks[:, :, None] * blk + jnp.arange(blk, dtype=jnp.int32)).reshape(micro, rows)
     valid = (local_pos < lengths[0][:, None])[:, :, None]
-    inputs = tokens[0].astype(WIDE)
-    centered = inputs - jnp.mean(inputs, axis=-1, keepdims=True)
-    inv_std = lax.rsqrt(jnp.mean(centered * centered, axis=-1, keepdims=True) + EPS)
-    hidden_home = (centered * inv_std * gain + shift).astype(LOW)
     gout_home = jnp.where(valid, cotangent[0], jnp.zeros((), LOW))
 
-    h_received = for_other(after(hidden_home, small), core, blk)
-    up_sent = columns_sent([after(piece, small) for piece in columns_cut(w_up, 1, core, shard)])
-    g_received = for_other(after(gout_home, h_received), core, blk)
-    h_dealt = deal_out(hidden_home, h_received, core, blk)
+    g_received = for_other(after(gout_home, hidden_home), core, blk)
+    h_dealt = deal_out(hidden_home)
     hidden_own = lax.all_gather(after(h_dealt, *[piece for _, _, piece in up_sent]), "fsdp", axis=0, tiled=True)
     hidden = (hidden_own, swap_dp(hidden_own))
     up_w = placed(up_sent, shard, w_up.shape[0])
-    g_dealt = deal_out(gout_home, after(g_received, h_dealt), core, blk)
+    g_dealt = deal_out(line_up(gout_home, after(g_received, h_dealt), core, blk))
     gout_own = lax.all_gather(g_dealt, "fsdp", axis=0, tiled=True)
 
     bias_ends = (bias_out.astype(WIDE) + bias_down.astype(WIDE)).reshape(-1)
@@ -982,7 +991,8 @@
     mine = scatter(jnp.concatenate([g_qkv, g_out], axis=3))[0]
     qkv_cols = g_qkv.shape[3]
     x_qkv = lax.all_to_all(mine[:, :, :qkv_cols], "fsdp", 0, 0, tiled=True)
-    t_mix = gather(jnp.concatenate([x_qkv, mine[:, :, qkv_cols:]], axis=2)[None])
+    t_qkv = gather(x_qkv[None])
+    t_out = gather(after(mine[:, :, qkv_cols:], x_qkv)[None])
     sums_tp = line_sum(jnp.concatenate([s_up, s_q, s_k, s_v], axis=1), place)
     tails = lax.all_gather(sums_tp, ("fsdp", "dp"), axis=0, tiled=True)
     b_oth = backward_call(dups[1], after(turned[1], g_qkv, x_up), up_w, qkv_w)
@@ -997,15 +1007,12 @@
     o_down = rows_out(core, shard, t_down, after(swap_dp(t_down), o_up))
     d_hidden = after(d_hidden, o_down).astype(WIDE)
     mixed = to_home(mixed, core, place, blk)
-    t_mix = after(t_mix, o_down)
-    t_mix = (t_mix, swap_dp(t_mix))
-    o_qkv = cols_out(core, shard, *t_mix, 3, 4)
-    o_out = flipped_out(core, shard, *t_mix, 3)
-
-    inputs = after(tokens[0], f_total).astype(WIDE)
-    centered = inputs - jnp.mean(inputs, axis=-1, keepdims=True)
-    inv_std = lax.rsqrt(jnp.mean(centered * centered, axis=-1, keepdims=True) + EPS)
-    normed = centered * inv_std
+    t_qkv = after(t_qkv, o_down)
+    o_qkv = cols_out(core, shard, t_qkv, swap_dp(t_qkv), 3, 3)
+    t_out = after(t_out, o_qkv)
+    o_out = flipped_out(core, shard, t_out, swap_dp(t_out), 0)
+
+    inputs, normed, inv_std = normed_rows(after(tokens[0], f_total))
     d_norm = d_hidden * gain
     d_inputs = inv_std * (
         d_norm

time: 938 us -> 901 us (0.961)
  waiting for transfers between devices: 299 us -> 254 us
    all_gather x1, waiting for transfers between devices: 47.2 us -> 26.1 us  [plane_body(): gout_own = lax.all_gather(g_dealt, 'fsdp', axis=0, tiled=True)]
    all_gather x3 -> x4, waiting for transfers between devices: 43.8 us -> 34.2 us  [gather(): return lax.all_gather(piece, 'ctx', axis=0, tiled=True)]
    ppermute x13 -> x14, waiting for transfers between devices: 21 us -> 23.1 us  [swap_dp(): return lax.ppermute(value, 'dp', SWAP)]
    pallas_call x2 -> x4, Pallas kernels: 33.2 us -> 31.7 us  [cols_half(): pl.pallas_call(kernel, grid_spec=pltpu.PrefetchScalarGridSpec(num_scalar_...]
  transfers between devices with their start and end apart: 52 -> 54, of which waited for: 26 -> 23; matrix products, arithmetic and copies ran while one was open for 9% -> 9% of each run, Pallas kernels for 35% -> 39%
where the time goes in v4:
time: 901 us; the launch traced here: 892 us
  Pallas kernels  378 us (42%)
  waiting for transfers between devices  254 us (28%)
  blocking collectives  80.4 us (9%)
  starting transfers between devices  60.2 us (7%)
  other arithmetic  54.8 us (6%)
  local copies, waits for them, and re-layouts  50.4 us (6%)
  between operations  14.9 us (2%)
    pallas_call x10, Pallas kernels, row_call(): pl.pallas_call(body, grid=(count // tile,), in_specs=[rows_spec(a.shape[1...  167 us
    ppermute x20, waiting for transfers between devices, swap_shard(): return lax.ppermute(value, 'fsdp', [(i, i ^ bits) for i in range(4)])  100 us
    pallas_call x4, Pallas kernels, grad_call(): pl.pallas_call(body, grid=(2 * steps,), in_specs=specs, out_specs=[fixed(...  86.8 us
    pallas_call x1, Pallas kernels, attention_call(): pl.pallas_call(kernel, grid_spec=pltpu.PrefetchScalarGridSpec(num_scalar_...  70.5 us
    all_to_all x1, blocking collectives, deal_out(): lax.all_to_all(lined, 'ctx', 0, 0, tiled=True).reshape(-1, lined.shape[2])  53.3 us
    all_gather x4, waiting for transfers between devices, gather(): return lax.all_gather(piece, 'ctx', axis=0, tiled=True)  34.2 us
    pallas_call x4, Pallas kernels, cols_half(): pl.pallas_call(kernel, grid_spec=pltpu.PrefetchScalarGridSpec(num_scalar_...  31.7 us
    all_gather x1, waiting for transfers between devices, plane_body(): lax.all_gather(after(h_dealt, *[piece for _, _, piece in up_sent]), 'fsdp...  28 us
  transfers between devices with their start and end apart: 54, of which 23 were waited for; matrix products, arithmetic and copies ran while one was open for 9% of the time, Pallas kernels for 39%

profile of v4, /device:TPU:0, one launch (start us, length us, event | category | flops | bytes accessed | tf_op | source)
XLA Modules:
  0.0 892.5 jit_solution(11547987636461217008)
XLA Ops:
  36.7 42.3 %collective-permute-done.2 = bf16[512,1024]{1,0:T(8,128)(2,1)S(1)} collective-permute-done((bf16[512,1024]{1,0:T(8,128)(2,1)S(1)}, bf16[512,1024]{1,0:T(8,128)(2,1)S(1)}, u32[]{:S(2)}, u32[]{:S(2)}) %collective-permute-start.2) | collective-permute-done | bytes 1048608 | tf_op jit(solution)/shard_map/ppermute | solution.py:355
  87.4 53.3 %all_to_all.30 = bf16[4,128,2048]{2,1,0:T(8,128)(2,1)} all-to-all(bf16[4,128,2048]{2,1,0:T(8,128)(2,1)S(1)} %bitcast.167), channel_id=1, replica_groups=mesh['dp'=2,'ctx'=4,'fsdp'=4] {'ctx'}, dimensions={0} | all-to-all | bytes 4194304 | tf_op jit(solution)/shard_map/all_to_all | solution.py:383
  140.9 28.0 %all-gather.12.cloned.1.call-done.rows_ref.refs_0_ = bf16[2048,2048]{1,0:T(8,128)(2,1)} async-done(((bf16[512,2048]{1,0:T(8,128)(2,1)}), bf16[2048,2048]{1,0:T(8,128)(2,1)}) %all-gather.12.cloned.1.call-update) | async-done | bytes 8388624 | tf_op jit(solution)/shard_map/all_gather | solution.py:931
  196.5 18.0 %shard_map.229 = (bf16[2048,1024]{1,0:T(8,128)(2,1)}, bf16[2048,1024]{1,0:T(8,128)(2,1)}) custom-call(bf16[2048,2048]{1,0:T(8,128)(2,1)} %all-gather.12.cloned.1.call-done.rows_ref.refs_0_, bf16[2048,1024]{1,0:T(8,128)(2,1)} %constant_dynamic-update-slice_fusion.4.weight_ref.refs_4_.refs_5_, f32[1,1024]{1,0:T(1,128)} %bitcast.205), custom_call_target="tpu_custom_call" | custom-call | flops 15461881856 | bytes 20975616 | tf_op jit(solution)/shard_map/pallas_call | solution.py:561
  214.5 18.0 %shard_map.230 = (bf16[2048,1024]{1,0:T(8,128)(2,1)}, bf16[2048,1024]{1,0:T(8,128)(2,1)}) custom-call(bf16[2048,2048]{1,0:T(8,128)(2,1)} %collective-permute-done.6.rows_ref.refs_1_, bf16[2048,1024]{1,0:T(8,128)(2,1)} %constant_dynamic-update-slice_fusion.4.weight_ref.refs_4_.refs_5_, f32[1,1024]{1,0:T(1,128)} %bitcast.206), custom_call_target="tpu_custom_call" | custom-call | flops 15461881856 | bytes 20975616 | tf_op jit(solution)/shard_map/pallas_call | solution.py:561
  232.5 26.1 %all-gather.14.cloned.1.call-done.refs_2_.rows_ref = bf16[2048,2048]{1,0:T(8,128)(2,1)} async-done(((bf16[512,2048]{1,0:T(8,128)(2,1)}), bf16[2048,2048]{1,0:T(8,128)(2,1)}) %all-gather.14.cloned.1.call-update) | async-done | bytes 8388624 | tf_op jit(solution)/shard_map/all_gather | solution.py:935
  258.7 13.5 %collective-permute-done.7.refs_3_.rows_ref = bf16[2048,2048]{1,0:T(8,128)(2,1)} collective-permute-done((bf16[2048,2048]{1,0:T(8,128)(2,1)}, bf16[2048,2048]{1,0:T(8,128)(2,1)}, u32[]{:S(2)}, u32[]{:S(2)}) %collective-permute-start.7) | collective-permute-done | bytes 8388640 | tf_op jit(solution)/shard_map/ppermute | solution.py:351
  272.2 25.4 %shard_map.231 = bf16[1024,2048]{1,0:T(8,128)(2,1)} custom-call(bf16[2048,1024]{1,0:T(8,128)(2,1)} %get-tuple-element.111.refs_0_, bf16[2048,1024]{1,0:T(8,128)(2,1)} %get-tuple-element.109.refs_1_.refs_0_, bf16[2048,2048]{1,0:T(8,128)(2,1)} %all-gather.14.cloned.1.call-done.refs_2_.rows_ref, bf16[2048,2048]{1,0:T(8,128)(2,1)} %collective-permute-done.7.refs_3_.rows_ref), custom_call_target="tpu_custom_call" | custom-call | flops 30923763712 | bytes 25165824 | tf_op jit(solution)/shard_map/pallas_call | solution.py:719
  309.9 16.9 %shard_map.232 = (bf16[2048,1024]{1,0:T(8,128)(2,1)}, bf16[2048,256]{1,0:T(8,128)(2,1)}) custom-call(bf16[2048,2048]{1,0:T(8,128)(2,1)} %all-gather.14.cloned.1.call-done.refs_2_.rows_ref, bf16[2048,1024]{1,0:T(8,128)(2,1)} %get-tuple-element.82.slope_ref, bf16[1024,2048]{1,0:T(8,128)(2,1)} %constant_dynamic-slice_fusion.28.down_ref.refs_2_.refs_3_, ...), custom_call_target="tpu_custom_call" | custom-call | flops 19327352832 | bytes 23068672 | tf_op jit(solution)/shard_map/pallas_call | solution.py:561
  326.7 16.8 %shard_map.233 = (bf16[2048,1024]{1,0:T(8,128)(2,1)}, bf16[2048,256]{1,0:T(8,128)(2,1)}) custom-call(bf16[2048,2048]{1,0:T(8,128)(2,1)} %collective-permute-done.7.refs_3_.rows_ref, bf16[2048,1024]{1,0:T(8,128)(2,1)} %get-tuple-element.84.slope_ref, bf16[1024,2048]{1,0:T(8,128)(2,1)} %constant_dynamic-slice_fusion.28.down_ref.refs_2_.refs_3_, ...), custom_call_target="tpu_custom_call" | custom-call | flops 19327352832 | bytes 23068672 | tf_op jit(solution)/shard_map/pallas_call | solution.py:561
  343.7 26.8 %shard_map.234 = (bf16[4,4,128,1024]{3,2,1,0:T(8,128)(2,1)}, f32[1,1024]{1,0:T(1,128)}) custom-call(bf16[2048,2048]{1,0:T(8,128)(2,1)} %all-gather.12.cloned.1.call-done.rows_ref.refs_0_, bf16[2048,2048]{1,0:T(8,128)(2,1)} %collective-permute-done.6.rows_ref.refs_1_, bf16[2048,1024]{1,0:T(8,128)(2,1)} %get-tuple-element.110.refs_2_.refs_0_, ...), custom_call_target="tpu_custom_call" | custom-call | flops 30923763712 | bytes 25165824 | tf_op jit(solution)/shard_map/pallas_call | solution.py:719
  379.5 10.8 %shard_map.236 = bf16[2048,768]{1,0:T(8,128)(2,1)} custom-call(bf16[2048,2048]{1,0:T(8,128)(2,1)} %collective-permute-done.6.rows_ref.refs_1_, bf16[2048,768]{1,0:T(8,128)(2,1)} %copy-done.10, f32[1,768]{1,0:T(1,128)} %convert.16.bias_ref), custom_call_target="tpu_custom_call" | custom-call | flops 11596411904 | bytes 14683136 | tf_op jit(solution)/shard_map/pallas_call | solution.py:561
  401.1 70.5 %shard_map.237 = (bf16[4,512,256]{2,1,0:T(8,128)(2,1)}, bf16[4,512,256]{2,1,0:T(8,128)(2,1)}, bf16[4,512,256]{2,1,0:T(8,128)(2,1)}, bf16[4,512,256]{2,1,0:T(8,12...) custom-call(s32[4,4]{1,0:T(4,128)} %bitcast.209, ...), custom_call_target="tpu_custom_call" | custom-call | flops 69578473472 | bytes 16777216 | tf_op jit(solution)/shard_map/pallas_call | solution.py:834
  471.6 13.2 %shard_map.238 = bf16[4,4,128,256]{3,2,1,0:T(8,128)(2,1)} custom-call(bf16[2048,256]{1,0:T(8,128)(2,1)} %bitcast.219, bf16[2048,256]{1,0:T(8,128)(2,1)} %bitcast.229, bf16[2048,2048]{1,0:T(8,128)(2,1)} %all-gather.14.cloned.1.call-done.refs_2_.rows_ref, bf16[2048,2048]{1,0:T(8,128)(2,1)} %collective-permute-done.7.refs_3_.rows_ref), custom_call_target="tpu_custom_call" | custom-call | flops 7730940928 | bytes 18874368 | tf_op jit(solution)/shard_map/pallas_call | solution.py:719
  488.4 21.4 %shard_map.239 = (bf16[4,4,128,768]{3,2,1,0:T(8,128)(2,1)}, f32[1,256]{1,0:T(1,128)}, f32[1,256]{1,0:T(1,128)}, f32[1,256]{1,0:T(1,128)}) custom-call(bf16[2048,2048]{1,0:T(8,128)(2,1)} %all-gather.12.cloned.1.call-done.rows_ref.refs_0_, bf16[2048,2048]{1,0:T(8,128)(2,1)} %collective-permute-done.6.rows_ref.refs_1_, bf16[2048,256]{1,0:T(8,128)(2,1)} %bitcast.223, ...), custom_call_target="tpu_custom_call" | custom-call | flops 23192823808 | bytes 23068672 | tf_op jit(solution)/shard_map/pallas_call | solution.py:719
  514.8 21.6 %shard_map.240 = bf16[2048,2048]{1,0:T(8,128)(2,1)} custom-call(bf16[2048,1024]{1,0:T(8,128)(2,1)} %get-tuple-element.85.refs_3_.refs_0_, bf16[2048,256]{1,0:T(8,128)(2,1)} %bitcast.232, bf16[2048,256]{1,0:T(8,128)(2,1)} %bitcast.234, bf16[2048,256]{1,0:T(8,128)(2,1)} %bitcast.236, ...), custom_call_target="tpu_custom_call" | custom-call | flops 27058294784 | bytes 23068672 | tf_op jit(solution)/shard_map/pallas_call | solution.py:561
  537.4 15.8 %shard_map.241 = bf16[2048,2048]{1,0:T(8,128)(2,1)} custom-call(bf16[2048,1024]{1,0:T(8,128)(2,1)} %get-tuple-element.109.refs_1_.refs_0_, bf16[2048,256]{1,0:T(8,128)(2,1)} %bitcast.230, bf16[1024,2048]{1,0:T(8,128)(2,1)} %constant_dynamic-slice_fusion.28.down_ref.refs_2_.refs_3_, bf16[256,2048]{1,0:T(8,128)(2,1)} %constant_dynamic-slice_fusion.27.out_w_ref.refs_3_.refs_4_), custom_call_target="tpu_custom_call" | custom-call | flops 19327352832 | bytes 18874368 | tf_op jit(solution)/shard_map/pallas_call | solution.py:561
  553.2 21.9 %shard_map.242 = bf16[2048,2048]{1,0:T(8,128)(2,1)} custom-call(bf16[2048,1024]{1,0:T(8,128)(2,1)} %get-tuple-element.110.refs_2_.refs_0_, bf16[2048,256]{1,0:T(8,128)(2,1)} %bitcast.224, bf16[2048,256]{1,0:T(8,128)(2,1)} %bitcast.226, bf16[2048,256]{1,0:T(8,128)(2,1)} %bitcast.228, bf16[2048,2048]{1,0:T(8,128)(2,1)} %collective-permute-done.11.refs_4_, ...), custom_call_target="tpu_custom_call" | custom-call | flops 27058294784 | bytes 31457280 | tf_op jit(solution)/shard_map/pallas_call | solution.py:561
  581.3 16.5 %shard_map.243 = bf16[2048,2048]{1,0:T(8,128)(2,1)} custom-call(bf16[2048,1024]{1,0:T(8,128)(2,1)} %get-tuple-element.111.refs_0_, bf16[2048,256]{1,0:T(8,128)(2,1)} %bitcast.220, bf16[2048,2048]{1,0:T(8,128)(2,1)} %collective-permute-done.12.refs_2_, bf16[1024,2048]{1,0:T(8,128)(2,1)} %constant_dynamic-slice_fusion.28.down_ref.refs_2_.refs_3_, ...), custom_call_target="tpu_custom_call" | custom-call | flops 19327352832 | bytes 27262976 | tf_op jit(solution)/shard_map/pallas_call | solution.py:561
  615.7 12.1 %collective-permute-done.27 = bf16[256,2048]{1,0:T(8,128)(2,1)} collective-permute-done((bf16[256,2048]{1,0:T(8,128)(2,1)S(1)}, bf16[256,2048]{1,0:T(8,128)(2,1)}, u32[]{:S(2)}, u32[]{:S(2)}) %collective-permute-start.27) | collective-permute-done | bytes 1048608 | tf_op jit(solution)/shard_map/ppermute | solution.py:355
  656.8 16.0 %collective-permute-done.31 = bf16[256,2048]{1,0:T(8,128)(2,1)} collective-permute-done((bf16[256,2048]{1,0:T(8,128)(2,1)}, bf16[256,2048]{1,0:T(8,128)(2,1)}, u32[]{:S(2)}, u32[]{:S(2)}) %collective-permute-start.31) | collective-permute-done | bytes 1048608 | tf_op jit(solution)/shard_map/ppermute | solution.py:355
  686.9 27.3 %all-gather.20.cloned.1.call-done = bf16[16,128,1024]{2,1,0:T(8,128)(2,1)} async-done(((bf16[4,128,1024]{2,1,0:T(8,128)(2,1)}), bf16[16,128,1024]{2,1,0:T(8,128)(2,1)}) %all-gather.20.cloned.1.call-update) | async-done | bytes 4194320 | tf_op jit(solution)/shard_map/all_gather | solution.py:963
  750.3 22.0 %all-to-all-done.5 = bf16[4,128,2048]{2,1,0:T(8,128)(2,1)S(1)} async-done(((bf16[4,128,2048]{2,1,0:T(8,128)(2,1)}), bf16[4,128,2048]{2,1,0:T(8,128)(2,1)S(1)}, u32[]{:S(2)}, u32[]{:S(2)}) %all-to-all-start.5) | async-done | bytes 2097184 | tf_op jit(solution)/shard_map/all_to_all | solution.py:423
  804.4 14.0 %shard_map.246 = f32[2048,2048]{1,0:T(8,128)} custom-call(s32[2]{0:T(128)} %pad_add_fusion.where, bf16[1024,2048]{1,0:T(8,128)(2,1)} %all-gather.16.cloned.1.call-done.own_ref, bf16[1024,2048]{1,0:T(8,128)(2,1)} %collective-permute-done.20.oth_ref), custom_call_target="tpu_custom_call" | custom-call | bytes 25165824 | tf_op jit(solution)/shard_map/pallas_call | solution.py:488
  (305 shorter events, 309.3 us)
Async XLA Ops:
  25.4 55.4 %all-to-all-start = ((bf16[4,128,2048]{2,1,0:T(8,128)(2,1)}), bf16[4,128,2048]{2,1,0:T(8,128)(2,1)}, u32[]{:S(2)}, u32[]{:S(2)}) async-start(bf16[4,128,2048]{2,1,0:T(8,128)(2,1)} %fusion.18), calls=%async_computation | async-start | bytes 4194304 | tf_op jit(solution)/shard_map/all_to_all | solution.py:383
  30.3 138.6 %all-gather.12.cloned.1.call-start = ((), (), s32[]{:S(2)}) async-start(), calls=%async_computation.9 | async-start | bytes 10485760 | tf_op jit(solution)/shard_map/all_gather | solution.py:931
  33.1 45.8 %collective-permute-start.2 = (bf16[512,1024]{1,0:T(8,128)(2,1)S(1)}, bf16[512,1024]{1,0:T(8,128)(2,1)S(1)}, u32[]{:S(2)}, u32[]{:S(2)}) collective-permute-start(bf16[512,1024]{1,0:T(8,128)(2,1)S(1)} %get-tuple-element.72), channel_id=1, source_target_pairs={{0,2},{1,3},{2,0},{3,1},{4,6},{5,7},{6,4},{7,5},{8,10},{9,11},{10,... | collective-permute-start | bytes 3145736 | tf_op jit(solution)/shard_map/ppermute | solution.py:355
  34.7 44.3 %collective-permute-start.3 = (bf16[512,1024]{1,0:T(8,128)(2,1)S(1)}, bf16[512,1024]{1,0:T(8,128)(2,1)S(1)}, u32[]{:S(2)}, u32[]{:S(2)}) collective-permute-start(bf16[512,1024]{1,0:T(8,128)(2,1)S(1)} %get-tuple-element.73), channel_id=1, source_target_pairs={{0,3},{1,2},{2,1},{3,0},{4,7},{5,6},{6,5},{7,4},{8,11},{9,10},{10,... | collective-permute-start | bytes 3145736 | tf_op jit(solution)/shard_map/ppermute | solution.py:355
  36.1 44.7 %collective-permute-start.1 = (bf16[512,1024]{1,0:T(8,128)(2,1)S(1)}, bf16[512,1024]{1,0:T(8,128)(2,1)}, u32[]{:S(2)}, u32[]{:S(2)}) collective-permute-start(bf16[512,1024]{1,0:T(8,128)(2,1)S(1)} %get-tuple-element.71), channel_id=1, source_target_pairs={{0,1},{1,0},{2,3},{3,2},{4,5},{5,4},{6,7},{7,6},{8,9},{9,8},{10,11... | collective-permute-start | bytes 3145736 | tf_op jit(solution)/shard_map/ppermute | solution.py:355
  80.9 177.8 %all-gather.14.cloned.1.call-start = ((), (), s32[]{:S(2)}) async-start(), calls=%async_computation.10 | async-start | bytes 10485760 | tf_op jit(solution)/shard_map/all_gather | solution.py:935
  140.8 260.3 %reduce-scatter.6.cloned.1.call-start = ((), (), s32[]{:S(2)}) async-start(), calls=%async_computation.12 | async-start | bytes 5242880 | tf_op jit(solution)/shard_map/reduce_scatter | solution.py:960
  168.9 45.6 %collective-permute-start.6 = (bf16[2048,2048]{1,0:T(8,128)(2,1)}, bf16[2048,2048]{1,0:T(8,128)(2,1)}, u32[]{:S(2)}, u32[]{:S(2)}) collective-permute-start(bf16[2048,2048]{1,0:T(8,128)(2,1)} %all-gather.12.cloned.1.call-done.rows_ref.refs_0_), channel_id=1, source_target_pairs={{0,16},{16,0},{1,17},{17,1},{2,18},{18,2},{3,19},{19,3},{4,20},{20... | collective-permute-start | bytes 25165832 | tf_op jit(solution)/shard_map/ppermute | solution.py:351
  297.6 187.2 %reduce-scatter.4.cloned.1.call-start = ((), (), s32[]{:S(2)}) async-start(), calls=%async_computation.11 | async-start | bytes 5242880 | tf_op jit(solution)/shard_map/reduce_scatter | solution.py:960
  370.5 166.8 %all-gather.16.cloned.1.call-start = ((), (), s32[]{:S(2)}) async-start(), calls=%async_computation.13 | async-start | bytes 5242880 | tf_op jit(solution)/shard_map/all_gather | solution.py:963
  488.3 152.1 %reduce-scatter.8.cloned.1.call-start = ((), (), s32[]{:S(2)}) async-start(), calls=%async_computation.14 | async-start | bytes 5242880 | tf_op jit(solution)/shard_map/reduce_scatter | solution.py:960
  514.3 199.9 %all-gather.20.cloned.1.call-start = ((), (), s32[]{:S(2)}) async-start(), calls=%async_computation.16 | async-start | bytes 5242880 | tf_op jit(solution)/shard_map/all_gather | solution.py:963
  580.8 47.1 %collective-permute-start.27 = (bf16[256,2048]{1,0:T(8,128)(2,1)S(1)}, bf16[256,2048]{1,0:T(8,128)(2,1)}, u32[]{:S(2)}, u32[]{:S(2)}) collective-permute-start(bf16[256,2048]{1,0:T(8,128)(2,1)S(1)} %get-tuple-element.136), channel_id=1, source_target_pairs={{0,1},{1,0},{2,3},{3,2},{4,5},{5,4},{6,7},{7,6},{8,9},{9,8},{10,11... | collective-permute-start | bytes 3145736 | tf_op jit(solution)/shard_map/ppermute | solution.py:355
  608.4 48.4 %collective-permute-start.32 = (bf16[256,2048]{1,0:T(8,128)(2,1)S(1)}, bf16[256,2048]{1,0:T(8,128)(2,1)}, u32[]{:S(2)}, u32[]{:S(2)}) collective-permute-start(bf16[256,2048]{1,0:T(8,128)(2,1)S(1)} %get-tuple-element.137), channel_id=1, source_target_pairs={{0,2},{1,3},{2,0},{3,1},{4,6},{5,7},{6,4},{7,5},{8,10},{9,11},{10,... | collective-permute-start | bytes 3145736 | tf_op jit(solution)/shard_map/ppermute | solution.py:355
  646.1 70.5 %collective-permute-start.13 = (bf16[256,2048]{1,0:T(8,128)(2,1)}, bf16[256,2048]{1,0:T(8,128)(2,1)}, u32[]{:S(2)}, u32[]{:S(2)}) collective-permute-start(bf16[256,2048]{1,0:T(8,128)(2,1)} %get-tuple-element.142), channel_id=1, source_target_pairs={{0,1},{1,0},{2,3},{3,2},{4,5},{5,4},{6,7},{7,6},{8,9},{9,8},{10,11... | collective-permute-start | bytes 3145736 | tf_op jit(solution)/shard_map/ppermute | solution.py:355
  648.1 66.6 %collective-permute-start.16 = (bf16[256,2048]{1,0:T(8,128)(2,1)}, bf16[256,2048]{1,0:T(8,128)(2,1)}, u32[]{:S(2)}, u32[]{:S(2)}) collective-permute-start(bf16[256,2048]{1,0:T(8,128)(2,1)} %get-tuple-element.144), channel_id=1, source_target_pairs={{0,2},{1,3},{2,0},{3,1},{4,6},{5,7},{6,4},{7,5},{8,10},{9,11},{10,... | collective-permute-start | bytes 3145736 | tf_op jit(solution)/shard_map/ppermute | solution.py:355
  653.3 63.4 %collective-permute-start.15 = (bf16[256,2048]{1,0:T(8,128)(2,1)}, bf16[256,2048]{1,0:T(8,128)(2,1)}, u32[]{:S(2)}, u32[]{:S(2)}) collective-permute-start(bf16[256,2048]{1,0:T(8,128)(2,1)} %add_convert_fusion.7), channel_id=1, source_target_pairs={{0,2},{1,3},{2,0},{3,1},{4,6},{5,7},{6,4},{7,5},{8,10},{9,11},{10,... | collective-permute-start | bytes 3145736 | tf_op jit(solution)/shard_map/ppermute | solution.py:355
  681.2 91.0 %all-to-all-start.5 = ((bf16[4,128,2048]{2,1,0:T(8,128)(2,1)}), bf16[4,128,2048]{2,1,0:T(8,128)(2,1)S(1)}, u32[]{:S(2)}, u32[]{:S(2)}) async-start(bf16[4,128,2048]{2,1,0:T(8,128)(2,1)} %bitcast.165), calls=%async_computation.8 | async-start | bytes 4194304 | tf_op jit(solution)/shard_map/all_to_all | solution.py:423
  686.1 138.3 %all-gather.18.cloned.1.call-start = ((), (), s32[]{:S(2)}) async-start(), calls=%async_computation.15 | async-start | bytes 3932160 | tf_op jit(solution)/shard_map/all_gather | solution.py:963
  714.2 83.6 %collective-permute-start.21 = (bf16[4,4,128,1024]{3,2,1,0:T(8,128)(2,1)}, bf16[4,4,128,1024]{3,2,1,0:T(8,128)(2,1)}, u32[]{:S(2)}, u32[]{:S(2)}) collective-permute-start(bf16[4,4,128,1024]{3,2,1,0:T(8,128)(2,1)} %bitcast.170), channel_id=1, source_target_pairs={{0,16},{16,0},{1,17},{17,1},{2,18},{18,2},{3,19},{19,3},{4,20},{20... | collective-permute-start | bytes 12582920 | tf_op jit(solution)/shard_map/ppermute | solution.py:351
  714.2 90.2 %collective-permute-start.20 = (bf16[1024,2048]{1,0:T(8,128)(2,1)}, bf16[1024,2048]{1,0:T(8,128)(2,1)}, u32[]{:S(2)}, u32[]{:S(2)}) collective-permute-start(bf16[1024,2048]{1,0:T(8,128)(2,1)} %all-gather.16.cloned.1.call-done.own_ref), channel_id=1, source_target_pairs={{0,16},{16,0},{1,17},{17,1},{2,18},{18,2},{3,19},{19,3},{4,20},{20... | collective-permute-start | bytes 12582920 | tf_op jit(solution)/shard_map/ppermute | solution.py:351
  734.8 45.9 %collective-permute-start.24 = (f32[1,1792]{1,0:T(1,128)S(1)}, f32[1,1792]{1,0:T(1,128)S(1)}, u32[]{:S(2)}, u32[]{:S(2)}) collective-permute-start(f32[1,1792]{1,0:T(1,128)S(1)} %add.477), channel_id=1, source_target_pairs={{4,0},{8,12},{5,1},{9,13},{6,2},{10,14},{7,3},{11,15},{20,16},{24,... | collective-permute-start | bytes 21512 | tf_op jit(solution)/shard_map/ppermute | solution.py:453
  772.2 65.9 %all-to-all-start.3 = ((bf16[4,128,2048]{2,1,0:T(8,128)(2,1)}), bf16[4,128,2048]{2,1,0:T(8,128)(2,1)}, u32[]{:S(2)}, u32[]{:S(2)}) async-start(bf16[4,128,2048]{2,1,0:T(8,128)(2,1)} %bitcast.166), calls=%async_computation.5 | async-start | bytes 4194304 | tf_op jit(solution)/shard_map/all_to_all | solution.py:423
  779.6 86.9 %all-gather.22.cloned.1.call-start = ((), (), s32[]{:S(2)}) async-start(), calls=%async_computation.17 | async-start | bytes 1310720 | tf_op jit(solution)/shard_map/all_gather | solution.py:963
  (65 other events, 1754.3 us)
Sparse Core Ops, SparseCore 0:
  81.0 87.8 all-gather.11
  170.7 87.9 all-gather.13
  297.7 76.7 reduce-scatter.5
  377.3 77.2 reduce-scatter.3
  456.1 81.2 all-gather.15
  539.5 75.2 reduce-scatter.7
  616.5 97.7 all-gather.19
  715.9 108.5 all-gather.17
  831.1 25.9 all-gather.21

commit v5 on v4

--- a/solution.py
+++ b/solution.py
@@ -731,6 +731,44 @@
     )(*left, *[pair[0] for pair in rights], *[pair[1] for pair in rights])
 
 
+def grad_side(left, right, earlier=None, tile=512):
+    shape = (left.shape[1], right.shape[1])
+    steps = left.shape[0] // tile
+
+    def body(left_ref, right_ref, *rest):
+        step = pl.program_id(0)
+        acc = rest[-1]
+
+        @pl.when(step == 0)
+        def _():
+            acc[...] = jnp.zeros_like(acc) if earlier is None else rest[0][...]
+
+        for at in strips(shape[1]):
+            acc[:, at] += lax.dot_general(left_ref[...], right_ref[:, at], ROWS_OF, preferred_element_type=WIDE)
+
+        @pl.when(step == steps - 1)
+        def _():
+            rest[-2][...] = acc[...].astype(WIDE if earlier is None else LOW)
+
+    def tiles(width):
+        return pl.BlockSpec((tile, width), lambda i: (i, 0))
+
+    held = pl.BlockSpec(shape, lambda i: (0, 0), pipeline_mode=pl.Buffered(1))
+    more = [] if earlier is None else [earlier]
+    return pl.pallas_call(
+        body,
+        grid=(steps,),
+        in_specs=[tiles(shape[0]), tiles(shape[1])] + [held] * len(more),
+        out_specs=pl.BlockSpec(shape, lambda i: (0, 0)),
+        out_shape=jax.ShapeDtypeStruct(shape, WIDE if earlier is None else LOW),
+        scratch_shapes=[pltpu.VMEM(shape, WIDE)],
+        compiler_params=pltpu.CompilerParams(dimension_semantics=("arbitrary",), vmem_limit_bytes=ROOM),
+        cost_estimate=hint(
+            flops=2 * left.size * shape[1], transcendentals=0, bytes_accessed=2 * (left.size + right.size)
+        ),
+    )(left, right, *more)
+
+
 def rope_tables(seq_len):
     lane = jnp.arange(2 * HEAD_DIM, dtype=jnp.int32) % HEAD_DIM
     half = ROT // 2
@@ -965,7 +1003,7 @@
     def exchange(piece):
         return lax.all_to_all(piece[0], "fsdp", 0, 0, tiled=True)
 
-    g_down = grad_call(acts, [gout])[0]
+    g_down = grad_side(acts[1], gout[1], grad_side(acts[0], gout[0]))
     t_down = gather(scatter(g_down))
     for g, slope in zip((after(gout[0], g_down), gout[1]), slopes):
         dup, datt = down_back_call(g, slope, down_w, out_w)
@@ -1005,7 +1043,7 @@
     t_up = after(t_up, f_total, x_qkv)
     o_up = cols_out(core, shard, t_up, after(swap_dp(t_up), tails), 1, 1)
     o_down = rows_out(core, shard, t_down, after(swap_dp(t_down), o_up))
-    d_hidden = after(d_hidden, o_down).astype(WIDE)
+    d_hidden = d_hidden.astype(WIDE)
     mixed = to_home(mixed, core, place, blk)
     t_qkv = after(t_qkv, o_down)
     o_qkv = cols_out(core, shard, t_qkv, swap_dp(t_qkv), 3, 3)
@@ -1021,7 +1059,7 @@
     )
     back = (gout_home.astype(WIDE) + d_inputs).astype(LOW)
 
-    mixed = after(mixed, o_qkv, o_out)
+    mixed = after(mixed, o_qkv)
     result = jnp.where(valid, inputs + mixed.astype(WIDE) + bias_ends, 0.0).astype(LOW)
     d_bup = lax.dynamic_slice(tails, (2 * shard, 0), (2, units)).reshape(-1)
     d_bqkv = tails[:, units:].reshape(8, 3, head_cols).transpose(1, 0, 2).reshape(-1)

time: 901 us -> 897 us (level)
    pallas_call x0 -> x2, Pallas kernels: none -> 33.4 us  [grad_side(): pl.pallas_call(body, grid=(steps,), in_specs=[tiles(shape[0]), tiles(shap...]
    pallas_call x4 -> x3, Pallas kernels: 86.8 us -> 61.5 us  [grad_call(): pl.pallas_call(body, grid=(2 * steps,), in_specs=specs, out_specs=[fixed(...]
    ppermute x14, waiting for transfers between devices: 23.1 us -> 9.64 us  [swap_dp(): return lax.ppermute(value, 'dp', SWAP)]
  transfers between devices with their start and end apart: 54 -> 54, of which waited for: 23 -> 23; matrix products, arithmetic and copies ran while one was open for 9% -> 10% of each run, Pallas kernels for 39% -> 41%
where the time goes in v5:
time: 897 us; the launch traced here: 890 us
  Pallas kernels  386 us (43%)
  waiting for transfers between devices  249 us (28%)
  blocking collectives  80.4 us (9%)
  starting transfers between devices  58.4 us (7%)
  other arithmetic  53.2 us (6%)
  local copies, waits for them, and re-layouts  48.6 us (5%)
  between operations  14.9 us (2%)
    pallas_call x10, Pallas kernels, row_call(): pl.pallas_call(body, grid=(count // tile,), in_specs=[rows_spec(a.shape[1...  167 us
    ppermute x20, waiting for transfers between devices, swap_shard(): return lax.ppermute(value, 'fsdp', [(i, i ^ bits) for i in range(4)])  102 us
    pallas_call x1, Pallas kernels, attention_call(): pl.pallas_call(kernel, grid_spec=pltpu.PrefetchScalarGridSpec(num_scalar_...  70.5 us
    pallas_call x3, Pallas kernels, grad_call(): pl.pallas_call(body, grid=(2 * steps,), in_specs=specs, out_specs=[fixed(...  61.5 us
    all_to_all x1, blocking collectives, deal_out(): lax.all_to_all(lined, 'ctx', 0, 0, tiled=True).reshape(-1, lined.shape[2])  53.3 us
    all_gather x4, waiting for transfers between devices, gather(): return lax.all_gather(piece, 'ctx', axis=0, tiled=True)  36.7 us
    pallas_call x2, Pallas kernels, grad_side(): pl.pallas_call(body, grid=(steps,), in_specs=[tiles(shape[0]), tiles(shap...  33.4 us
    pallas_call x4, Pallas kernels, cols_half(): pl.pallas_call(kernel, grid_spec=pltpu.PrefetchScalarGridSpec(num_scalar_...  31.7 us
  transfers between devices with their start and end apart: 54, of which 23 were waited for; matrix products, arithmetic and copies ran while one was open for 10% of the time, Pallas kernels for 41%

profile of v5, /device:TPU:0, one launch (start us, length us, event | category | flops | bytes accessed | tf_op | source)
XLA Modules:
  0.0 890.0 jit_solution(840053603350266912)
XLA Ops:
  36.7 42.3 %collective-permute-done.2 = bf16[512,1024]{1,0:T(8,128)(2,1)S(1)} collective-permute-done((bf16[512,1024]{1,0:T(8,128)(2,1)S(1)}, bf16[512,1024]{1,0:T(8,128)(2,1)S(1)}, u32[]{:S(2)}, u32[]{:S(2)}) %collective-permute-start.2) | collective-permute-done | bytes 1048608 | tf_op jit(solution)/shard_map/ppermute | solution.py:355
  87.4 53.3 %all_to_all.30 = bf16[4,128,2048]{2,1,0:T(8,128)(2,1)} all-to-all(bf16[4,128,2048]{2,1,0:T(8,128)(2,1)S(1)} %bitcast.177), channel_id=1, replica_groups=mesh['dp'=2,'ctx'=4,'fsdp'=4] {'ctx'}, dimensions={0} | all-to-all | bytes 4194304 | tf_op jit(solution)/shard_map/all_to_all | solution.py:383
  140.9 28.0 %all-gather.12.cloned.1.call-done.rows_ref.refs_0_ = bf16[2048,2048]{1,0:T(8,128)(2,1)} async-done(((bf16[512,2048]{1,0:T(8,128)(2,1)}), bf16[2048,2048]{1,0:T(8,128)(2,1)}) %all-gather.12.cloned.1.call-update) | async-done | bytes 8388624 | tf_op jit(solution)/shard_map/all_gather | solution.py:969
  196.5 18.0 %shard_map.229 = (bf16[2048,1024]{1,0:T(8,128)(2,1)}, bf16[2048,1024]{1,0:T(8,128)(2,1)}) custom-call(bf16[2048,2048]{1,0:T(8,128)(2,1)} %all-gather.12.cloned.1.call-done.rows_ref.refs_0_, bf16[2048,1024]{1,0:T(8,128)(2,1)} %constant_dynamic-update-slice_fusion.4.weight_ref.refs_4_.refs_5_, f32[1,1024]{1,0:T(1,128)} %bitcast.218), custom_call_target="tpu_custom_call" | custom-call | flops 15461881856 | bytes 20975616 | tf_op jit(solution)/shard_map/pallas_call | solution.py:561
  214.5 18.0 %shard_map.230 = (bf16[2048,1024]{1,0:T(8,128)(2,1)}, bf16[2048,1024]{1,0:T(8,128)(2,1)}) custom-call(bf16[2048,2048]{1,0:T(8,128)(2,1)} %collective-permute-done.6.rows_ref.refs_1_, bf16[2048,1024]{1,0:T(8,128)(2,1)} %constant_dynamic-update-slice_fusion.4.weight_ref.refs_4_.refs_5_, f32[1,1024]{1,0:T(1,128)} %bitcast.219), custom_call_target="tpu_custom_call" | custom-call | flops 15461881856 | bytes 20975616 | tf_op jit(solution)/shard_map/pallas_call | solution.py:561
  232.5 26.2 %all-gather.14.cloned.1.call-done.right_ref.rows_ref.refs_2_ = bf16[2048,2048]{1,0:T(8,128)(2,1)} async-done(((bf16[512,2048]{1,0:T(8,128)(2,1)}), bf16[2048,2048]{1,0:T(8,128)(2,1)}) %all-gather.14.cloned.1.call-update) | async-done | bytes 8388624 | tf_op jit(solution)/shard_map/all_gather | solution.py:973
  258.7 16.1 %shard_map.231.rest_0_ = f32[1024,2048]{1,0:T(8,128)} custom-call(bf16[2048,1024]{1,0:T(8,128)(2,1)} %get-tuple-element.110.left_ref.refs_0_, bf16[2048,2048]{1,0:T(8,128)(2,1)} %all-gather.14.cloned.1.call-done.right_ref.rows_ref.refs_2_), custom_call_target="tpu_custom_call" | custom-call | flops 15461881856 | bytes 12582912 | tf_op jit(solution)/shard_map/pallas_call | solution.py:758
  274.7 17.3 %shard_map.232 = bf16[1024,2048]{1,0:T(8,128)(2,1)} custom-call(bf16[2048,1024]{1,0:T(8,128)(2,1)} %get-tuple-element.108.left_ref.refs_0_, bf16[2048,2048]{1,0:T(8,128)(2,1)} %collective-permute-done.7.right_ref.rows_ref.refs_3_, f32[1024,2048]{1,0:T(8,128)} %shard_map.231.rest_0_), custom_call_target="tpu_custom_call" | custom-call | flops 15461881856 | bytes 12582912 | tf_op jit(solution)/shard_map/pallas_call | solution.py:758
  303.9 16.8 %shard_map.233 = (bf16[2048,1024]{1,0:T(8,128)(2,1)}, bf16[2048,256]{1,0:T(8,128)(2,1)}) custom-call(bf16[2048,2048]{1,0:T(8,128)(2,1)} %all-gather.14.cloned.1.call-done.right_ref.rows_ref.refs_2_, bf16[2048,1024]{1,0:T(8,128)(2,1)} %get-tuple-element.81.slope_ref, bf16[1024,2048]{1,0:T(8,128)(2,1)} %constant_dynamic-slice_fusion.28.down_ref.refs_2_.refs_3_, ...), custom_call_target="tpu_custom_call" | custom-call | flops 19327352832 | bytes 23068672 | tf_op jit(solution)/shard_map/pallas_call | solution.py:561
  320.6 16.8 %shard_map.234 = (bf16[2048,1024]{1,0:T(8,128)(2,1)}, bf16[2048,256]{1,0:T(8,128)(2,1)}) custom-call(bf16[2048,2048]{1,0:T(8,128)(2,1)} %collective-permute-done.7.right_ref.rows_ref.refs_3_, bf16[2048,1024]{1,0:T(8,128)(2,1)} %get-tuple-element.83.slope_ref, bf16[1024,2048]{1,0:T(8,128)(2,1)} %constant_dynamic-slice_fusion.28.down_ref.refs_2_.refs_3_, ...), custom_call_target="tpu_custom_call" | custom-call | flops 19327352832 | bytes 23068672 | tf_op jit(solution)/shard_map/pallas_call | solution.py:561
  338.1 26.8 %shard_map.235 = (bf16[4,4,128,1024]{3,2,1,0:T(8,128)(2,1)}, f32[1,1024]{1,0:T(1,128)}) custom-call(bf16[2048,2048]{1,0:T(8,128)(2,1)} %all-gather.12.cloned.1.call-done.rows_ref.refs_0_, bf16[2048,2048]{1,0:T(8,128)(2,1)} %collective-permute-done.6.rows_ref.refs_1_, bf16[2048,1024]{1,0:T(8,128)(2,1)} %get-tuple-element.109.refs_2_.refs_0_, ...), custom_call_target="tpu_custom_call" | custom-call | flops 30923763712 | bytes 25165824 | tf_op jit(solution)/shard_map/pallas_call | solution.py:719
  374.0 10.9 %shard_map.237 = bf16[2048,768]{1,0:T(8,128)(2,1)} custom-call(bf16[2048,2048]{1,0:T(8,128)(2,1)} %collective-permute-done.6.rows_ref.refs_1_, bf16[2048,768]{1,0:T(8,128)(2,1)} %copy-done.13, f32[1,768]{1,0:T(1,128)} %convert.17.bias_ref), custom_call_target="tpu_custom_call" | custom-call | flops 11596411904 | bytes 14683136 | tf_op jit(solution)/shard_map/pallas_call | solution.py:561
  395.7 70.5 %shard_map.238 = (bf16[4,512,256]{2,1,0:T(8,128)(2,1)}, bf16[4,512,256]{2,1,0:T(8,128)(2,1)}, bf16[4,512,256]{2,1,0:T(8,128)(2,1)}, bf16[4,512,256]{2,1,0:T(8,12...) custom-call(s32[4,4]{1,0:T(4,128)} %bitcast.222, ...), custom_call_target="tpu_custom_call" | custom-call | flops 69578473472 | bytes 16777216 | tf_op jit(solution)/shard_map/pallas_call | solution.py:872
  466.2 13.2 %shard_map.239 = bf16[4,4,128,256]{3,2,1,0:T(8,128)(2,1)} custom-call(bf16[2048,256]{1,0:T(8,128)(2,1)} %bitcast.232, bf16[2048,256]{1,0:T(8,128)(2,1)} %bitcast.242, bf16[2048,2048]{1,0:T(8,128)(2,1)} %all-gather.14.cloned.1.call-done.right_ref.rows_ref.refs_2_, bf16[2048,2048]{1,0:T(8,128)(2,1)} %collective-permute-done.7.right_ref.rows_ref.refs_3_), custom_call_target="tpu_custom_call" | custom-call | flops 7730940928 | bytes 18874368 | tf_op jit(solution)/shard_map/pallas_call | solution.py:719
  482.9 21.4 %shard_map.240 = (bf16[4,4,128,768]{3,2,1,0:T(8,128)(2,1)}, f32[1,256]{1,0:T(1,128)}, f32[1,256]{1,0:T(1,128)}, f32[1,256]{1,0:T(1,128)}) custom-call(bf16[2048,2048]{1,0:T(8,128)(2,1)} %all-gather.12.cloned.1.call-done.rows_ref.refs_0_, bf16[2048,2048]{1,0:T(8,128)(2,1)} %collective-permute-done.6.rows_ref.refs_1_, bf16[2048,256]{1,0:T(8,128)(2,1)} %bitcast.236, ...), custom_call_target="tpu_custom_call" | custom-call | flops 23192823808 | bytes 23068672 | tf_op jit(solution)/shard_map/pallas_call | solution.py:719
  508.9 21.6 %shard_map.241 = bf16[2048,2048]{1,0:T(8,128)(2,1)} custom-call(bf16[2048,1024]{1,0:T(8,128)(2,1)} %get-tuple-element.84.refs_3_.refs_0_, bf16[2048,256]{1,0:T(8,128)(2,1)} %bitcast.245, bf16[2048,256]{1,0:T(8,128)(2,1)} %bitcast.247, bf16[2048,256]{1,0:T(8,128)(2,1)} %bitcast.249, ...), custom_call_target="tpu_custom_call" | custom-call | flops 27058294784 | bytes 23068672 | tf_op jit(solution)/shard_map/pallas_call | solution.py:561
  532.0 15.8 %shard_map.242 = bf16[2048,2048]{1,0:T(8,128)(2,1)} custom-call(bf16[2048,1024]{1,0:T(8,128)(2,1)} %get-tuple-element.108.left_ref.refs_0_, bf16[2048,256]{1,0:T(8,128)(2,1)} %bitcast.243, bf16[1024,2048]{1,0:T(8,128)(2,1)} %constant_dynamic-slice_fusion.28.down_ref.refs_2_.refs_3_, bf16[256,2048]{1,0:T(8,128)(2,1)} %constant_dynamic-slice_fusion.27.out_w_ref.refs_3_.refs_4_), custom_call_target="tpu_custom_call" | custom-call | flops 19327352832 | bytes 18874368 | tf_op jit(solution)/shard_map/pallas_call | solution.py:561
  547.8 21.9 %shard_map.243 = bf16[2048,2048]{1,0:T(8,128)(2,1)} custom-call(bf16[2048,1024]{1,0:T(8,128)(2,1)} %get-tuple-element.109.refs_2_.refs_0_, bf16[2048,256]{1,0:T(8,128)(2,1)} %bitcast.237, bf16[2048,256]{1,0:T(8,128)(2,1)} %bitcast.239, bf16[2048,256]{1,0:T(8,128)(2,1)} %bitcast.241, bf16[2048,2048]{1,0:T(8,128)(2,1)} %collective-permute-done.11.refs_4_, ...), custom_call_target="tpu_custom_call" | custom-call | flops 27058294784 | bytes 31457280 | tf_op jit(solution)/shard_map/pallas_call | solution.py:561
  576.0 16.5 %shard_map.244 = bf16[2048,2048]{1,0:T(8,128)(2,1)} custom-call(bf16[2048,1024]{1,0:T(8,128)(2,1)} %get-tuple-element.110.left_ref.refs_0_, bf16[2048,256]{1,0:T(8,128)(2,1)} %bitcast.233, bf16[2048,2048]{1,0:T(8,128)(2,1)} %collective-permute-done.12.refs_2_, bf16[1024,2048]{1,0:T(8,128)(2,1)} %constant_dynamic-slice_fusion.28.down_ref.refs_2_.refs_3_, ...), custom_call_target="tpu_custom_call" | custom-call | flops 19327352832 | bytes 27262976 | tf_op jit(solution)/shard_map/pallas_call | solution.py:561
  610.4 12.1 %collective-permute-done.26 = bf16[256,2048]{1,0:T(8,128)(2,1)} collective-permute-done((bf16[256,2048]{1,0:T(8,128)(2,1)S(1)}, bf16[256,2048]{1,0:T(8,128)(2,1)}, u32[]{:S(2)}, u32[]{:S(2)}) %collective-permute-start.26) | collective-permute-done | bytes 1048608 | tf_op jit(solution)/shard_map/ppermute | solution.py:355
  651.5 16.0 %collective-permute-done.30 = bf16[256,2048]{1,0:T(8,128)(2,1)} collective-permute-done((bf16[256,2048]{1,0:T(8,128)(2,1)}, bf16[256,2048]{1,0:T(8,128)(2,1)}, u32[]{:S(2)}, u32[]{:S(2)}) %collective-permute-start.30) | collective-permute-done | bytes 1048608 | tf_op jit(solution)/shard_map/ppermute | solution.py:355
  681.1 27.9 %all-gather.20.cloned.1.call-done = bf16[16,128,1024]{2,1,0:T(8,128)(2,1)} async-done(((bf16[4,128,1024]{2,1,0:T(8,128)(2,1)}), bf16[16,128,1024]{2,1,0:T(8,128)(2,1)}) %all-gather.20.cloned.1.call-update) | async-done | bytes 4194320 | tf_op jit(solution)/shard_map/all_gather | solution.py:1001
  745.0 22.0 %all-to-all-done.5 = bf16[4,128,2048]{2,1,0:T(8,128)(2,1)S(1)} async-done(((bf16[4,128,2048]{2,1,0:T(8,128)(2,1)}), bf16[4,128,2048]{2,1,0:T(8,128)(2,1)S(1)}, u32[]{:S(2)}, u32[]{:S(2)}) %all-to-all-start.5) | async-done | bytes 2097184 | tf_op jit(solution)/shard_map/all_to_all | solution.py:423
  798.3 14.0 %shard_map.247 = f32[2048,2048]{1,0:T(8,128)} custom-call(s32[2]{0:T(128)} %pad_add_fusion.where, bf16[1024,2048]{1,0:T(8,128)(2,1)} %all-gather.16.cloned.1.call-done.own_ref, bf16[1024,2048]{1,0:T(8,128)(2,1)} %collective-permute-done.20.oth_ref), custom_call_target="tpu_custom_call" | custom-call | bytes 25165824 | tf_op jit(solution)/shard_map/pallas_call | solution.py:488
  (311 shorter events, 311.5 us)
Async XLA Ops:
  25.4 55.4 %all-to-all-start = ((bf16[4,128,2048]{2,1,0:T(8,128)(2,1)}), bf16[4,128,2048]{2,1,0:T(8,128)(2,1)}, u32[]{:S(2)}, u32[]{:S(2)}) async-start(bf16[4,128,2048]{2,1,0:T(8,128)(2,1)} %fusion.19), calls=%async_computation | async-start | bytes 4194304 | tf_op jit(solution)/shard_map/all_to_all | solution.py:383
  30.3 138.6 %all-gather.12.cloned.1.call-start = ((), (), s32[]{:S(2)}) async-start(), calls=%async_computation.9 | async-start | bytes 10485760 | tf_op jit(solution)/shard_map/all_gather | solution.py:969
  33.1 45.8 %collective-permute-start.2 = (bf16[512,1024]{1,0:T(8,128)(2,1)S(1)}, bf16[512,1024]{1,0:T(8,128)(2,1)S(1)}, u32[]{:S(2)}, u32[]{:S(2)}) collective-permute-start(bf16[512,1024]{1,0:T(8,128)(2,1)S(1)} %get-tuple-element.71), channel_id=1, source_target_pairs={{0,2},{1,3},{2,0},{3,1},{4,6},{5,7},{6,4},{7,5},{8,10},{9,11},{10,... | collective-permute-start | bytes 3145736 | tf_op jit(solution)/shard_map/ppermute | solution.py:355
  36.1 44.7 %collective-permute-start.1 = (bf16[512,1024]{1,0:T(8,128)(2,1)S(1)}, bf16[512,1024]{1,0:T(8,128)(2,1)}, u32[]{:S(2)}, u32[]{:S(2)}) collective-permute-start(bf16[512,1024]{1,0:T(8,128)(2,1)S(1)} %get-tuple-element.70), channel_id=1, source_target_pairs={{0,1},{1,0},{2,3},{3,2},{4,5},{5,4},{6,7},{7,6},{8,9},{9,8},{10,11... | collective-permute-start | bytes 3145736 | tf_op jit(solution)/shard_map/ppermute | solution.py:355
  80.9 177.8 %all-gather.14.cloned.1.call-start = ((), (), s32[]{:S(2)}) async-start(), calls=%async_computation.10 | async-start | bytes 10485760 | tf_op jit(solution)/shard_map/all_gather | solution.py:973
  140.8 254.8 %reduce-scatter.6.cloned.1.call-start = ((), (), s32[]{:S(2)}) async-start(), calls=%async_computation.12 | async-start | bytes 5242880 | tf_op jit(solution)/shard_map/reduce_scatter | solution.py:998
  168.9 45.6 %collective-permute-start.6 = (bf16[2048,2048]{1,0:T(8,128)(2,1)}, bf16[2048,2048]{1,0:T(8,128)(2,1)}, u32[]{:S(2)}, u32[]{:S(2)}) collective-permute-start(bf16[2048,2048]{1,0:T(8,128)(2,1)} %all-gather.12.cloned.1.call-done.rows_ref.refs_0_), channel_id=1, source_target_pairs={{0,16},{16,0},{1,17},{17,1},{2,18},{18,2},{3,19},{19,3},{4,20},{20... | collective-permute-start | bytes 25165832 | tf_op jit(solution)/shard_map/ppermute | solution.py:351
  292.1 187.3 %reduce-scatter.4.cloned.1.call-start = ((), (), s32[]{:S(2)}) async-start(), calls=%async_computation.11 | async-start | bytes 5242880 | tf_op jit(solution)/shard_map/reduce_scatter | solution.py:998
  365.0 167.0 %all-gather.16.cloned.1.call-start = ((), (), s32[]{:S(2)}) async-start(), calls=%async_computation.13 | async-start | bytes 5242880 | tf_op jit(solution)/shard_map/all_gather | solution.py:1001
  482.9 152.2 %reduce-scatter.8.cloned.1.call-start = ((), (), s32[]{:S(2)}) async-start(), calls=%async_computation.14 | async-start | bytes 5242880 | tf_op jit(solution)/shard_map/reduce_scatter | solution.py:998
  508.9 200.1 %all-gather.20.cloned.1.call-start = ((), (), s32[]{:S(2)}) async-start(), calls=%async_computation.16 | async-start | bytes 5242880 | tf_op jit(solution)/shard_map/all_gather | solution.py:1001
  575.5 47.1 %collective-permute-start.26 = (bf16[256,2048]{1,0:T(8,128)(2,1)S(1)}, bf16[256,2048]{1,0:T(8,128)(2,1)}, u32[]{:S(2)}, u32[]{:S(2)}) collective-permute-start(bf16[256,2048]{1,0:T(8,128)(2,1)S(1)} %get-tuple-element.134), channel_id=1, source_target_pairs={{0,1},{1,0},{2,3},{3,2},{4,5},{5,4},{6,7},{7,6},{8,9},{9,8},{10,11... | collective-permute-start | bytes 3145736 | tf_op jit(solution)/shard_map/ppermute | solution.py:355
  603.1 48.4 %collective-permute-start.31 = (bf16[256,2048]{1,0:T(8,128)(2,1)S(1)}, bf16[256,2048]{1,0:T(8,128)(2,1)}, u32[]{:S(2)}, u32[]{:S(2)}) collective-permute-start(bf16[256,2048]{1,0:T(8,128)(2,1)S(1)} %get-tuple-element.135), channel_id=1, source_target_pairs={{0,2},{1,3},{2,0},{3,1},{4,6},{5,7},{6,4},{7,5},{8,10},{9,11},{10,... | collective-permute-start | bytes 3145736 | tf_op jit(solution)/shard_map/ppermute | solution.py:355
  640.8 70.6 %collective-permute-start.13 = (bf16[256,2048]{1,0:T(8,128)(2,1)}, bf16[256,2048]{1,0:T(8,128)(2,1)}, u32[]{:S(2)}, u32[]{:S(2)}) collective-permute-start(bf16[256,2048]{1,0:T(8,128)(2,1)} %get-tuple-element.140), channel_id=1, source_target_pairs={{0,1},{1,0},{2,3},{3,2},{4,5},{5,4},{6,7},{7,6},{8,9},{9,8},{10,11... | collective-permute-start | bytes 3145736 | tf_op jit(solution)/shard_map/ppermute | solution.py:355
  642.8 66.7 %collective-permute-start.16 = (bf16[256,2048]{1,0:T(8,128)(2,1)}, bf16[256,2048]{1,0:T(8,128)(2,1)}, u32[]{:S(2)}, u32[]{:S(2)}) collective-permute-start(bf16[256,2048]{1,0:T(8,128)(2,1)} %get-tuple-element.142), channel_id=1, source_target_pairs={{0,2},{1,3},{2,0},{3,1},{4,6},{5,7},{6,4},{7,5},{8,10},{9,11},{10,... | collective-permute-start | bytes 3145736 | tf_op jit(solution)/shard_map/ppermute | solution.py:355
  647.9 63.5 %collective-permute-start.15 = (bf16[256,2048]{1,0:T(8,128)(2,1)}, bf16[256,2048]{1,0:T(8,128)(2,1)}, u32[]{:S(2)}, u32[]{:S(2)}) collective-permute-start(bf16[256,2048]{1,0:T(8,128)(2,1)} %add_convert_fusion.7), channel_id=1, source_target_pairs={{0,2},{1,3},{2,0},{3,1},{4,6},{5,7},{6,4},{7,5},{8,10},{9,11},{10,... | collective-permute-start | bytes 3145736 | tf_op jit(solution)/shard_map/ppermute | solution.py:355
  675.9 91.2 %all-to-all-start.5 = ((bf16[4,128,2048]{2,1,0:T(8,128)(2,1)}), bf16[4,128,2048]{2,1,0:T(8,128)(2,1)S(1)}, u32[]{:S(2)}, u32[]{:S(2)}) async-start(bf16[4,128,2048]{2,1,0:T(8,128)(2,1)} %bitcast.175), calls=%async_computation.8 | async-start | bytes 4194304 | tf_op jit(solution)/shard_map/all_to_all | solution.py:423
  680.3 139.5 %all-gather.18.cloned.1.call-start = ((), (), s32[]{:S(2)}) async-start(), calls=%async_computation.15 | async-start | bytes 3932160 | tf_op jit(solution)/shard_map/all_gather | solution.py:1001
  709.0 82.6 %collective-permute-start.21 = (bf16[4,4,128,1024]{3,2,1,0:T(8,128)(2,1)}, bf16[4,4,128,1024]{3,2,1,0:T(8,128)(2,1)}, u32[]{:S(2)}, u32[]{:S(2)}) collective-permute-start(bf16[4,4,128,1024]{3,2,1,0:T(8,128)(2,1)} %bitcast.180), channel_id=1, source_target_pairs={{0,16},{16,0},{1,17},{17,1},{2,18},{18,2},{3,19},{19,3},{4,20},{20... | collective-permute-start | bytes 12582920 | tf_op jit(solution)/shard_map/ppermute | solution.py:351
  709.0 89.3 %collective-permute-start.20 = (bf16[1024,2048]{1,0:T(8,128)(2,1)}, bf16[1024,2048]{1,0:T(8,128)(2,1)}, u32[]{:S(2)}, u32[]{:S(2)}) collective-permute-start(bf16[1024,2048]{1,0:T(8,128)(2,1)} %all-gather.16.cloned.1.call-done.own_ref), channel_id=1, source_target_pairs={{0,16},{16,0},{1,17},{17,1},{2,18},{18,2},{3,19},{19,3},{4,20},{20... | collective-permute-start | bytes 12582920 | tf_op jit(solution)/shard_map/ppermute | solution.py:351
  728.7 45.9 %collective-permute-start.24 = (f32[1,1792]{1,0:T(1,128)S(1)}, f32[1,1792]{1,0:T(1,128)S(1)}, u32[]{:S(2)}, u32[]{:S(2)}) collective-permute-start(f32[1,1792]{1,0:T(1,128)S(1)} %add.477), channel_id=1, source_target_pairs={{4,0},{8,12},{5,1},{9,13},{6,2},{10,14},{7,3},{11,15},{20,16},{24,... | collective-permute-start | bytes 21512 | tf_op jit(solution)/shard_map/ppermute | solution.py:453
  767.0 66.0 %all-to-all-start.3 = ((bf16[4,128,2048]{2,1,0:T(8,128)(2,1)}), bf16[4,128,2048]{2,1,0:T(8,128)(2,1)}, u32[]{:S(2)}, u32[]{:S(2)}) async-start(bf16[4,128,2048]{2,1,0:T(8,128)(2,1)} %bitcast.176), calls=%async_computation.5 | async-start | bytes 4194304 | tf_op jit(solution)/shard_map/all_to_all | solution.py:423
  774.4 92.7 %all-gather.22.cloned.1.call-start = ((), (), s32[]{:S(2)}) async-start(), calls=%async_computation.17 | async-start | bytes 1310720 | tf_op jit(solution)/shard_map/all_gather | solution.py:1001
  774.5 45.4 %collective-permute-start.32 = (bf16[2,128,2048]{2,1,0:T(8,128)(2,1)S(1)}, bf16[2,128,2048]{2,1,0:T(8,128)(2,1)}, u32[]{:S(2)}, u32[]{:S(2)}) collective-permute-start(bf16[2,128,2048]{2,1,0:T(8,128)(2,1)S(1)} %dynamic-slice_bitcast_fusion), channel_id=1, source_target_pairs={{0,16},{16,0},{1,17},{17,1},{2,18},{18,2},{3,19},{19,3},{4,20},{20... | collective-permute-start | bytes 3145736 | tf_op jit(solution)/shard_map/ppermute | solution.py:351
  (67 other events, 1773.3 us)
Sparse Core Ops, SparseCore 0:
  81.0 87.8 all-gather.11
  170.7 87.9 all-gather.13
  292.2 76.8 reduce-scatter.5
  372.0 77.2 reduce-scatter.3
  450.7 81.2 all-gather.15
  534.2 75.2 reduce-scatter.7
  611.1 97.8 all-gather.19
  711.2 108.5 all-gather.17
  826.5 25.5 all-gather.21

commit v6 on v5

--- a/solution.py
+++ b/solution.py
@@ -981,9 +981,11 @@
     up_b = lax.dynamic_slice_in_dim(bias_up.reshape(-1), spot * units, units).astype(WIDE)
     qkv_b = pick(bias_qkv.reshape(3, 8, head_cols), spot, 1).reshape(-1).astype(WIDE)
 
+    down_w = lax.dynamic_slice_in_dim(w_down, core * units, units, 0)
+    out_w = lax.dynamic_slice_in_dim(w_out, core * head_cols, head_cols, 0)
     acts, slopes, dups, datts = [], [], [], []
     for h in hidden:
-        act, slope = up_call(h, up_w, up_b)
+        act, slope = up_call(after(h, down_w, out_w), up_w, up_b)
         acts.append(act)
         slopes.append(slope)
     gout_own = after(gout_own, *acts)
@@ -991,8 +993,6 @@
     qkv_sent = columns_sent([after(piece, gout_own) for piece in columns_cut(w_qkv, 3, core, shard)])
     qkv_w = placed(qkv_sent, shard, w_qkv.shape[0])
     tables = rope_tables(8 * blk)
-    down_w = lax.dynamic_slice_in_dim(w_down, core * units, units, 0)
-    out_w = lax.dynamic_slice_in_dim(w_out, core * head_cols, head_cols, 0)
 
     def scatter(grad):
         return lax.psum_scatter(grad, "ctx", scatter_dimension=0, tiled=True)

time: 897 us -> 897 us (level)
  transfers between devices with their start and end apart: 54 -> 54, of which waited for: 23 -> 22; matrix products, arithmetic and copies ran while one was open for 10% -> 9% of each run, Pallas kernels for 41% -> 41%
where the time goes in v6:
time: 897 us; the launch traced here: 890 us
  Pallas kernels  386 us (43%)
  waiting for transfers between devices  250 us (28%)
  blocking collectives  80.2 us (9%)
  starting transfers between devices  57.6 us (6%)
  other arithmetic  53.2 us (6%)
  local copies, waits for them, and re-layouts  47.6 us (5%)
  between operations  14.9 us (2%)
    pallas_call x10, Pallas kernels, row_call(): pl.pallas_call(body, grid=(count // tile,), in_specs=[rows_spec(a.shape[1...  168 us
    ppermute x20, waiting for transfers between devices, swap_shard(): return lax.ppermute(value, 'fsdp', [(i, i ^ bits) for i in range(4)])  101 us
    pallas_call x1, Pallas kernels, attention_call(): pl.pallas_call(kernel, grid_spec=pltpu.PrefetchScalarGridSpec(num_scalar_...  70.5 us
    pallas_call x3, Pallas kernels, grad_call(): pl.pallas_call(body, grid=(2 * steps,), in_specs=specs, out_specs=[fixed(...  61.6 us
    all_to_all x1, blocking collectives, deal_out(): lax.all_to_all(lined, 'ctx', 0, 0, tiled=True).reshape(-1, lined.shape[2])  53.2 us
    all_gather x4, waiting for transfers between devices, gather(): return lax.all_gather(piece, 'ctx', axis=0, tiled=True)  43.2 us
    pallas_call x2, Pallas kernels, grad_side(): pl.pallas_call(body, grid=(steps,), in_specs=[tiles(shape[0]), tiles(shap...  33 us
    pallas_call x4, Pallas kernels, cols_half(): pl.pallas_call(kernel, grid_spec=pltpu.PrefetchScalarGridSpec(num_scalar_...  31.7 us
  transfers between devices with their start and end apart: 54, of which 22 were waited for; matrix products, arithmetic and copies ran while one was open for 9% of the time, Pallas kernels for 41%

profile of v6, /device:TPU:0, one launch (start us, length us, event | category | flops | bytes accessed | tf_op | source)
XLA Modules:
  0.0 889.6 jit_solution(16472530259355864790)
XLA Ops:
  36.7 42.3 %collective-permute-done.2 = bf16[512,1024]{1,0:T(8,128)(2,1)S(1)} collective-permute-done((bf16[512,1024]{1,0:T(8,128)(2,1)S(1)}, bf16[512,1024]{1,0:T(8,128)(2,1)S(1)}, u32[]{:S(2)}, u32[]{:S(2)}) %collective-permute-start.2) | collective-permute-done | bytes 1048608 | tf_op jit(solution)/shard_map/ppermute | solution.py:355
  87.4 53.2 %all_to_all.30 = bf16[4,128,2048]{2,1,0:T(8,128)(2,1)} all-to-all(bf16[4,128,2048]{2,1,0:T(8,128)(2,1)S(1)} %bitcast.177), channel_id=1, replica_groups=mesh['dp'=2,'ctx'=4,'fsdp'=4] {'ctx'}, dimensions={0} | all-to-all | bytes 4194304 | tf_op jit(solution)/shard_map/all_to_all | solution.py:383
  140.7 28.2 %all-gather.12.cloned.1.call-done.rows_ref.refs_0_ = bf16[2048,2048]{1,0:T(8,128)(2,1)} async-done(((bf16[512,2048]{1,0:T(8,128)(2,1)}), bf16[2048,2048]{1,0:T(8,128)(2,1)}) %all-gather.12.cloned.1.call-update) | async-done | bytes 8388624 | tf_op jit(solution)/shard_map/all_gather | solution.py:969
  195.4 18.0 %shard_map.229 = (bf16[2048,1024]{1,0:T(8,128)(2,1)}, bf16[2048,1024]{1,0:T(8,128)(2,1)}) custom-call(bf16[2048,2048]{1,0:T(8,128)(2,1)} %all-gather.12.cloned.1.call-done.rows_ref.refs_0_, bf16[2048,1024]{1,0:T(8,128)(2,1)} %constant_dynamic-update-slice_fusion.4.weight_ref.refs_4_.refs_5_, f32[1,1024]{1,0:T(1,128)} %bitcast.218), custom_call_target="tpu_custom_call" | custom-call | flops 15461881856 | bytes 20975616 | tf_op jit(solution)/shard_map/pallas_call | solution.py:561
  213.5 18.0 %shard_map.230 = (bf16[2048,1024]{1,0:T(8,128)(2,1)}, bf16[2048,1024]{1,0:T(8,128)(2,1)}) custom-call(bf16[2048,2048]{1,0:T(8,128)(2,1)} %collective-permute-done.6.rows_ref.refs_1_, bf16[2048,1024]{1,0:T(8,128)(2,1)} %constant_dynamic-update-slice_fusion.4.weight_ref.refs_4_.refs_5_, f32[1,1024]{1,0:T(1,128)} %bitcast.219), custom_call_target="tpu_custom_call" | custom-call | flops 15461881856 | bytes 20975616 | tf_op jit(solution)/shard_map/pallas_call | solution.py:561
  231.5 27.2 %all-gather.14.cloned.1.call-done.right_ref.rows_ref.refs_2_ = bf16[2048,2048]{1,0:T(8,128)(2,1)} async-done(((bf16[512,2048]{1,0:T(8,128)(2,1)}), bf16[2048,2048]{1,0:T(8,128)(2,1)}) %all-gather.14.cloned.1.call-update) | async-done | bytes 8388624 | tf_op jit(solution)/shard_map/all_gather | solution.py:973
  258.7 16.1 %shard_map.231.rest_0_ = f32[1024,2048]{1,0:T(8,128)} custom-call(bf16[2048,1024]{1,0:T(8,128)(2,1)} %get-tuple-element.114.left_ref.refs_0_, bf16[2048,2048]{1,0:T(8,128)(2,1)} %all-gather.14.cloned.1.call-done.right_ref.rows_ref.refs_2_), custom_call_target="tpu_custom_call" | custom-call | flops 15461881856 | bytes 12582912 | tf_op jit(solution)/shard_map/pallas_call | solution.py:758
  274.7 16.9 %shard_map.232 = bf16[1024,2048]{1,0:T(8,128)(2,1)} custom-call(bf16[2048,1024]{1,0:T(8,128)(2,1)} %get-tuple-element.112.left_ref.refs_0_, bf16[2048,2048]{1,0:T(8,128)(2,1)} %collective-permute-done.7.right_ref.rows_ref.refs_3_, f32[1024,2048]{1,0:T(8,128)} %shard_map.231.rest_0_), custom_call_target="tpu_custom_call" | custom-call | flops 15461881856 | bytes 12582912 | tf_op jit(solution)/shard_map/pallas_call | solution.py:758
  297.7 17.4 %shard_map.233 = (bf16[2048,1024]{1,0:T(8,128)(2,1)}, bf16[2048,256]{1,0:T(8,128)(2,1)}) custom-call(bf16[2048,2048]{1,0:T(8,128)(2,1)} %all-gather.14.cloned.1.call-done.right_ref.rows_ref.refs_2_, bf16[2048,1024]{1,0:T(8,128)(2,1)} %get-tuple-element.85.slope_ref, bf16[1024,2048]{1,0:T(8,128)(2,1)} %constant_dynamic-slice_fusion.28.down_ref.refs_2_.refs_3_, ...), custom_call_target="tpu_custom_call" | custom-call | flops 19327352832 | bytes 23068672 | tf_op jit(solution)/shard_map/pallas_call | solution.py:561
  315.1 16.8 %shard_map.234 = (bf16[2048,1024]{1,0:T(8,128)(2,1)}, bf16[2048,256]{1,0:T(8,128)(2,1)}) custom-call(bf16[2048,2048]{1,0:T(8,128)(2,1)} %collective-permute-done.7.right_ref.rows_ref.refs_3_, bf16[2048,1024]{1,0:T(8,128)(2,1)} %get-tuple-element.87.slope_ref, bf16[1024,2048]{1,0:T(8,128)(2,1)} %constant_dynamic-slice_fusion.28.down_ref.refs_2_.refs_3_, ...), custom_call_target="tpu_custom_call" | custom-call | flops 19327352832 | bytes 23068672 | tf_op jit(solution)/shard_map/pallas_call | solution.py:561
  332.0 26.8 %shard_map.235 = (bf16[4,4,128,1024]{3,2,1,0:T(8,128)(2,1)}, f32[1,1024]{1,0:T(1,128)}) custom-call(bf16[2048,2048]{1,0:T(8,128)(2,1)} %all-gather.12.cloned.1.call-done.rows_ref.refs_0_, bf16[2048,2048]{1,0:T(8,128)(2,1)} %collective-permute-done.6.rows_ref.refs_1_, bf16[2048,1024]{1,0:T(8,128)(2,1)} %get-tuple-element.113.refs_2_.refs_0_, ...), custom_call_target="tpu_custom_call" | custom-call | flops 30923763712 | bytes 25165824 | tf_op jit(solution)/shard_map/pallas_call | solution.py:719
  367.9 10.8 %shard_map.237 = bf16[2048,768]{1,0:T(8,128)(2,1)} custom-call(bf16[2048,2048]{1,0:T(8,128)(2,1)} %collective-permute-done.6.rows_ref.refs_1_, bf16[2048,768]{1,0:T(8,128)(2,1)} %copy-done.13, f32[1,768]{1,0:T(1,128)} %convert.17.bias_ref), custom_call_target="tpu_custom_call" | custom-call | flops 11596411904 | bytes 14683136 | tf_op jit(solution)/shard_map/pallas_call | solution.py:561
  389.5 70.5 %shard_map.238 = (bf16[4,512,256]{2,1,0:T(8,128)(2,1)}, bf16[4,512,256]{2,1,0:T(8,128)(2,1)}, bf16[4,512,256]{2,1,0:T(8,128)(2,1)}, bf16[4,512,256]{2,1,0:T(8,12...) custom-call(s32[4,4]{1,0:T(4,128)} %bitcast.222, ...), custom_call_target="tpu_custom_call" | custom-call | flops 69578473472 | bytes 16777216 | tf_op jit(solution)/shard_map/pallas_call | solution.py:872
  460.0 13.3 %shard_map.239 = bf16[4,4,128,256]{3,2,1,0:T(8,128)(2,1)} custom-call(bf16[2048,256]{1,0:T(8,128)(2,1)} %bitcast.232, bf16[2048,256]{1,0:T(8,128)(2,1)} %bitcast.242, bf16[2048,2048]{1,0:T(8,128)(2,1)} %all-gather.14.cloned.1.call-done.right_ref.rows_ref.refs_2_, bf16[2048,2048]{1,0:T(8,128)(2,1)} %collective-permute-done.7.right_ref.rows_ref.refs_3_), custom_call_target="tpu_custom_call" | custom-call | flops 7730940928 | bytes 18874368 | tf_op jit(solution)/shard_map/pallas_call | solution.py:719
  477.0 21.4 %shard_map.240 = (bf16[4,4,128,768]{3,2,1,0:T(8,128)(2,1)}, f32[1,256]{1,0:T(1,128)}, f32[1,256]{1,0:T(1,128)}, f32[1,256]{1,0:T(1,128)}) custom-call(bf16[2048,2048]{1,0:T(8,128)(2,1)} %all-gather.12.cloned.1.call-done.rows_ref.refs_0_, bf16[2048,2048]{1,0:T(8,128)(2,1)} %collective-permute-done.6.rows_ref.refs_1_, bf16[2048,256]{1,0:T(8,128)(2,1)} %bitcast.236, ...), custom_call_target="tpu_custom_call" | custom-call | flops 23192823808 | bytes 23068672 | tf_op jit(solution)/shard_map/pallas_call | solution.py:719
  503.0 21.7 %shard_map.241 = bf16[2048,2048]{1,0:T(8,128)(2,1)} custom-call(bf16[2048,1024]{1,0:T(8,128)(2,1)} %get-tuple-element.88.refs_3_.refs_0_, bf16[2048,256]{1,0:T(8,128)(2,1)} %bitcast.245, bf16[2048,256]{1,0:T(8,128)(2,1)} %bitcast.247, bf16[2048,256]{1,0:T(8,128)(2,1)} %bitcast.249, ...), custom_call_target="tpu_custom_call" | custom-call | flops 27058294784 | bytes 23068672 | tf_op jit(solution)/shard_map/pallas_call | solution.py:561
  531.6 15.8 %shard_map.242 = bf16[2048,2048]{1,0:T(8,128)(2,1)} custom-call(bf16[2048,1024]{1,0:T(8,128)(2,1)} %get-tuple-element.112.left_ref.refs_0_, bf16[2048,256]{1,0:T(8,128)(2,1)} %bitcast.243, bf16[1024,2048]{1,0:T(8,128)(2,1)} %constant_dynamic-slice_fusion.28.down_ref.refs_2_.refs_3_, bf16[256,2048]{1,0:T(8,128)(2,1)} %constant_dynamic-slice_fusion.27.out_w_ref.refs_3_.refs_4_), custom_call_target="tpu_custom_call" | custom-call | flops 19327352832 | bytes 18874368 | tf_op jit(solution)/shard_map/pallas_call | solution.py:561
  547.4 21.9 %shard_map.243 = bf16[2048,2048]{1,0:T(8,128)(2,1)} custom-call(bf16[2048,1024]{1,0:T(8,128)(2,1)} %get-tuple-element.113.refs_2_.refs_0_, bf16[2048,256]{1,0:T(8,128)(2,1)} %bitcast.237, bf16[2048,256]{1,0:T(8,128)(2,1)} %bitcast.239, bf16[2048,256]{1,0:T(8,128)(2,1)} %bitcast.241, bf16[2048,2048]{1,0:T(8,128)(2,1)} %collective-permute-done.11.refs_4_, ...), custom_call_target="tpu_custom_call" | custom-call | flops 27058294784 | bytes 31457280 | tf_op jit(solution)/shard_map/pallas_call | solution.py:561
  575.6 16.5 %shard_map.244 = bf16[2048,2048]{1,0:T(8,128)(2,1)} custom-call(bf16[2048,1024]{1,0:T(8,128)(2,1)} %get-tuple-element.114.left_ref.refs_0_, bf16[2048,256]{1,0:T(8,128)(2,1)} %bitcast.233, bf16[2048,2048]{1,0:T(8,128)(2,1)} %collective-permute-done.12.refs_2_, bf16[1024,2048]{1,0:T(8,128)(2,1)} %constant_dynamic-slice_fusion.28.down_ref.refs_2_.refs_3_, ...), custom_call_target="tpu_custom_call" | custom-call | flops 19327352832 | bytes 27262976 | tf_op jit(solution)/shard_map/pallas_call | solution.py:561
  610.0 12.1 %collective-permute-done.26 = bf16[256,2048]{1,0:T(8,128)(2,1)} collective-permute-done((bf16[256,2048]{1,0:T(8,128)(2,1)S(1)}, bf16[256,2048]{1,0:T(8,128)(2,1)}, u32[]{:S(2)}, u32[]{:S(2)}) %collective-permute-start.26) | collective-permute-done | bytes 1048608 | tf_op jit(solution)/shard_map/ppermute | solution.py:355
  651.0 16.0 %collective-permute-done.30 = bf16[256,2048]{1,0:T(8,128)(2,1)} collective-permute-done((bf16[256,2048]{1,0:T(8,128)(2,1)}, bf16[256,2048]{1,0:T(8,128)(2,1)}, u32[]{:S(2)}, u32[]{:S(2)}) %collective-permute-start.30) | collective-permute-done | bytes 1048608 | tf_op jit(solution)/shard_map/ppermute | solution.py:355
  679.8 28.9 %all-gather.20.cloned.1.call-done = bf16[16,128,1024]{2,1,0:T(8,128)(2,1)} async-done(((bf16[4,128,1024]{2,1,0:T(8,128)(2,1)}), bf16[16,128,1024]{2,1,0:T(8,128)(2,1)}) %all-gather.20.cloned.1.call-update) | async-done | bytes 4194320 | tf_op jit(solution)/shard_map/all_gather | solution.py:1001
  744.6 21.9 %all-to-all-done.5 = bf16[4,128,2048]{2,1,0:T(8,128)(2,1)S(1)} async-done(((bf16[4,128,2048]{2,1,0:T(8,128)(2,1)}), bf16[4,128,2048]{2,1,0:T(8,128)(2,1)S(1)}, u32[]{:S(2)}, u32[]{:S(2)}) %all-to-all-start.5) | async-done | bytes 2097184 | tf_op jit(solution)/shard_map/all_to_all | solution.py:423
  797.9 14.0 %shard_map.247 = f32[2048,2048]{1,0:T(8,128)} custom-call(s32[2]{0:T(128)} %pad_add_fusion.where, bf16[1024,2048]{1,0:T(8,128)(2,1)} %all-gather.16.cloned.1.call-done.own_ref, bf16[1024,2048]{1,0:T(8,128)(2,1)} %collective-permute-done.20.oth_ref), custom_call_target="tpu_custom_call" | custom-call | bytes 25165824 | tf_op jit(solution)/shard_map/pallas_call | solution.py:488
  (313 shorter events, 308.8 us)
Async XLA Ops:
  25.4 55.4 %all-to-all-start = ((bf16[4,128,2048]{2,1,0:T(8,128)(2,1)}), bf16[4,128,2048]{2,1,0:T(8,128)(2,1)}, u32[]{:S(2)}, u32[]{:S(2)}) async-start(bf16[4,128,2048]{2,1,0:T(8,128)(2,1)} %fusion.19), calls=%async_computation | async-start | bytes 4194304 | tf_op jit(solution)/shard_map/all_to_all | solution.py:383
  30.3 138.6 %all-gather.12.cloned.1.call-start = ((), (), s32[]{:S(2)}) async-start(), calls=%async_computation.9 | async-start | bytes 10485760 | tf_op jit(solution)/shard_map/all_gather | solution.py:969
  33.1 45.8 %collective-permute-start.2 = (bf16[512,1024]{1,0:T(8,128)(2,1)S(1)}, bf16[512,1024]{1,0:T(8,128)(2,1)S(1)}, u32[]{:S(2)}, u32[]{:S(2)}) collective-permute-start(bf16[512,1024]{1,0:T(8,128)(2,1)S(1)} %get-tuple-element.73), channel_id=1, source_target_pairs={{0,2},{1,3},{2,0},{3,1},{4,6},{5,7},{6,4},{7,5},{8,10},{9,11},{10,... | collective-permute-start | bytes 3145736 | tf_op jit(solution)/shard_map/ppermute | solution.py:355
  36.1 44.7 %collective-permute-start.1 = (bf16[512,1024]{1,0:T(8,128)(2,1)S(1)}, bf16[512,1024]{1,0:T(8,128)(2,1)}, u32[]{:S(2)}, u32[]{:S(2)}) collective-permute-start(bf16[512,1024]{1,0:T(8,128)(2,1)S(1)} %get-tuple-element.72), channel_id=1, source_target_pairs={{0,1},{1,0},{2,3},{3,2},{4,5},{5,4},{6,7},{7,6},{8,9},{9,8},{10,11... | collective-permute-start | bytes 3145736 | tf_op jit(solution)/shard_map/ppermute | solution.py:355
  80.9 177.8 %all-gather.14.cloned.1.call-start = ((), (), s32[]{:S(2)}) async-start(), calls=%async_computation.10 | async-start | bytes 10485760 | tf_op jit(solution)/shard_map/all_gather | solution.py:973
  140.6 248.8 %reduce-scatter.6.cloned.1.call-start = ((), (), s32[]{:S(2)}) async-start(), calls=%async_computation.12 | async-start | bytes 5242880 | tf_op jit(solution)/shard_map/reduce_scatter | solution.py:998
  168.9 44.6 %collective-permute-start.6 = (bf16[2048,2048]{1,0:T(8,128)(2,1)}, bf16[2048,2048]{1,0:T(8,128)(2,1)}, u32[]{:S(2)}, u32[]{:S(2)}) collective-permute-start(bf16[2048,2048]{1,0:T(8,128)(2,1)} %all-gather.12.cloned.1.call-done.rows_ref.refs_0_), channel_id=1, source_target_pairs={{0,16},{16,0},{1,17},{17,1},{2,18},{18,2},{3,19},{19,3},{4,20},{20... | collective-permute-start | bytes 25165832 | tf_op jit(solution)/shard_map/ppermute | solution.py:351
  291.7 181.6 %reduce-scatter.4.cloned.1.call-start = ((), (), s32[]{:S(2)}) async-start(), calls=%async_computation.11 | async-start | bytes 5242880 | tf_op jit(solution)/shard_map/reduce_scatter | solution.py:998
  358.8 172.8 %all-gather.16.cloned.1.call-start = ((), (), s32[]{:S(2)}) async-start(), calls=%async_computation.13 | async-start | bytes 5242880 | tf_op jit(solution)/shard_map/all_gather | solution.py:1001
  477.0 157.6 %reduce-scatter.8.cloned.1.call-start = ((), (), s32[]{:S(2)}) async-start(), calls=%async_computation.14 | async-start | bytes 5242880 | tf_op jit(solution)/shard_map/reduce_scatter | solution.py:998
  503.0 205.7 %all-gather.20.cloned.1.call-start = ((), (), s32[]{:S(2)}) async-start(), calls=%async_computation.16 | async-start | bytes 5242880 | tf_op jit(solution)/shard_map/all_gather | solution.py:1001
  575.0 47.1 %collective-permute-start.26 = (bf16[256,2048]{1,0:T(8,128)(2,1)S(1)}, bf16[256,2048]{1,0:T(8,128)(2,1)}, u32[]{:S(2)}, u32[]{:S(2)}) collective-permute-start(bf16[256,2048]{1,0:T(8,128)(2,1)S(1)} %get-tuple-element.138), channel_id=1, source_target_pairs={{0,1},{1,0},{2,3},{3,2},{4,5},{5,4},{6,7},{7,6},{8,9},{9,8},{10,11... | collective-permute-start | bytes 3145736 | tf_op jit(solution)/shard_map/ppermute | solution.py:355
  602.7 48.4 %collective-permute-start.31 = (bf16[256,2048]{1,0:T(8,128)(2,1)S(1)}, bf16[256,2048]{1,0:T(8,128)(2,1)}, u32[]{:S(2)}, u32[]{:S(2)}) collective-permute-start(bf16[256,2048]{1,0:T(8,128)(2,1)S(1)} %get-tuple-element.139), channel_id=1, source_target_pairs={{0,2},{1,3},{2,0},{3,1},{4,6},{5,7},{6,4},{7,5},{8,10},{9,11},{10,... | collective-permute-start | bytes 3145736 | tf_op jit(solution)/shard_map/ppermute | solution.py:355
  640.4 70.6 %collective-permute-start.13 = (bf16[256,2048]{1,0:T(8,128)(2,1)}, bf16[256,2048]{1,0:T(8,128)(2,1)}, u32[]{:S(2)}, u32[]{:S(2)}) collective-permute-start(bf16[256,2048]{1,0:T(8,128)(2,1)} %get-tuple-element.144), channel_id=1, source_target_pairs={{0,1},{1,0},{2,3},{3,2},{4,5},{5,4},{6,7},{7,6},{8,9},{9,8},{10,11... | collective-permute-start | bytes 3145736 | tf_op jit(solution)/shard_map/ppermute | solution.py:355
  642.4 66.7 %collective-permute-start.16 = (bf16[256,2048]{1,0:T(8,128)(2,1)}, bf16[256,2048]{1,0:T(8,128)(2,1)}, u32[]{:S(2)}, u32[]{:S(2)}) collective-permute-start(bf16[256,2048]{1,0:T(8,128)(2,1)} %get-tuple-element.146), channel_id=1, source_target_pairs={{0,2},{1,3},{2,0},{3,1},{4,6},{5,7},{6,4},{7,5},{8,10},{9,11},{10,... | collective-permute-start | bytes 3145736 | tf_op jit(solution)/shard_map/ppermute | solution.py:355
  647.5 63.5 %collective-permute-start.15 = (bf16[256,2048]{1,0:T(8,128)(2,1)}, bf16[256,2048]{1,0:T(8,128)(2,1)}, u32[]{:S(2)}, u32[]{:S(2)}) collective-permute-start(bf16[256,2048]{1,0:T(8,128)(2,1)} %add_convert_fusion.7), channel_id=1, source_target_pairs={{0,2},{1,3},{2,0},{3,1},{4,6},{5,7},{6,4},{7,5},{8,10},{9,11},{10,... | collective-permute-start | bytes 3145736 | tf_op jit(solution)/shard_map/ppermute | solution.py:355
  675.5 91.1 %all-to-all-start.5 = ((bf16[4,128,2048]{2,1,0:T(8,128)(2,1)}), bf16[4,128,2048]{2,1,0:T(8,128)(2,1)S(1)}, u32[]{:S(2)}, u32[]{:S(2)}) async-start(bf16[4,128,2048]{2,1,0:T(8,128)(2,1)} %bitcast.175), calls=%async_computation.8 | async-start | bytes 4194304 | tf_op jit(solution)/shard_map/all_to_all | solution.py:423
  679.1 140.4 %all-gather.18.cloned.1.call-start = ((), (), s32[]{:S(2)}) async-start(), calls=%async_computation.15 | async-start | bytes 3932160 | tf_op jit(solution)/shard_map/all_gather | solution.py:1001
  708.7 82.6 %collective-permute-start.21 = (bf16[4,4,128,1024]{3,2,1,0:T(8,128)(2,1)}, bf16[4,4,128,1024]{3,2,1,0:T(8,128)(2,1)}, u32[]{:S(2)}, u32[]{:S(2)}) collective-permute-start(bf16[4,4,128,1024]{3,2,1,0:T(8,128)(2,1)} %bitcast.180), channel_id=1, source_target_pairs={{0,16},{16,0},{1,17},{17,1},{2,18},{18,2},{3,19},{19,3},{4,20},{20... | collective-permute-start | bytes 12582920 | tf_op jit(solution)/shard_map/ppermute | solution.py:351
  708.7 89.3 %collective-permute-start.20 = (bf16[1024,2048]{1,0:T(8,128)(2,1)}, bf16[1024,2048]{1,0:T(8,128)(2,1)}, u32[]{:S(2)}, u32[]{:S(2)}) collective-permute-start(bf16[1024,2048]{1,0:T(8,128)(2,1)} %all-gather.16.cloned.1.call-done.own_ref), channel_id=1, source_target_pairs={{0,16},{16,0},{1,17},{17,1},{2,18},{18,2},{3,19},{19,3},{4,20},{20... | collective-permute-start | bytes 12582920 | tf_op jit(solution)/shard_map/ppermute | solution.py:351
  727.9 46.3 %collective-permute-start.24 = (f32[1,1792]{1,0:T(1,128)S(1)}, f32[1,1792]{1,0:T(1,128)S(1)}, u32[]{:S(2)}, u32[]{:S(2)}) collective-permute-start(f32[1,1792]{1,0:T(1,128)S(1)} %add.477), channel_id=1, source_target_pairs={{4,0},{8,12},{5,1},{9,13},{6,2},{10,14},{7,3},{11,15},{20,16},{24,... | collective-permute-start | bytes 21512 | tf_op jit(solution)/shard_map/ppermute | solution.py:453
  766.5 66.1 %all-to-all-start.3 = ((bf16[4,128,2048]{2,1,0:T(8,128)(2,1)}), bf16[4,128,2048]{2,1,0:T(8,128)(2,1)}, u32[]{:S(2)}, u32[]{:S(2)}) async-start(bf16[4,128,2048]{2,1,0:T(8,128)(2,1)} %bitcast.176), calls=%async_computation.5 | async-start | bytes 4194304 | tf_op jit(solution)/shard_map/all_to_all | solution.py:423
  774.0 92.8 %all-gather.22.cloned.1.call-start = ((), (), s32[]{:S(2)}) async-start(), calls=%async_computation.17 | async-start | bytes 1310720 | tf_op jit(solution)/shard_map/all_gather | solution.py:1001
  774.1 45.4 %collective-permute-start.32 = (bf16[2,128,2048]{2,1,0:T(8,128)(2,1)S(1)}, bf16[2,128,2048]{2,1,0:T(8,128)(2,1)}, u32[]{:S(2)}, u32[]{:S(2)}) collective-permute-start(bf16[2,128,2048]{2,1,0:T(8,128)(2,1)S(1)} %dynamic-slice_bitcast_fusion), channel_id=1, source_target_pairs={{0,16},{16,0},{1,17},{17,1},{2,18},{18,2},{3,19},{19,3},{4,20},{20... | collective-permute-start | bytes 3145736 | tf_op jit(solution)/shard_map/ppermute | solution.py:351
  (68 other events, 1329.6 us)
Sparse Core Ops, SparseCore 0:
  81.0 87.8 all-gather.11
  170.7 87.9 all-gather.13
  291.8 76.8 reduce-scatter.5
  371.6 77.2 reduce-scatter.3
  450.3 81.2 all-gather.15
  533.8 75.2 reduce-scatter.7
  610.7 97.9 all-gather.19
  710.9 108.5 all-gather.17
  826.1 25.4 all-gather.21
